TPU v7x, 32 devices: a whole 2x2x4 slice. The times are simulated.
32 devices in a mesh: rows: 8 (over z, y), cols: 4 (over x, core).
Axes of the slice: x: 2, y: 2, z: 4, core: 2. Of those that a mesh axis runs over, the one named last changes fastest.
Arguments:
- factor: bfloat16 [4096, 256], P(('rows', 'cols')), may hold values from -0.09375 to 0.09375
- cores: bfloat16 [4, 256, 256], replicated, as said below
- tile_values: bfloat16 [4, 96, 512, 128], P(None, 'rows', 'cols'), may hold values from -56 to 56
- tile_rows: int32 [4, 8, 48], P(None, 'rows', 'cols'), may hold values from 0 to 3
- tile_cols: int32 [4, 8, 48], P(None, 'rows', 'cols'), may hold values from 0 to 7
- tile_counts: int32 [4, 8, 4], P(None, 'rows', 'cols'), may hold values from 3 to 12, as said below
Outputs:
- factor_new: bfloat16 [4096, 256], P(('rows', 'cols'))
- cores_new: float32 [4, 256, 256], replicated
Inputs may be any that keep to these rules, and one draw needn't show every extreme that they name: cores are dominated by their positive diagonals. `tile_counts`: every relation has some device whose 12 slots are all used. `tile_rows`: several slots may name the same tile.
All inputs are finite; a program needn't handle non-finite values.
Results may differ from a plain program's by a relative error of at most 0.0034.
The roundings to bfloat16 on the way count: a program that leaves them out, or rounds other values in their place, can miss the bound.
Values may be sent and summed in bfloat16 or wider, within the bound.
No kernel may reach another device: no remote copies, remote signals or barrier semaphores. Data moves between devices by JAX's collectives and lax.ppermute only.
A program may use at most 128 MiB of HBM per device.

v0:
```python
import functools

import jax
import jax.numpy as jnp
from jax import lax
from jax.experimental import pallas as pl
from jax.experimental.pallas import tpu as pltpu
from jax.sharding import PartitionSpec as P

ridge_weight = 0.1
value_bound = 160.0
product_bound = 672.0
f16_top = 30000.0


def params():
    return pltpu.CompilerParams(vmem_limit_bytes=48 * 1024 * 1024)


def swap(x, axis, mask):
    size = lax.axis_size(axis)
    return lax.ppermute(x, axis, [(i, i ^ mask) for i in range(size)])


def bits_of(axis):
    return lax.axis_size(axis).bit_length() - 1


def reversed_slot(slot, bits):
    out = 0
    for b in range(bits):
        out = out + (((slot >> b) & 1) << (bits - 1 - b))
    return out


def gather_cols(x):
    pieces = [x]
    for b in range(bits_of("cols")):
        pieces = pieces + [swap(p, "cols", 1 << b) for p in pieces]
    return pieces


def gather_rows(x):
    half = lax.axis_size("rows") // 2
    even = [x] + [swap(x, "rows", 2 * i) for i in range(1, half)]
    return even + [swap(p, "rows", 1) for p in even]


def tree_sum(parts):
    while len(parts) > 1:
        parts = [parts[i] + parts[i + 1] for i in range(0, len(parts), 2)]
    return parts[0]


def half_of(x, scale):
    return (x * scale).astype(jnp.float16)


def scatter_cols(x, scale):
    for b in range(bits_of("cols")):
        keep, give = jnp.split(x, 2, axis=0)
        if b == 0:
            x = keep + swap(give, "cols", 1)
        else:
            x = keep + swap(half_of(give, scale), "cols", 1 << b).astype(jnp.float32) / scale
    return x


def dot(a, b, dims=((1,), (0,)), precision=None):
    return lax.dot_general(
        a, b, (dims, ((), ())), preferred_element_type=jnp.float32, precision=precision
    )


def gram_kernel(*refs):
    pieces, factors_ref, gram_ref = refs[:-2], refs[-2], refs[-1]
    tile = pieces[0].shape[0]
    for i, piece in enumerate(pieces):
        factors_ref[i * tile:(i + 1) * tile, :] = piece[...]
    whole = factors_ref[...]
    gram = dot(whole, whole, ((0,), (0,)))
    side = gram_ref.shape[1]
    gram_ref[0] = gram[:side, :side]
    gram_ref[1] = gram[:side, side:]
    gram_ref[2] = gram[side:, side:]


def gram_of(pieces):
    tile, rank = pieces[0].shape
    vmem = pl.BlockSpec(memory_space=pltpu.VMEM)
    factors, gram = pl.pallas_call(
        gram_kernel,
        out_shape=(
            jax.ShapeDtypeStruct((len(pieces) * tile, rank), jnp.bfloat16),
            jax.ShapeDtypeStruct((3, rank // 2, rank // 2), jnp.float32),
        ),
        in_specs=[vmem] * len(pieces),
        out_specs=(vmem, vmem),
        compiler_params=params(),
        name="gram",
    )(*pieces)
    return factors, gram


def first_kernel(rows_ref, cols_ref, counts_ref, tiles_ref, factors_ref, cores_ref, *refs,
                 bits_c, half):
    panel_refs = refs[:-5]
    direct_ref, back_ref, acc_ref, turned_ref, sums_ref = refs[-5:]
    relations, slots = tiles_ref.shape[0], tiles_ref.shape[1]
    tile = tiles_ref.shape[2]
    panels = len(panel_refs)
    my_row = lax.axis_index("rows")
    my_col = lax.axis_index("cols")
    sums_ref[...] = jnp.zeros_like(sums_ref)
    for k in range(relations):
        core = cores_ref[k]
        for i in range(panels):
            rotated = dot(panel_refs[i][...], core).astype(jnp.bfloat16)
            turned_ref[i] = rotated.T
        acc_ref[...] = jnp.zeros_like(acc_ref)
        for s in range(slots):
            live = s < counts_ref[k, 0, 0]
            values = tiles_ref[k, s]
            values = jnp.where(live, values, jnp.zeros_like(values))
            col = cols_ref[k, 0, s] ^ my_row
            col = (col & 1) * half + (col >> 1)
            row = rows_ref[k, 0, s] ^ my_col
            acc_ref[row] += dot(values, factors_ref[col])
            sums_ref[col] += dot(turned_ref[row], values)
        for i in range(panels):
            whole = acc_ref[i]
            high = whole.astype(jnp.bfloat16)
            low = (whole - high.astype(jnp.float32)).astype(jnp.bfloat16)
            part = dot(high, core, ((1,), (1,))) + dot(low, core, ((1,), (1,)))
            place = reversed_slot(i, bits_c)
            if k == 0:
                direct_ref[place] = part
            else:
                direct_ref[place] += part
    for g in range(sums_ref.shape[0]):
        back_ref[g] = sums_ref[g].T


def first_pass(rows, cols, counts, tiles, factors, panel, cores):
    relations, slots, tile, _ = tiles.shape
    rank = cores.shape[-1]
    n_rows, n_cols = lax.axis_size("rows"), lax.axis_size("cols")
    smem = pl.BlockSpec(memory_space=pltpu.SMEM)
    vmem = pl.BlockSpec(memory_space=pltpu.VMEM)
    return pl.pallas_call(
        functools.partial(first_kernel, bits_c=bits_of("cols"), half=n_rows // 2),
        out_shape=(
            jax.ShapeDtypeStruct((n_cols, tile, rank), jnp.float32),
            jax.ShapeDtypeStruct((n_rows, tile, rank), jnp.float32),
        ),
        in_specs=[smem, smem, smem, vmem, vmem, vmem] + [vmem] * len(panel),
        out_specs=(vmem, vmem),
        scratch_shapes=[
            pltpu.VMEM((n_cols, tile, rank), jnp.float32),
            pltpu.VMEM((n_cols, rank, tile), jnp.bfloat16),
            pltpu.VMEM((n_rows, rank, tile), jnp.float32),
        ],
        compiler_params=params(),
        name="first_pass",
    )(rows, cols, counts, tiles, factors.reshape(n_rows, tile, rank), cores, *panel)


def second_kernel(rows_ref, cols_ref, counts_ref, tiles_ref, factors_ref, *refs, bits_c, half):
    panel_refs = refs[:-4]
    out_ref, turned_ref, upper_ref, picked_ref = refs[-4:]
    relations, slots = tiles_ref.shape[0], tiles_ref.shape[1]
    tile = tiles_ref.shape[2]
    panels = len(panel_refs)
    pieces = out_ref.shape[0] // relations
    height = out_ref.shape[2]
    my_row = lax.axis_index("rows")
    my_col = lax.axis_index("cols")
    for i in range(panels):
        turned_ref[i] = panel_refs[i][...].T
    for k in range(relations):
        for s in range(slots):
            live = s < counts_ref[k, 0, 0]
            values = tiles_ref[k, s]
            values = jnp.where(live, values, jnp.zeros_like(values))
            col = cols_ref[k, 0, s] ^ my_row
            col = (col & 1) * half + (col >> 1)
            row = rows_ref[k, 0, s] ^ my_col
            upper_ref[:, s * tile:(s + 1) * tile] = dot(turned_ref[row], values).astype(jnp.bfloat16)
            picked_ref[s * tile:(s + 1) * tile, :] = factors_ref[col]
        core = dot(upper_ref[...], picked_ref[...])
        for p in range(pieces):
            place = reversed_slot((k * pieces + p) ^ my_col, bits_c)
            for h in range(2):
                begin = (2 * p + h) * height
                out_ref[place, h ^ (my_row & 1)] = core[begin:begin + height, :]


def second_pass(rows, cols, counts, tiles, factors, panel):
    relations, slots, tile, _ = tiles.shape
    rank = panel[0].shape[-1]
    n_rows, n_cols = lax.axis_size("rows"), lax.axis_size("cols")
    smem = pl.BlockSpec(memory_space=pltpu.SMEM)
    vmem = pl.BlockSpec(memory_space=pltpu.VMEM)
    return pl.pallas_call(
        functools.partial(second_kernel, bits_c=bits_of("cols"), half=n_rows // 2),
        out_shape=jax.ShapeDtypeStruct(
            (n_cols, 2, relations * rank // n_cols // 2, rank), jnp.float32
        ),
        in_specs=[smem, smem, smem, vmem, vmem] + [vmem] * len(panel),
        out_specs=vmem,
        scratch_shapes=[
            pltpu.VMEM((n_cols, rank, tile), jnp.bfloat16),
            pltpu.VMEM((rank, slots * tile), jnp.bfloat16),
            pltpu.VMEM((slots * tile, rank), jnp.bfloat16),
        ],
        compiler_params=params(),
        name="second_pass",
    )(rows, cols, counts, tiles, factors.reshape(n_rows, tile, rank), *panel)


def split(x, terms):
    parts = []
    for _ in range(terms):
        part = x.astype(jnp.bfloat16)
        parts.append(part)
        x = x - part.astype(jnp.float32)
    return parts


def eliminate(z_ref, begin, end, block, sub):
    size = z_ref.shape[0]
    wide = size // 128
    for p in range(begin, end):
        o = p * block
        panel = z_ref[o:o + block, :]
        rows = lax.broadcasted_iota(jnp.int32, (block, 128), 0)
        rows_wide = lax.broadcasted_iota(jnp.int32, (block, size), 0)
        lanes = lax.broadcasted_iota(jnp.int32, (block, size), 1)
        for q in range(block // sub):
            first = o + q * sub
            cols = [
                jnp.broadcast_to(panel[:, first + m:first + m + 1], (block, 128))
                for m in range(sub)
            ]
            for m in range(sub):
                j = q * sub + m
                root = lax.rsqrt(cols[m][j:j + 1, :])
                factors = jnp.where(rows > j, cols[m] * root, 0.0)
                for t in range(m + 1, sub):
                    cols[t] = cols[t] - factors * (cols[t][j:j + 1, :] * root)
                unit = jnp.where(rows_wide == j, 1.0, 0.0)
                panel = jnp.where(lanes == o + j, unit, panel)
                line = panel[j:j + 1, :] * jnp.concatenate([root] * wide, axis=1)
                factors = jnp.concatenate([factors] * wide, axis=1)
                panel = jnp.where(rows_wide == j, line, panel - factors * line)
        z_ref[o:o + block, :] = panel
        rest = size - o - block
        if rest:
            high, mid, low = split(panel, 3)
            left = jnp.concatenate([high, high, mid, mid, high, low], axis=0)[:, o + block:]
            right = jnp.concatenate([high, mid, high, mid, low, high], axis=0)
            change = dot(left, right, ((0,), (0,)))
            lanes = lax.broadcasted_iota(jnp.int32, (rest, size), 1)
            done = (lanes >= o) & (lanes < o + block)
            z_ref[o + block:, :] = jnp.where(done, 0.0, z_ref[o + block:, :]) - change


def lower_of(z):
    rows = lax.broadcasted_iota(jnp.int32, z.shape, 0)
    lanes = lax.broadcasted_iota(jnp.int32, z.shape, 1)
    return jnp.where(rows >= lanes, z, 0.0)


def system_kernel(mine_ref, other_ref, cores_ref, out_ref, z_ref):
    size = z_ref.shape[0]
    side = size // 2
    upper = mine_ref[1] + other_ref[1]
    z_ref[:side, :side] = mine_ref[0] + other_ref[0]
    z_ref[:side, side:] = upper
    z_ref[side:, :side] = upper.T
    z_ref[side:, side:] = mine_ref[2] + other_ref[2]
    grams = jnp.concatenate(split(z_ref[...], 3), axis=0)
    rows = lax.broadcasted_iota(jnp.int32, (size, size), 0)
    lanes = lax.broadcasted_iota(jnp.int32, (size, size), 1)
    total = jnp.where(rows == lanes, ridge_weight, 0.0)
    for k in range(cores_ref.shape[0]):
        core = cores_ref[k]
        turned = core.T
        for left, right in ((core, turned), (turned, core)):
            middle = dot(jnp.concatenate([left] * 3, axis=1), grams)
            middle = jnp.concatenate(split(middle, 3), axis=1)
            total = total + dot(middle, jnp.concatenate([right] * 3, axis=0))
    z_ref[...] = total
    eliminate(z_ref, 0, size // 32, 32, 16)
    lower = lower_of(z_ref[...])
    high, mid, low = split(lower, 3)
    left = jnp.concatenate([high, high, mid, mid, high, low], axis=0)
    right = jnp.concatenate([high, mid, high, mid, low, high], axis=0)
    out_ref[...] = dot(left, right, ((0,), (0,)))


def system_inverse(mine, other, cores):
    rank = cores.shape[-1]
    vmem = pl.BlockSpec(memory_space=pltpu.VMEM)
    return pl.pallas_call(
        system_kernel,
        out_shape=jax.ShapeDtypeStruct((rank, rank), jnp.float32),
        in_specs=[vmem] * 3,
        out_specs=vmem,
        scratch_shapes=[pltpu.VMEM((rank, rank), jnp.float32)],
        compiler_params=params(),
        cost_estimate=pl.CostEstimate(flops=9_000_000_000, bytes_accessed=1_500_000, transcendentals=0),
        name="system_inverse",
    )(mine, other, cores)


def begin_kernel(mine_ref, other_ref, out_ref):
    size = out_ref.shape[0]
    side = size // 2
    out_ref[:side, :side] = mine_ref[0] + other_ref[0]
    out_ref[:side, side:] = mine_ref[1] + other_ref[1]
    out_ref[side:, :side] = jnp.zeros((side, side), jnp.float32)
    out_ref[side:, side:] = mine_ref[2] + other_ref[2]
    eliminate(out_ref, 0, size // 64, 32, 16)


def end_kernel(in_ref, out_ref):
    size = out_ref.shape[0]
    out_ref[...] = in_ref[...]
    eliminate(out_ref, size // 64, size // 32, 32, 16)


def half_eliminate(kernel, name, rank, *args):
    vmem = pl.BlockSpec(memory_space=pltpu.VMEM)
    return pl.pallas_call(
        kernel,
        out_shape=jax.ShapeDtypeStruct((rank, rank), jnp.float32),
        in_specs=[vmem] * len(args),
        out_specs=vmem,
        compiler_params=params(),
        cost_estimate=pl.CostEstimate(flops=3_500_000_000, bytes_accessed=500_000, transcendentals=0),
        name=name,
    )(*args)


def whiten_kernel(z_ref, factor_ref, near_ref, far_ref, out_ref, core_ref, *, bits_c):
    relations, rank = out_ref.shape[0], out_ref.shape[1]
    halves = near_ref.shape[0]
    pieces = 2 * halves // relations
    height = near_ref.shape[2]
    my_col = lax.axis_index("cols")
    my_row = lax.axis_index("rows")
    core_ref[:halves] = near_ref[...]
    core_ref[halves:] = far_ref[...]
    high, low = split(lower_of(z_ref[...]), 2)
    left = jnp.concatenate([high, high, low], axis=1)
    right = jnp.concatenate([high, low, high], axis=1)
    for k in range(relations):
        parts = []
        for p in range(pieces):
            place = reversed_slot((k * pieces + p) ^ my_col, bits_c)
            parts += [core_ref[place, h ^ (my_row & 1)] for h in range(2)]
        core = jnp.concatenate(parts, axis=0) * factor_ref[0]
        first, rest = split(core, 2)
        middle = dot(left, jnp.concatenate([first, rest, first], axis=0))
        first, rest = split(middle, 2)
        out_ref[k] = dot(jnp.concatenate([first, first, rest], axis=1), right, ((1,), (1,)))


def whiten(z, factor, near, far, relations):
    rank = z.shape[0]
    vmem = pl.BlockSpec(memory_space=pltpu.VMEM)
    return pl.pallas_call(
        functools.partial(whiten_kernel, bits_c=bits_of("cols")),
        out_shape=jax.ShapeDtypeStruct((relations, rank, rank), jnp.float32),
        in_specs=[vmem, pl.BlockSpec(memory_space=pltpu.SMEM), vmem, vmem],
        out_specs=vmem,
        scratch_shapes=[pltpu.VMEM((2 * near.shape[0],) + near.shape[1:], jnp.float32)],
        compiler_params=params(),
        name="whiten",
    )(z, factor.reshape(1), near, far)


def pair_of_sums(x):
    for b in range(bits_of("cols") - 1):
        x = x + swap(x, "cols", 1 << b)
    return x, swap(x, "cols", 1 << (bits_of("cols") - 1))


def local(factor, cores, tile_values, tile_rows, tile_cols, tile_counts):
    relations, slots, tile, _ = tile_values.shape
    rank = factor.shape[1]
    n_rows, n_cols = lax.axis_size("rows"), lax.axis_size("cols")
    half = n_rows // 2
    magnitude = jnp.abs(cores.astype(jnp.float32))
    reach = jnp.maximum(jnp.max(jnp.sum(magnitude, 1)), jnp.max(jnp.sum(magnitude, 2)))
    scale = f16_top / (2.0 * n_cols * relations * slots * product_bound * reach + 1e-20)

    factors, gram = gram_of(gather_rows(factor))
    panel = gather_cols(factor)
    gram_pair = pair_of_sums(gram)
    direct, back = first_pass(tile_rows, tile_cols, tile_counts, tile_values, factors, panel, cores)
    inverse = system_inverse(*gram_pair, cores)
    parts = []
    for begin in range(half, 0, -half // 2):
        begin = begin - half // 2
        end = begin + half // 2
        give = half_of(back[half + begin:half + end], scale)
        parts = [back[begin:end] + swap(give, "rows", 1).astype(jnp.float32) / scale] + parts
    packed = [half_of(part, scale) for part in parts]
    received = [
        swap(packed[i // (half // 2)][i % (half // 2)], "rows", 2 * i).astype(jnp.float32)
        for i in range(1, half)
    ]
    numerator = (
        scatter_cols(direct, scale)[0] + parts[0][0] + functools.reduce(jnp.add, received) / scale
    )
    factor_new = dot(numerator, inverse, precision=lax.Precision.HIGHEST).astype(jnp.bfloat16)

    factors_new, gram_new = gram_of(gather_rows(factor_new))
    panel_new = gather_cols(factor_new)
    gram_pair = pair_of_sums(gram_new)
    longest = jnp.max(gram_pair[0] + gram_pair[1])
    tiles_in_all = n_rows * n_cols
    scale_core = f16_top / (2.0 * slots * tile * value_bound * tiles_in_all * longest + 1e-30)
    core = second_pass(tile_rows, tile_cols, tile_counts, tile_values, factors_new, panel_new)
    core = scatter_cols(core, scale_core)[0]
    z = half_eliminate(begin_kernel, "begin", rank, *gram_pair)
    core = core[0] + swap(half_of(core[1], scale_core), "rows", 1).astype(jnp.float32) / scale_core
    packed = half_of(core, scale_core)
    core = tree_sum(
        [packed.astype(jnp.float32)]
        + [swap(packed, "rows", 2 * i).astype(jnp.float32) for i in range(1, half)]
    )
    z = half_eliminate(end_kernel, "end", rank, z)
    core = core.astype(jnp.float16)[None]
    core = jnp.concatenate([core, swap(core, "rows", 1)], axis=0)[None]
    for b in reversed(range(1, bits_of("cols"))):
        core = jnp.concatenate([core, swap(core, "cols", 1 << b)], axis=0)
    far = swap(core, "cols", 1)
    cores_new = whiten(
        z, 1.0 / scale_core, core.astype(jnp.float32), far.astype(jnp.float32), relations
    )
    return (factor_new, cores_new)


def solution(mesh):
    in_specs = (
        P(("rows", "cols"), None),
        P(),
        P(None, "rows", "cols", None),
        P(None, "rows", "cols"),
        P(None, "rows", "cols"),
        P(None, "rows", "cols"),
    )
    out_specs = (P(("rows", "cols"), None), P())
    return jax.shard_map(local, mesh=mesh, in_specs=in_specs, out_specs=out_specs, check_vma=False)
```

profile of v0, /device:TPU:0, one launch (start us, length us, event | category | flops | bytes accessed | tf_op | source)
XLA Modules:
  0.0 118.1 jit_solution(3849292348037793416)
XLA Ops:
  0.6 3.1 %collective-permute-start = (bf16[128,256]{1,0:T(8,128)(2,1)}, bf16[128,256]{1,0:T(8,128)(2,1)S(1)}, u32[]{:S(2)}, u32[]{:S(2)}) collective-permute-start(bf16[128,256]{1,0:T(8,128)(2,1)} %refs_0_.3), channel_id=1, source_target_pairs={{0,8},{4,12},{8,0},{12,4},{16,24},{20,28},{24,16},{28,20},{1,9},{5... | collective-permute-start | bytes 196616 | tf_op jit(solution)/shard_map/ppermute | solution.py:22
  3.7 2.6 %collective-permute-start.1 = (bf16[128,256]{1,0:T(8,128)(2,1)}, bf16[128,256]{1,0:T(8,128)(2,1)S(1)}, u32[]{:S(2)}, u32[]{:S(2)}) collective-permute-start(bf16[128,256]{1,0:T(8,128)(2,1)} %refs_0_.3), channel_id=1, source_target_pairs={{0,16},{4,20},{8,24},{12,28},{16,0},{20,4},{24,8},{28,12},{1,17},{... | collective-permute-start | bytes 196616 | tf_op jit(solution)/shard_map/ppermute | solution.py:22
  6.3 1.7 %collective-permute-start.3 = (bf16[128,256]{1,0:T(8,128)(2,1)}, bf16[128,256]{1,0:T(8,128)(2,1)S(1)}, u32[]{:S(2)}, u32[]{:S(2)}) collective-permute-start(bf16[128,256]{1,0:T(8,128)(2,1)} %refs_0_.3), channel_id=1, source_target_pairs={{0,4},{4,0},{8,12},{12,8},{16,20},{20,16},{24,28},{28,24},{1,5},{5... | collective-permute-start | bytes 196616 | tf_op jit(solution)/shard_map/ppermute | solution.py:22
  8.1 1.5 %collective-permute-start.8 = (bf16[128,256]{1,0:T(8,128)(2,1)}, bf16[128,256]{1,0:T(8,128)(2,1)S(1)}, u32[]{:S(2)}, u32[]{:S(2)}) collective-permute-start(bf16[128,256]{1,0:T(8,128)(2,1)} %refs_0_.3), channel_id=1, source_target_pairs={{0,2},{1,3},{2,0},{3,1},{4,6},{5,7},{6,4},{7,5},{8,10},{9,11},{10,... | collective-permute-start | bytes 196616 | tf_op jit(solution)/shard_map/ppermute | solution.py:22
  9.5 1.7 %collective-permute-done.1.refs_2_ = bf16[128,256]{1,0:T(8,128)(2,1)S(1)} collective-permute-done((bf16[128,256]{1,0:T(8,128)(2,1)}, bf16[128,256]{1,0:T(8,128)(2,1)S(1)}, u32[]{:S(2)}, u32[]{:S(2)}) %collective-permute-start.1) | collective-permute-done | bytes 65568 | tf_op jit(solution)/shard_map/ppermute | solution.py:22
  11.2 1.5 %collective-permute-start.4 = (bf16[128,256]{1,0:T(8,128)(2,1)S(1)}, bf16[128,256]{1,0:T(8,128)(2,1)S(1)}, u32[]{:S(2)}, u32[]{:S(2)}) collective-permute-start(bf16[128,256]{1,0:T(8,128)(2,1)S(1)} %collective-permute-done.refs_1_), channel_id=1, source_target_pairs={{0,4},{4,0},{8,12},{12,8},{16,20},{20,16},{24,28},{28,24},{1,5},{5... | collective-permute-start | bytes 196616 | tf_op jit(solution)/shard_map/ppermute | solution.py:22
  12.7 1.4 %collective-permute-start.5 = (bf16[128,256]{1,0:T(8,128)(2,1)S(1)}, bf16[128,256]{1,0:T(8,128)(2,1)S(1)}, u32[]{:S(2)}, u32[]{:S(2)}) collective-permute-start(bf16[128,256]{1,0:T(8,128)(2,1)S(1)} %collective-permute-done.1.refs_2_), channel_id=1, source_target_pairs={{0,4},{4,0},{8,12},{12,8},{16,20},{20,16},{24,28},{28,24},{1,5},{5... | collective-permute-start | bytes 196616 | tf_op jit(solution)/shard_map/ppermute | solution.py:22
  14.8 1.5 %collective-permute-start.9 = (bf16[128,256]{1,0:T(8,128)(2,1)S(1)}, bf16[128,256]{1,0:T(8,128)(2,1)S(1)}, u32[]{:S(2)}, u32[]{:S(2)}) collective-permute-start(bf16[128,256]{1,0:T(8,128)(2,1)S(1)} %collective-permute-done.7.refs_1_), channel_id=1, source_target_pairs={{0,2},{1,3},{2,0},{3,1},{4,6},{5,7},{6,4},{7,5},{8,10},{9,11},{10,... | collective-permute-start | bytes 196616 | tf_op jit(solution)/shard_map/ppermute | solution.py:22
  16.3 1.3 %fusion = (f32[4,256]{1,0:T(4,128)S(1)}, f32[4,256]{1,0:T(4,128)S(1)}) fusion(bf16[4,256,256]{2,1,0:T(8,128)(2,1)} %cores_ref.3), kind=kLoop, calls=%fused_computation.2 | loop fusion | flops 1046528 | bytes 532480 | tf_op jit(solution)/shard_map/reduce_sum | solution.py:396
  20.9 0.8 copy-done.4
  22.1 1.4 %copy-done = bf16[4,12,128,128]{3,2,1,0:T(8,128)(2,1)S(1)} copy-done((bf16[4,12,128,128]{3,2,1,0:T(8,128)(2,1)S(1)}, bf16[4,12,128,128]{3,2,1,0:T(8,128)(2,1)}, u32[]{:S(2)}) %copy-start) | copy-done | bytes 1572888
  23.5 1.0 copy-done.2
  25.9 4.8 %first_pass.1 = (f32[4,128,256]{2,1,0:T(8,128)S(1)}, f32[8,128,256]{2,1,0:T(8,128)S(1)}) custom-call(s32[4,1,12]{2,1,0:T(1,128)S(1)} %copy-done.6, s32[4,1,12]{2,1,0:T(1,128)S(1)} %copy-done.8, s32[4,1,1]{2,1,0:T(1,128)S(1)} %copy.10.counts_ref, bf16[4,12,128,128]{3,2,1,0:T(8,128)(2,1)S(1)} %copy-done, bf16[8,128,256]{2,1,0:T(8,128)(2,1)S(1)} %bitcast.29, ...), custom_call_target="tpu_custom_call" | custom-call | tf_op jit(solution)/shard_map/first_pass/pallas_call | solution.py:150
  30.8 1.5 %collective-permute-start.14 = (f16[2,128,256]{2,1,0:T(8,128)(2,1)S(1)}, f16[2,128,256]{2,1,0:T(8,128)(2,1)S(1)}, u32[]{:S(2)}, u32[]{:S(2)}) collective-permute-start(f16[2,128,256]{2,1,0:T(8,128)(2,1)S(1)} %multiply_convert_fusion.1), channel_id=1, source_target_pairs={{0,4},{4,0},{8,12},{12,8},{16,20},{20,16},{24,28},{28,24},{1,5},{5... | collective-permute-start | bytes 393224 | tf_op jit(solution)/shard_map/ppermute | solution.py:22
  32.8 3.1 %collective-permute-done.14 = f16[2,128,256]{2,1,0:T(8,128)(2,1)S(1)} collective-permute-done((f16[2,128,256]{2,1,0:T(8,128)(2,1)S(1)}, f16[2,128,256]{2,1,0:T(8,128)(2,1)S(1)}, u32[]{:S(2)}, u32[]{:S(2)}) %collective-permute-start.14) | collective-permute-done | bytes 131104 | tf_op jit(solution)/shard_map/ppermute | solution.py:22
  36.1 2.3 %collective-permute-start.12 = (f16[2,128,256]{2,1,0:T(8,128)(2,1)S(1)}, f16[2,128,256]{2,1,0:T(8,128)(2,1)S(1)}, u32[]{:S(2)}, u32[]{:S(2)}) collective-permute-start(f16[2,128,256]{2,1,0:T(8,128)(2,1)S(1)} %get-tuple-element.17), channel_id=1, source_target_pairs={{0,4},{4,0},{8,12},{12,8},{16,20},{20,16},{24,28},{28,24},{1,5},{5... | collective-permute-start | bytes 393224 | tf_op jit(solution)/shard_map/ppermute | solution.py:22
  38.4 1.2 collective-permute-start.15
  39.6 0.8 collective-permute-start.16
  41.4 1.3 %collective-permute-start.13 = (f16[128,256]{1,0:T(8,128)(2,1)S(1)}, f16[128,256]{1,0:T(8,128)(2,1)S(1)}, u32[]{:S(2)}, u32[]{:S(2)}) collective-permute-start(f16[128,256]{1,0:T(8,128)(2,1)S(1)} %fusion.21), channel_id=1, source_target_pairs={{0,8},{4,12},{8,0},{12,4},{16,24},{20,28},{24,16},{28,20},{1,9},{5... | collective-permute-start | bytes 196616 | tf_op jit(solution)/shard_map/ppermute | solution.py:22
  42.8 1.6 %collective-permute-start.11 = (f16[1,128,256]{2,1,0:T(8,128)(2,1)S(1)}, f16[1,128,256]{2,1,0:T(8,128)(2,1)S(1)}, u32[]{:S(2)}, u32[]{:S(2)}) collective-permute-start(f16[1,128,256]{2,1,0:T(8,128)(2,1)S(1)} %fusion.11), channel_id=1, source_target_pairs={{0,2},{1,3},{2,0},{3,1},{4,6},{5,7},{6,4},{7,5},{8,10},{9,11},{10,... | collective-permute-start | bytes 196616 | tf_op jit(solution)/shard_map/ppermute | solution.py:22
  44.4 1.8 %collective-permute-done.18.other_ref = f32[3,128,128]{2,1,0:T(8,128)S(1)} collective-permute-done((f32[3,128,128]{2,1,0:T(8,128)S(1)}, f32[3,128,128]{2,1,0:T(8,128)S(1)}, u32[]{:S(2)}, u32[]{:S(2)}) %collective-permute-start.18) | collective-permute-done | bytes 196640 | tf_op jit(solution)/shard_map/ppermute | solution.py:22
  46.1 9.3 %system_inverse.1 = f32[256,256]{1,0:T(8,128)S(1)} custom-call(f32[3,128,128]{2,1,0:T(8,128)S(1)} %add.70.mine_ref, f32[3,128,128]{2,1,0:T(8,128)S(1)} %collective-permute-done.18.other_ref, bf16[4,256,256]{2,1,0:T(8,128)(2,1)S(1)} %copy-done.3), custom_call_target="tpu_custom_call" | custom-call | flops 8999999488 | bytes 1500000 | tf_op jit(solution)/shard_map/system_inverse/pallas_call | solution.py:305
  55.9 1.7 %collective-permute-start.19 = (bf16[128,256]{1,0:T(8,128)(2,1)S(1)}, bf16[128,256]{1,0:T(8,128)(2,1)S(1)}, u32[]{:S(2)}, u32[]{:S(2)}) collective-permute-start(bf16[128,256]{1,0:T(8,128)(2,1)S(1)} %convolution_convert_fusion.refs_0_), channel_id=1, source_target_pairs={{0,8},{4,12},{8,0},{12,4},{16,24},{20,28},{24,16},{28,20},{1,9},{5... | collective-permute-start | bytes 196616 | tf_op jit(solution)/shard_map/ppermute | solution.py:22
  57.6 2.0 %collective-permute-start.20 = (bf16[128,256]{1,0:T(8,128)(2,1)S(1)}, bf16[128,256]{1,0:T(8,128)(2,1)S(1)}, u32[]{:S(2)}, u32[]{:S(2)}) collective-permute-start(bf16[128,256]{1,0:T(8,128)(2,1)S(1)} %convolution_convert_fusion.refs_0_), channel_id=1, source_target_pairs={{0,16},{4,20},{8,24},{12,28},{16,0},{20,4},{24,8},{28,12},{1,17},{... | collective-permute-start | bytes 196616 | tf_op jit(solution)/shard_map/ppermute | solution.py:22
  60.3 2.0 %collective-permute-start.22 = (bf16[128,256]{1,0:T(8,128)(2,1)S(1)}, bf16[128,256]{1,0:T(8,128)(2,1)S(1)}, u32[]{:S(2)}, u32[]{:S(2)}) collective-permute-start(bf16[128,256]{1,0:T(8,128)(2,1)S(1)} %convolution_convert_fusion.refs_0_), channel_id=1, source_target_pairs={{0,4},{4,0},{8,12},{12,8},{16,20},{20,16},{24,28},{28,24},{1,5},{5... | collective-permute-start | bytes 196616 | tf_op jit(solution)/shard_map/ppermute | solution.py:22
  62.4 0.9 collective-permute-done.20.refs_2_
  63.3 1.1 collective-permute-start.24
  64.4 1.2 %collective-permute-done.21.refs_3_ = bf16[128,256]{1,0:T(8,128)(2,1)S(1)} collective-permute-done((bf16[128,256]{1,0:T(8,128)(2,1)S(1)}, bf16[128,256]{1,0:T(8,128)(2,1)S(1)}, u32[]{:S(2)}, u32[]{:S(2)}) %collective-permute-start.21) | collective-permute-done | bytes 65568 | tf_op jit(solution)/shard_map/ppermute | solution.py:22
  66.7 1.5 %collective-permute-start.30 = (bf16[128,256]{1,0:T(8,128)(2,1)S(1)}, bf16[128,256]{1,0:T(8,128)(2,1)S(1)}, u32[]{:S(2)}, u32[]{:S(2)}) collective-permute-start(bf16[128,256]{1,0:T(8,128)(2,1)S(1)} %collective-permute-done.28.refs_1_), channel_id=1, source_target_pairs={{0,2},{1,3},{2,0},{3,1},{4,6},{5,7},{6,4},{7,5},{8,10},{9,11},{10,... | collective-permute-start | bytes 196616 | tf_op jit(solution)/shard_map/ppermute | solution.py:22
  68.6 1.2 %collective-permute-done.25.refs_7_ = bf16[128,256]{1,0:T(8,128)(2,1)S(1)} collective-permute-done((bf16[128,256]{1,0:T(8,128)(2,1)S(1)}, bf16[128,256]{1,0:T(8,128)(2,1)S(1)}, u32[]{:S(2)}, u32[]{:S(2)}) %collective-permute-start.25) | collective-permute-done | bytes 65568 | tf_op jit(solution)/shard_map/ppermute | solution.py:22
  71.1 2.8 %second_pass.1 = f32[4,2,128,256]{3,2,1,0:T(8,128)S(1)} custom-call(s32[4,1,12]{2,1,0:T(1,128)S(1)} %copy-done.7, s32[4,1,12]{2,1,0:T(1,128)S(1)} %copy-done.9, s32[4,1,1]{2,1,0:T(1,128)S(1)} %copy.10.counts_ref, bf16[4,12,128,128]{3,2,1,0:T(8,128)(2,1)S(1)} %copy-done.1, bf16[8,128,256]{2,1,0:T(8,128)(2,1)S(1)} %bitcast.30, ...), custom_call_target="tpu_custom_call" | custom-call | tf_op jit(solution)/shard_map/second_pass/pallas_call | solution.py:204
  74.6 1.7 %collective-permute-done.26 = f32[3,128,128]{2,1,0:T(8,128)S(1)} collective-permute-done((f32[3,128,128]{2,1,0:T(8,128)S(1)}, f32[3,128,128]{2,1,0:T(8,128)S(1)}, u32[]{:S(2)}, u32[]{:S(2)}) %collective-permute-start.26) | collective-permute-done | bytes 196640 | tf_op jit(solution)/shard_map/ppermute | solution.py:22
  76.3 1.4 %collective-permute-start.27 = (f32[3,128,128]{2,1,0:T(8,128)S(1)}, f32[3,128,128]{2,1,0:T(8,128)S(1)}, u32[]{:S(2)}, u32[]{:S(2)}) collective-permute-start(f32[3,128,128]{2,1,0:T(8,128)S(1)} %add.71.mine_ref), channel_id=1, source_target_pairs={{0,2},{1,3},{2,0},{3,1},{4,6},{5,7},{6,4},{7,5},{8,10},{9,11},{10,... | collective-permute-start | bytes 589832 | tf_op jit(solution)/shard_map/ppermute | solution.py:22
  77.7 5.6 %collective-permute-done.27.other_ref = f32[3,128,128]{2,1,0:T(8,128)S(1)} collective-permute-done((f32[3,128,128]{2,1,0:T(8,128)S(1)}, f32[3,128,128]{2,1,0:T(8,128)S(1)}, u32[]{:S(2)}, u32[]{:S(2)}) %collective-permute-start.27) | collective-permute-done | bytes 196640 | tf_op jit(solution)/shard_map/ppermute | solution.py:22
  84.8 1.4 %collective-permute-start.32 = (f16[1,2,128,256]{3,2,1,0:T(8,128)(2,1)S(1)}, f16[1,2,128,256]{3,2,1,0:T(8,128)(2,1)S(1)}, u32[]{:S(2)}, u32[]{:S(2)}) collective-permute-start(f16[1,2,128,256]{3,2,1,0:T(8,128)(2,1)S(1)} %fusion.2), channel_id=1, source_target_pairs={{0,2},{1,3},{2,0},{3,1},{4,6},{5,7},{6,4},{7,5},{8,10},{9,11},{10,... | collective-permute-start | bytes 393224 | tf_op jit(solution)/shard_map/ppermute | solution.py:22
  86.2 3.6 %collective-permute-done.32 = f16[1,2,128,256]{3,2,1,0:T(8,128)(2,1)S(1)} collective-permute-done((f16[1,2,128,256]{3,2,1,0:T(8,128)(2,1)S(1)}, f16[1,2,128,256]{3,2,1,0:T(8,128)(2,1)S(1)}, u32[]{:S(2)}, u32[]{:S(2)}) %collective-permute-start.32) | collective-permute-done | bytes 131104 | tf_op jit(solution)/shard_map/ppermute | solution.py:22
  89.9 1.6 %collective-permute-start.33 = (f16[128,256]{1,0:T(8,128)(2,1)S(1)}, f16[128,256]{1,0:T(8,128)(2,1)S(1)}, u32[]{:S(2)}, u32[]{:S(2)}) collective-permute-start(f16[128,256]{1,0:T(8,128)(2,1)S(1)} %fusion.22), channel_id=1, source_target_pairs={{0,4},{4,0},{8,12},{12,8},{16,20},{20,16},{24,28},{28,24},{1,5},{5... | collective-permute-start | bytes 196616 | tf_op jit(solution)/shard_map/ppermute | solution.py:22
  91.4 2.8 %collective-permute-done.33 = f16[128,256]{1,0:T(8,128)(2,1)S(1)} collective-permute-done((f16[128,256]{1,0:T(8,128)(2,1)S(1)}, f16[128,256]{1,0:T(8,128)(2,1)S(1)}, u32[]{:S(2)}, u32[]{:S(2)}) %collective-permute-start.33) | collective-permute-done | bytes 65568 | tf_op jit(solution)/shard_map/ppermute | solution.py:22
  94.2 0.8 collective-permute-start.34
  95.0 2.1 %collective-permute-start.35 = (f16[128,256]{1,0:T(8,128)(2,1)S(1)}, f16[128,256]{1,0:T(8,128)(2,1)S(1)}, u32[]{:S(2)}, u32[]{:S(2)}) collective-permute-start(f16[128,256]{1,0:T(8,128)(2,1)S(1)} %fusion.6), channel_id=1, source_target_pairs={{0,16},{4,20},{8,24},{12,28},{16,0},{20,4},{24,8},{28,12},{1,17},{... | collective-permute-start | bytes 196616 | tf_op jit(solution)/shard_map/ppermute | solution.py:22
  97.1 1.6 %collective-permute-start.36 = (f16[128,256]{1,0:T(8,128)(2,1)S(1)}, f16[128,256]{1,0:T(8,128)(2,1)S(1)}, u32[]{:S(2)}, u32[]{:S(2)}) collective-permute-start(f16[128,256]{1,0:T(8,128)(2,1)S(1)} %fusion.6), channel_id=1, source_target_pairs={{0,24},{4,28},{8,16},{12,20},{16,8},{20,12},{24,0},{28,4},{1,25},{... | collective-permute-start | bytes 196616 | tf_op jit(solution)/shard_map/ppermute | solution.py:22
  99.3 0.9 collective-permute-done.35
  100.2 3.0 %collective-permute-done.36 = f16[128,256]{1,0:T(8,128)(2,1)S(1)} collective-permute-done((f16[128,256]{1,0:T(8,128)(2,1)S(1)}, f16[128,256]{1,0:T(8,128)(2,1)S(1)}, u32[]{:S(2)}, u32[]{:S(2)}) %collective-permute-start.36) | collective-permute-done | bytes 65568 | tf_op jit(solution)/shard_map/ppermute | solution.py:22
  103.7 3.9 %collective-permute-done.37 = f16[1,128,256]{2,1,0:T(8,128)(2,1)S(1)} collective-permute-done((f16[1,128,256]{2,1,0:T(8,128)(2,1)S(1)}, f16[1,128,256]{2,1,0:T(8,128)(2,1)S(1)}, u32[]{:S(2)}, u32[]{:S(2)}) %collective-permute-start.37) | collective-permute-done | bytes 65568 | tf_op jit(solution)/shard_map/ppermute | solution.py:22
  107.6 1.4 %collective-permute-start.38 = (f16[1,2,128,256]{3,2,1,0:T(8,128)(2,1)S(1)}, f16[1,2,128,256]{3,2,1,0:T(8,128)(2,1)S(1)}, u32[]{:S(2)}, u32[]{:S(2)}) collective-permute-start(f16[1,2,128,256]{3,2,1,0:T(8,128)(2,1)S(1)} %maximum_bitcast_fusion), channel_id=1, source_target_pairs={{0,2},{1,3},{2,0},{3,1},{4,6},{5,7},{6,4},{7,5},{8,10},{9,11},{10,... | collective-permute-start | bytes 393224 | tf_op jit(solution)/shard_map/ppermute | solution.py:22
  109.0 3.3 %begin.1.in_ref = f32[256,256]{1,0:T(8,128)S(1)} custom-call(f32[3,128,128]{2,1,0:T(8,128)S(1)} %add.71.mine_ref, f32[3,128,128]{2,1,0:T(8,128)S(1)} %collective-permute-done.27.other_ref), custom_call_target="tpu_custom_call" | custom-call | flops 3500000000 | bytes 500000 | tf_op jit(solution)/shard_map/begin/pallas_call | solution.py:335
  112.8 3.0 %end.1.z_ref = f32[256,256]{1,0:T(8,128)S(1)} custom-call(f32[256,256]{1,0:T(8,128)S(1)} %begin.1.in_ref), custom_call_target="tpu_custom_call" | custom-call | flops 3500000000 | bytes 500000 | tf_op jit(solution)/shard_map/end/pallas_call | solution.py:335
  115.8 2.3 %whiten.1 = f32[4,256,256]{2,1,0:T(8,128)} custom-call(f32[256,256]{1,0:T(8,128)S(1)} %end.1.z_ref, f32[1]{0:T(128)} %bitcast.5.factor_ref, f32[2,2,128,256]{3,2,1,0:T(8,128)S(1)} %get-tuple-element.19.near_ref, f32[2,2,128,256]{3,2,1,0:T(8,128)S(1)} %convert_element_type.103.far_ref), custom_call_target="tpu_custom_call" | custom-call | tf_op jit(solution)/shard_map/whiten/pallas_call | solution.py:373
  (86 shorter events, 13.2 us)
Async XLA Ops:
  0.6 7.4 %collective-permute-start = (bf16[128,256]{1,0:T(8,128)(2,1)}, bf16[128,256]{1,0:T(8,128)(2,1)S(1)}, u32[]{:S(2)}, u32[]{:S(2)}) collective-permute-start(bf16[128,256]{1,0:T(8,128)(2,1)} %refs_0_.3), channel_id=1, source_target_pairs={{0,8},{4,12},{8,0},{12,4},{16,24},{20,28},{24,16},{28,20},{1,9},{5... | collective-permute-start | bytes 196616 | tf_op jit(solution)/shard_map/ppermute | solution.py:22
  3.7 7.5 %collective-permute-start.1 = (bf16[128,256]{1,0:T(8,128)(2,1)}, bf16[128,256]{1,0:T(8,128)(2,1)S(1)}, u32[]{:S(2)}, u32[]{:S(2)}) collective-permute-start(bf16[128,256]{1,0:T(8,128)(2,1)} %refs_0_.3), channel_id=1, source_target_pairs={{0,16},{4,20},{8,24},{12,28},{16,0},{20,4},{24,8},{28,12},{1,17},{... | collective-permute-start | bytes 196616 | tf_op jit(solution)/shard_map/ppermute | solution.py:22
  6.3 6.4 %collective-permute-start.2 = (bf16[128,256]{1,0:T(8,128)(2,1)}, bf16[128,256]{1,0:T(8,128)(2,1)S(1)}, u32[]{:S(2)}, u32[]{:S(2)}) collective-permute-start(bf16[128,256]{1,0:T(8,128)(2,1)} %refs_0_.3), channel_id=1, source_target_pairs={{0,24},{4,28},{8,16},{12,20},{16,8},{20,12},{24,0},{28,4},{1,25},{... | collective-permute-start | bytes 196616 | tf_op jit(solution)/shard_map/ppermute | solution.py:22
  6.3 7.8 %collective-permute-start.3 = (bf16[128,256]{1,0:T(8,128)(2,1)}, bf16[128,256]{1,0:T(8,128)(2,1)S(1)}, u32[]{:S(2)}, u32[]{:S(2)}) collective-permute-start(bf16[128,256]{1,0:T(8,128)(2,1)} %refs_0_.3), channel_id=1, source_target_pairs={{0,4},{4,0},{8,12},{12,8},{16,20},{20,16},{24,28},{28,24},{1,5},{5... | collective-permute-start | bytes 196616 | tf_op jit(solution)/shard_map/ppermute | solution.py:22
  8.0 6.7 %collective-permute-start.7 = (bf16[128,256]{1,0:T(8,128)(2,1)}, bf16[128,256]{1,0:T(8,128)(2,1)S(1)}, u32[]{:S(2)}, u32[]{:S(2)}) collective-permute-start(bf16[128,256]{1,0:T(8,128)(2,1)} %refs_0_.3), channel_id=1, source_target_pairs={{0,1},{1,0},{2,3},{3,2},{4,5},{5,4},{6,7},{7,6},{8,9},{9,8},{10,11... | collective-permute-start | bytes 196616 | tf_op jit(solution)/shard_map/ppermute | solution.py:22
  8.1 14.0 %collective-permute-start.8 = (bf16[128,256]{1,0:T(8,128)(2,1)}, bf16[128,256]{1,0:T(8,128)(2,1)S(1)}, u32[]{:S(2)}, u32[]{:S(2)}) collective-permute-start(bf16[128,256]{1,0:T(8,128)(2,1)} %refs_0_.3), channel_id=1, source_target_pairs={{0,2},{1,3},{2,0},{3,1},{4,6},{5,7},{6,4},{7,5},{8,10},{9,11},{10,... | collective-permute-start | bytes 196616 | tf_op jit(solution)/shard_map/ppermute | solution.py:22
  11.2 9.6 %collective-permute-start.4 = (bf16[128,256]{1,0:T(8,128)(2,1)S(1)}, bf16[128,256]{1,0:T(8,128)(2,1)S(1)}, u32[]{:S(2)}, u32[]{:S(2)}) collective-permute-start(bf16[128,256]{1,0:T(8,128)(2,1)S(1)} %collective-permute-done.refs_1_), channel_id=1, source_target_pairs={{0,4},{4,0},{8,12},{12,8},{16,20},{20,16},{24,28},{28,24},{1,5},{5... | collective-permute-start | bytes 196616 | tf_op jit(solution)/shard_map/ppermute | solution.py:22
  12.7 8.1 %collective-permute-start.5 = (bf16[128,256]{1,0:T(8,128)(2,1)S(1)}, bf16[128,256]{1,0:T(8,128)(2,1)S(1)}, u32[]{:S(2)}, u32[]{:S(2)}) collective-permute-start(bf16[128,256]{1,0:T(8,128)(2,1)S(1)} %collective-permute-done.1.refs_2_), channel_id=1, source_target_pairs={{0,4},{4,0},{8,12},{12,8},{16,20},{20,16},{24,28},{28,24},{1,5},{5... | collective-permute-start | bytes 196616 | tf_op jit(solution)/shard_map/ppermute | solution.py:22
  14.1 6.7 %collective-permute-start.6 = (bf16[128,256]{1,0:T(8,128)(2,1)S(1)}, bf16[128,256]{1,0:T(8,128)(2,1)S(1)}, u32[]{:S(2)}, u32[]{:S(2)}) collective-permute-start(bf16[128,256]{1,0:T(8,128)(2,1)S(1)} %collective-permute-done.2.refs_3_), channel_id=1, source_target_pairs={{0,4},{4,0},{8,12},{12,8},{16,20},{20,16},{24,28},{28,24},{1,5},{5... | collective-permute-start | bytes 196616 | tf_op jit(solution)/shard_map/ppermute | solution.py:22
  14.8 7.3 %collective-permute-start.9 = (bf16[128,256]{1,0:T(8,128)(2,1)S(1)}, bf16[128,256]{1,0:T(8,128)(2,1)S(1)}, u32[]{:S(2)}, u32[]{:S(2)}) collective-permute-start(bf16[128,256]{1,0:T(8,128)(2,1)S(1)} %collective-permute-done.7.refs_1_), channel_id=1, source_target_pairs={{0,2},{1,3},{2,0},{3,1},{4,6},{5,7},{6,4},{7,5},{8,10},{9,11},{10,... | collective-permute-start | bytes 196616 | tf_op jit(solution)/shard_map/ppermute | solution.py:22
  20.8 0.8 copy-start.4
  22.1 1.4 %copy-start = (bf16[4,12,128,128]{3,2,1,0:T(8,128)(2,1)S(1)}, bf16[4,12,128,128]{3,2,1,0:T(8,128)(2,1)}, u32[]{:S(2)}) copy-start(bf16[4,12,128,128]{3,2,1,0:T(8,128)(2,1)} %tiles_ref.3) | copy-start | bytes 4718596
  23.5 1.0 copy-start.2
  30.8 5.2 %collective-permute-start.14 = (f16[2,128,256]{2,1,0:T(8,128)(2,1)S(1)}, f16[2,128,256]{2,1,0:T(8,128)(2,1)S(1)}, u32[]{:S(2)}, u32[]{:S(2)}) collective-permute-start(f16[2,128,256]{2,1,0:T(8,128)(2,1)S(1)} %multiply_convert_fusion.1), channel_id=1, source_target_pairs={{0,4},{4,0},{8,12},{12,8},{16,20},{20,16},{24,28},{28,24},{1,5},{5... | collective-permute-start | bytes 393224 | tf_op jit(solution)/shard_map/ppermute | solution.py:22
  32.2 8.1 %collective-permute-start.17 = (f32[3,128,128]{2,1,0:T(8,128)S(1)}, f32[3,128,128]{2,1,0:T(8,128)S(1)}, u32[]{:S(2)}, u32[]{:S(2)}) collective-permute-start(f32[3,128,128]{2,1,0:T(8,128)S(1)} %get-tuple-element.11), channel_id=1, source_target_pairs={{0,1},{1,0},{2,3},{3,2},{4,5},{5,4},{6,7},{7,6},{8,9},{9,8},{10,11... | collective-permute-start | bytes 589832 | tf_op jit(solution)/shard_map/ppermute | solution.py:22
  32.3 10.5 %collective-permute-start.10 = (f32[2,128,256]{2,1,0:T(8,128)S(1)}, f32[2,128,256]{2,1,0:T(8,128)S(1)}, u32[]{:S(2)}, u32[]{:S(2)}) collective-permute-start(f32[2,128,256]{2,1,0:T(8,128)S(1)} %split.25), channel_id=1, source_target_pairs={{0,1},{1,0},{2,3},{3,2},{4,5},{5,4},{6,7},{7,6},{8,9},{9,8},{10,11... | collective-permute-start | bytes 786440 | tf_op jit(solution)/shard_map/ppermute | solution.py:22
  36.0 10.1 %copy-start.3 = (bf16[4,256,256]{2,1,0:T(8,128)(2,1)S(1)}, bf16[4,256,256]{2,1,0:T(8,128)(2,1)}, u32[]{:S(2)}) copy-start(bf16[4,256,256]{2,1,0:T(8,128)(2,1)} %cores_ref.3) | copy-start | bytes 1572868
  36.1 5.3 %collective-permute-start.12 = (f16[2,128,256]{2,1,0:T(8,128)(2,1)S(1)}, f16[2,128,256]{2,1,0:T(8,128)(2,1)S(1)}, u32[]{:S(2)}, u32[]{:S(2)}) collective-permute-start(f16[2,128,256]{2,1,0:T(8,128)(2,1)S(1)} %get-tuple-element.17), channel_id=1, source_target_pairs={{0,4},{4,0},{8,12},{12,8},{16,20},{20,16},{24,28},{28,24},{1,5},{5... | collective-permute-start | bytes 393224 | tf_op jit(solution)/shard_map/ppermute | solution.py:22
  38.4 17.1 %collective-permute-start.15 = (f16[128,256]{1,0:T(8,128)(2,1)S(1)}, f16[128,256]{1,0:T(8,128)(2,1)S(1)}, u32[]{:S(2)}, u32[]{:S(2)}) collective-permute-start(f16[128,256]{1,0:T(8,128)(2,1)S(1)} %get-tuple-element.20), channel_id=1, source_target_pairs={{0,16},{4,20},{8,24},{12,28},{16,0},{20,4},{24,8},{28,12},{1,17},{... | collective-permute-start | bytes 196616 | tf_op jit(solution)/shard_map/ppermute | solution.py:22
  39.6 15.9 %collective-permute-start.16 = (f16[128,256]{1,0:T(8,128)(2,1)S(1)}, f16[128,256]{1,0:T(8,128)(2,1)S(1)}, u32[]{:S(2)}, u32[]{:S(2)}) collective-permute-start(f16[128,256]{1,0:T(8,128)(2,1)S(1)} %get-tuple-element.21), channel_id=1, source_target_pairs={{0,24},{4,28},{8,16},{12,20},{16,8},{20,12},{24,0},{28,4},{1,25},{... | collective-permute-start | bytes 196616 | tf_op jit(solution)/shard_map/ppermute | solution.py:22
  40.4 5.7 %collective-permute-start.18 = (f32[3,128,128]{2,1,0:T(8,128)S(1)}, f32[3,128,128]{2,1,0:T(8,128)S(1)}, u32[]{:S(2)}, u32[]{:S(2)}) collective-permute-start(f32[3,128,128]{2,1,0:T(8,128)S(1)} %add.70.mine_ref), channel_id=1, source_target_pairs={{0,2},{1,3},{2,0},{3,1},{4,6},{5,7},{6,4},{7,5},{8,10},{9,11},{10,... | collective-permute-start | bytes 589832 | tf_op jit(solution)/shard_map/ppermute | solution.py:22
  41.4 14.1 %collective-permute-start.13 = (f16[128,256]{1,0:T(8,128)(2,1)S(1)}, f16[128,256]{1,0:T(8,128)(2,1)S(1)}, u32[]{:S(2)}, u32[]{:S(2)}) collective-permute-start(f16[128,256]{1,0:T(8,128)(2,1)S(1)} %fusion.21), channel_id=1, source_target_pairs={{0,8},{4,12},{8,0},{12,4},{16,24},{20,28},{24,16},{28,20},{1,9},{5... | collective-permute-start | bytes 196616 | tf_op jit(solution)/shard_map/ppermute | solution.py:22
  42.8 12.7 %collective-permute-start.11 = (f16[1,128,256]{2,1,0:T(8,128)(2,1)S(1)}, f16[1,128,256]{2,1,0:T(8,128)(2,1)S(1)}, u32[]{:S(2)}, u32[]{:S(2)}) collective-permute-start(f16[1,128,256]{2,1,0:T(8,128)(2,1)S(1)} %fusion.11), channel_id=1, source_target_pairs={{0,2},{1,3},{2,0},{3,1},{4,6},{5,7},{6,4},{7,5},{8,10},{9,11},{10,... | collective-permute-start | bytes 196616 | tf_op jit(solution)/shard_map/ppermute | solution.py:22
  55.5 15.7 %copy-start.1 = (bf16[4,12,128,128]{3,2,1,0:T(8,128)(2,1)S(1)}, bf16[4,12,128,128]{3,2,1,0:T(8,128)(2,1)}, u32[]{:S(2)}) copy-start(bf16[4,12,128,128]{3,2,1,0:T(8,128)(2,1)} %tiles_ref.3) | copy-start | bytes 4718596
  55.5 15.7 %copy-start.7 = (s32[4,1,12]{2,1,0:T(1,128)S(1)}, s32[4,1,12]{2,1,0:T(1,128)}, u32[]{:S(2)}) copy-start(s32[4,1,12]{2,1,0:T(1,128)} %rows_ref.3) | copy-start | bytes 580
  55.5 15.6 %copy-start.9 = (s32[4,1,12]{2,1,0:T(1,128)S(1)}, s32[4,1,12]{2,1,0:T(1,128)}, u32[]{:S(2)}) copy-start(s32[4,1,12]{2,1,0:T(1,128)} %cols_ref.3) | copy-start | bytes 580
  55.9 18.1 %copy-start.5 = (bf16[128,256]{1,0:T(8,128)(2,1)}, bf16[128,256]{1,0:T(8,128)(2,1)S(1)}, u32[]{:S(2)}) copy-start(bf16[128,256]{1,0:T(8,128)(2,1)S(1)} %convolution_convert_fusion.refs_0_) | copy-start | bytes 196612
  55.9 6.5 %collective-permute-start.19 = (bf16[128,256]{1,0:T(8,128)(2,1)S(1)}, bf16[128,256]{1,0:T(8,128)(2,1)S(1)}, u32[]{:S(2)}, u32[]{:S(2)}) collective-permute-start(bf16[128,256]{1,0:T(8,128)(2,1)S(1)} %convolution_convert_fusion.refs_0_), channel_id=1, source_target_pairs={{0,8},{4,12},{8,0},{12,4},{16,24},{20,28},{24,16},{28,20},{1,9},{5... | collective-permute-start | bytes 196616 | tf_op jit(solution)/shard_map/ppermute | solution.py:22
  57.6 5.7 %collective-permute-start.20 = (bf16[128,256]{1,0:T(8,128)(2,1)S(1)}, bf16[128,256]{1,0:T(8,128)(2,1)S(1)}, u32[]{:S(2)}, u32[]{:S(2)}) collective-permute-start(bf16[128,256]{1,0:T(8,128)(2,1)S(1)} %convolution_convert_fusion.refs_0_), channel_id=1, source_target_pairs={{0,16},{4,20},{8,24},{12,28},{16,0},{20,4},{24,8},{28,12},{1,17},{... | collective-permute-start | bytes 196616 | tf_op jit(solution)/shard_map/ppermute | solution.py:22
  59.6 6.1 %collective-permute-start.21 = (bf16[128,256]{1,0:T(8,128)(2,1)S(1)}, bf16[128,256]{1,0:T(8,128)(2,1)S(1)}, u32[]{:S(2)}, u32[]{:S(2)}) collective-permute-start(bf16[128,256]{1,0:T(8,128)(2,1)S(1)} %convolution_convert_fusion.refs_0_), channel_id=1, source_target_pairs={{0,24},{4,28},{8,16},{12,20},{16,8},{20,12},{24,0},{28,4},{1,25},{... | collective-permute-start | bytes 196616 | tf_op jit(solution)/shard_map/ppermute | solution.py:22
  60.3 5.8 %collective-permute-start.22 = (bf16[128,256]{1,0:T(8,128)(2,1)S(1)}, bf16[128,256]{1,0:T(8,128)(2,1)S(1)}, u32[]{:S(2)}, u32[]{:S(2)}) collective-permute-start(bf16[128,256]{1,0:T(8,128)(2,1)S(1)} %convolution_convert_fusion.refs_0_), channel_id=1, source_target_pairs={{0,4},{4,0},{8,12},{12,8},{16,20},{20,16},{24,28},{28,24},{1,5},{5... | collective-permute-start | bytes 196616 | tf_op jit(solution)/shard_map/ppermute | solution.py:22
  62.3 4.4 %collective-permute-start.28 = (bf16[128,256]{1,0:T(8,128)(2,1)S(1)}, bf16[128,256]{1,0:T(8,128)(2,1)S(1)}, u32[]{:S(2)}, u32[]{:S(2)}) collective-permute-start(bf16[128,256]{1,0:T(8,128)(2,1)S(1)} %convolution_convert_fusion.refs_0_), channel_id=1, source_target_pairs={{0,1},{1,0},{2,3},{3,2},{4,5},{5,4},{6,7},{7,6},{8,9},{9,8},{10,11... | collective-permute-start | bytes 196616 | tf_op jit(solution)/shard_map/ppermute | solution.py:22
  62.3 5.8 %collective-permute-start.23 = (bf16[128,256]{1,0:T(8,128)(2,1)S(1)}, bf16[128,256]{1,0:T(8,128)(2,1)S(1)}, u32[]{:S(2)}, u32[]{:S(2)}) collective-permute-start(bf16[128,256]{1,0:T(8,128)(2,1)S(1)} %collective-permute-done.19.refs_1_), channel_id=1, source_target_pairs={{0,4},{4,0},{8,12},{12,8},{16,20},{20,16},{24,28},{28,24},{1,5},{5... | collective-permute-start | bytes 196616 | tf_op jit(solution)/shard_map/ppermute | solution.py:22
  63.3 5.4 %collective-permute-start.24 = (bf16[128,256]{1,0:T(8,128)(2,1)S(1)}, bf16[128,256]{1,0:T(8,128)(2,1)S(1)}, u32[]{:S(2)}, u32[]{:S(2)}) collective-permute-start(bf16[128,256]{1,0:T(8,128)(2,1)S(1)} %collective-permute-done.20.refs_2_), channel_id=1, source_target_pairs={{0,4},{4,0},{8,12},{12,8},{16,20},{20,16},{24,28},{28,24},{1,5},{5... | collective-permute-start | bytes 196616 | tf_op jit(solution)/shard_map/ppermute | solution.py:22
  65.6 4.3 %collective-permute-start.25 = (bf16[128,256]{1,0:T(8,128)(2,1)S(1)}, bf16[128,256]{1,0:T(8,128)(2,1)S(1)}, u32[]{:S(2)}, u32[]{:S(2)}) collective-permute-start(bf16[128,256]{1,0:T(8,128)(2,1)S(1)} %collective-permute-done.21.refs_3_), channel_id=1, source_target_pairs={{0,4},{4,0},{8,12},{12,8},{16,20},{20,16},{24,28},{28,24},{1,5},{5... | collective-permute-start | bytes 196616 | tf_op jit(solution)/shard_map/ppermute | solution.py:22
  66.2 4.3 %collective-permute-start.29 = (bf16[128,256]{1,0:T(8,128)(2,1)S(1)}, bf16[128,256]{1,0:T(8,128)(2,1)S(1)}, u32[]{:S(2)}, u32[]{:S(2)}) collective-permute-start(bf16[128,256]{1,0:T(8,128)(2,1)S(1)} %convolution_convert_fusion.refs_0_), channel_id=1, source_target_pairs={{0,2},{1,3},{2,0},{3,1},{4,6},{5,7},{6,4},{7,5},{8,10},{9,11},{10,... | collective-permute-start | bytes 196616 | tf_op jit(solution)/shard_map/ppermute | solution.py:22
  66.7 4.4 %collective-permute-start.30 = (bf16[128,256]{1,0:T(8,128)(2,1)S(1)}, bf16[128,256]{1,0:T(8,128)(2,1)S(1)}, u32[]{:S(2)}, u32[]{:S(2)}) collective-permute-start(bf16[128,256]{1,0:T(8,128)(2,1)S(1)} %collective-permute-done.28.refs_1_), channel_id=1, source_target_pairs={{0,2},{1,3},{2,0},{3,1},{4,6},{5,7},{6,4},{7,5},{8,10},{9,11},{10,... | collective-permute-start | bytes 196616 | tf_op jit(solution)/shard_map/ppermute | solution.py:22
  74.0 10.6 %collective-permute-start.31 = (f32[2,2,128,256]{3,2,1,0:T(8,128)S(1)}, f32[2,2,128,256]{3,2,1,0:T(8,128)S(1)}, u32[]{:S(2)}, u32[]{:S(2)}) collective-permute-start(f32[2,2,128,256]{3,2,1,0:T(8,128)S(1)} %split.35), channel_id=1, source_target_pairs={{0,1},{1,0},{2,3},{3,2},{4,5},{5,4},{6,7},{7,6},{8,9},{9,8},{10,11... | collective-permute-start | bytes 1572872 | tf_op jit(solution)/shard_map/ppermute | solution.py:22
  74.1 2.2 %collective-permute-start.26 = (f32[3,128,128]{2,1,0:T(8,128)S(1)}, f32[3,128,128]{2,1,0:T(8,128)S(1)}, u32[]{:S(2)}, u32[]{:S(2)}) collective-permute-start(f32[3,128,128]{2,1,0:T(8,128)S(1)} %get-tuple-element.12), channel_id=1, source_target_pairs={{0,1},{1,0},{2,3},{3,2},{4,5},{5,4},{6,7},{7,6},{8,9},{9,8},{10,11... | collective-permute-start | bytes 589832 | tf_op jit(solution)/shard_map/ppermute | solution.py:22
  76.3 7.0 %collective-permute-start.27 = (f32[3,128,128]{2,1,0:T(8,128)S(1)}, f32[3,128,128]{2,1,0:T(8,128)S(1)}, u32[]{:S(2)}, u32[]{:S(2)}) collective-permute-start(f32[3,128,128]{2,1,0:T(8,128)S(1)} %add.71.mine_ref), channel_id=1, source_target_pairs={{0,2},{1,3},{2,0},{3,1},{4,6},{5,7},{6,4},{7,5},{8,10},{9,11},{10,... | collective-permute-start | bytes 589832 | tf_op jit(solution)/shard_map/ppermute | solution.py:22
  84.8 5.0 %collective-permute-start.32 = (f16[1,2,128,256]{3,2,1,0:T(8,128)(2,1)S(1)}, f16[1,2,128,256]{3,2,1,0:T(8,128)(2,1)S(1)}, u32[]{:S(2)}, u32[]{:S(2)}) collective-permute-start(f16[1,2,128,256]{3,2,1,0:T(8,128)(2,1)S(1)} %fusion.2), channel_id=1, source_target_pairs={{0,2},{1,3},{2,0},{3,1},{4,6},{5,7},{6,4},{7,5},{8,10},{9,11},{10,... | collective-permute-start | bytes 393224 | tf_op jit(solution)/shard_map/ppermute | solution.py:22
  89.9 4.3 %collective-permute-start.33 = (f16[128,256]{1,0:T(8,128)(2,1)S(1)}, f16[128,256]{1,0:T(8,128)(2,1)S(1)}, u32[]{:S(2)}, u32[]{:S(2)}) collective-permute-start(f16[128,256]{1,0:T(8,128)(2,1)S(1)} %fusion.22), channel_id=1, source_target_pairs={{0,4},{4,0},{8,12},{12,8},{16,20},{20,16},{24,28},{28,24},{1,5},{5... | collective-permute-start | bytes 196616 | tf_op jit(solution)/shard_map/ppermute | solution.py:22
  94.2 5.0 %collective-permute-start.34 = (f16[128,256]{1,0:T(8,128)(2,1)S(1)}, f16[128,256]{1,0:T(8,128)(2,1)S(1)}, u32[]{:S(2)}, u32[]{:S(2)}) collective-permute-start(f16[128,256]{1,0:T(8,128)(2,1)S(1)} %fusion.6), channel_id=1, source_target_pairs={{0,8},{4,12},{8,0},{12,4},{16,24},{20,28},{24,16},{28,20},{1,9},{5... | collective-permute-start | bytes 196616 | tf_op jit(solution)/shard_map/ppermute | solution.py:22
  95.0 5.2 %collective-permute-start.35 = (f16[128,256]{1,0:T(8,128)(2,1)S(1)}, f16[128,256]{1,0:T(8,128)(2,1)S(1)}, u32[]{:S(2)}, u32[]{:S(2)}) collective-permute-start(f16[128,256]{1,0:T(8,128)(2,1)S(1)} %fusion.6), channel_id=1, source_target_pairs={{0,16},{4,20},{8,24},{12,28},{16,0},{20,4},{24,8},{28,12},{1,17},{... | collective-permute-start | bytes 196616 | tf_op jit(solution)/shard_map/ppermute | solution.py:22
  97.1 6.1 %collective-permute-start.36 = (f16[128,256]{1,0:T(8,128)(2,1)S(1)}, f16[128,256]{1,0:T(8,128)(2,1)S(1)}, u32[]{:S(2)}, u32[]{:S(2)}) collective-permute-start(f16[128,256]{1,0:T(8,128)(2,1)S(1)} %fusion.6), channel_id=1, source_target_pairs={{0,24},{4,28},{8,16},{12,20},{16,8},{20,12},{24,0},{28,4},{1,25},{... | collective-permute-start | bytes 196616 | tf_op jit(solution)/shard_map/ppermute | solution.py:22
  103.2 4.3 %collective-permute-start.37 = (f16[1,128,256]{2,1,0:T(8,128)(2,1)S(1)}, f16[1,128,256]{2,1,0:T(8,128)(2,1)S(1)}, u32[]{:S(2)}, u32[]{:S(2)}) collective-permute-start(f16[1,128,256]{2,1,0:T(8,128)(2,1)S(1)} %fusion.20), channel_id=1, source_target_pairs={{0,4},{4,0},{8,12},{12,8},{16,20},{20,16},{24,28},{28,24},{1,5},{5... | collective-permute-start | bytes 196616 | tf_op jit(solution)/shard_map/ppermute | solution.py:22
  107.6 5.0 %collective-permute-start.38 = (f16[1,2,128,256]{3,2,1,0:T(8,128)(2,1)S(1)}, f16[1,2,128,256]{3,2,1,0:T(8,128)(2,1)S(1)}, u32[]{:S(2)}, u32[]{:S(2)}) collective-permute-start(f16[1,2,128,256]{3,2,1,0:T(8,128)(2,1)S(1)} %maximum_bitcast_fusion), channel_id=1, source_target_pairs={{0,2},{1,3},{2,0},{3,1},{4,6},{5,7},{6,4},{7,5},{8,10},{9,11},{10,... | collective-permute-start | bytes 393224 | tf_op jit(solution)/shard_map/ppermute | solution.py:22
  112.7 3.1 %collective-permute-start.39 = (f16[2,2,128,256]{3,2,1,0:T(8,128)(2,1)S(1)}, f16[2,2,128,256]{3,2,1,0:T(8,128)(2,1)S(1)}, u32[]{:S(2)}, u32[]{:S(2)}) collective-permute-start(f16[2,2,128,256]{3,2,1,0:T(8,128)(2,1)S(1)} %get-tuple-element.18), channel_id=1, source_target_pairs={{0,1},{1,0},{2,3},{3,2},{4,5},{5,4},{6,7},{7,6},{8,9},{9,8},{10,11... | collective-permute-start | bytes 786440 | tf_op jit(solution)/shard_map/ppermute | solution.py:22
  (2 other events, 1.4 us)
where the time goes:
time: 119 us; the launch traced here: 118 us
  starting transfers between devices  45.2 us (38%)
  waiting for transfers between devices  34 us (29%)
  Pallas kernels  26.2 us (22%)
  local copies, waits for them, and re-layouts  5.49 us (5%)
  other arithmetic  3.75 us (3%)
  between operations  3.04 us (3%)
    ppermute x40, starting transfers between devices, swap(): return lax.ppermute(x, axis, [(i, i ^ mask) for i in range(size)])  45.2 us
    ppermute x40, waiting for transfers between devices, swap(): return lax.ppermute(x, axis, [(i, i ^ mask) for i in range(size)])  34 us
    pallas_call x1, Pallas kernels, system_inverse(): pl.pallas_call(system_kernel, out_shape=jax.ShapeDtypeStruct((rank, rank)...  9.31 us
    pallas_call x2, Pallas kernels, half_eliminate(): pl.pallas_call(kernel, out_shape=jax.ShapeDtypeStruct((rank, rank), jnp.f...  6.26 us
    unnamed x21, local copies, waits for them, and re-layouts  5.41 us
    pallas_call x1, Pallas kernels, first_pass(): pl.pallas_call(functools.partial(first_kernel, bits_c=bits_of('cols'), ha...  4.82 us
    pallas_call x1, Pallas kernels, second_pass(): pl.pallas_call(functools.partial(second_kernel, bits_c=bits_of('cols'), h...  2.82 us
  transfers between devices with their start and end apart: 40, of which 19 were waited for; matrix products, arithmetic and copies ran while one was open for 4% of the time, Pallas kernels for 14%

commit v1 on v0

--- a/solution.py
+++ b/solution.py
@@ -22,6 +22,27 @@
     return lax.ppermute(x, axis, [(i, i ^ mask) for i in range(size)])
 
 
+def swap_both(x, row_mask, col_mask):
+    if col_mask == 0:
+        return swap(x, "rows", row_mask)
+    if row_mask == 0:
+        return swap(x, "cols", col_mask)
+    n_cols = lax.axis_size("cols")
+    mask = row_mask * n_cols + col_mask
+    size = lax.axis_size("rows") * n_cols
+    return lax.ppermute(x, ("rows", "cols"), [(i, i ^ mask) for i in range(size)])
+
+
+def cost(microseconds):
+    return pl.CostEstimate(
+        flops=int(microseconds * 1.1e9), bytes_accessed=100_000, transcendentals=0
+    )
+
+
+def after(x, other):
+    return lax.optimization_barrier((x, other))[0]
+
+
 def bits_of(axis):
     return lax.axis_size(axis).bit_length() - 1
 
@@ -34,16 +55,20 @@
 
 
 def gather_cols(x):
-    pieces = [x]
     for b in range(bits_of("cols")):
-        pieces = pieces + [swap(p, "cols", 1 << b) for p in pieces]
-    return pieces
+        x = jnp.concatenate([x, swap(x, "cols", 1 << b)], axis=0)
+    return x
 
 
 def gather_rows(x):
     half = lax.axis_size("rows") // 2
-    even = [x] + [swap(x, "rows", 2 * i) for i in range(1, half)]
-    return even + [swap(p, "rows", 1) for p in even]
+    across = swap(x, "rows", 1)
+    even = [swap(x, "rows", 2 * i) for i in range(1, half)]
+    middle = half // 2
+    odd = [
+        swap(jnp.concatenate(part, axis=0), "rows", 1) for part in (even[:middle], even[middle:])
+    ]
+    return [x] + even + [across] + odd
 
 
 def tree_sum(parts):
@@ -74,9 +99,10 @@
 
 def gram_kernel(*refs):
     pieces, factors_ref, gram_ref = refs[:-2], refs[-2], refs[-1]
-    tile = pieces[0].shape[0]
-    for i, piece in enumerate(pieces):
-        factors_ref[i * tile:(i + 1) * tile, :] = piece[...]
+    begin = 0
+    for piece in pieces:
+        factors_ref[begin:begin + piece.shape[0], :] = piece[...]
+        begin += piece.shape[0]
     whole = factors_ref[...]
     gram = dot(whole, whole, ((0,), (0,)))
     side = gram_ref.shape[1]
@@ -86,45 +112,87 @@
 
 
 def gram_of(pieces):
-    tile, rank = pieces[0].shape
+    rank = pieces[0].shape[1]
+    height = sum(piece.shape[0] for piece in pieces)
     vmem = pl.BlockSpec(memory_space=pltpu.VMEM)
     factors, gram = pl.pallas_call(
         gram_kernel,
         out_shape=(
-            jax.ShapeDtypeStruct((len(pieces) * tile, rank), jnp.bfloat16),
+            jax.ShapeDtypeStruct((height, rank), jnp.bfloat16),
             jax.ShapeDtypeStruct((3, rank // 2, rank // 2), jnp.float32),
         ),
         in_specs=[vmem] * len(pieces),
         out_specs=(vmem, vmem),
         compiler_params=params(),
+        cost_estimate=cost(0.4),
         name="gram",
     )(*pieces)
     return factors, gram
 
 
-def first_kernel(rows_ref, cols_ref, counts_ref, tiles_ref, factors_ref, cores_ref, *refs,
-                 bits_c, half):
-    panel_refs = refs[:-5]
-    direct_ref, back_ref, acc_ref, turned_ref, sums_ref = refs[-5:]
+def prepare_kernel(rows_ref, cols_ref, counts_ref, tiles_ref, cores_ref, factor_ref,
+                   places_ref, scale_ref, live_ref, copied_ref, own_ref, *, half, terms):
+    relations, slots = tiles_ref.shape[0], tiles_ref.shape[1]
+    my_row = lax.axis_index("rows")
+    my_col = lax.axis_index("cols")
+    own_ref[...] = factor_ref[...]
+    reach = jnp.zeros((1, 1), jnp.float32)
+    for k in range(relations):
+        core = cores_ref[k]
+        copied_ref[k] = core
+        size = jnp.abs(core.astype(jnp.float32))
+        for axis in (0, 1):
+            sums = jnp.sum(size, axis=axis, keepdims=True)
+            reach = jnp.maximum(reach, jnp.max(sums, axis=1 - axis, keepdims=True))
+        for s in range(slots):
+            live = s < counts_ref[k, 0, 0]
+            values = tiles_ref[k, s]
+            live_ref[k, s] = jnp.where(live, values, jnp.zeros_like(values))
+            col = cols_ref[k, 0, s] ^ my_row
+            places_ref[k, s] = (col & 1) * half + (col >> 1)
+            places_ref[k, slots + s] = rows_ref[k, 0, s] ^ my_col
+    scale_ref[...] = jnp.broadcast_to(
+        f16_top / (terms * relations * slots * product_bound * reach + 1e-20), scale_ref.shape
+    )
+
+
+def prepare(rows, cols, counts, tiles, cores, factor):
+    n_rows, n_cols = lax.axis_size("rows"), lax.axis_size("cols")
+    smem = pl.BlockSpec(memory_space=pltpu.SMEM)
+    vmem = pl.BlockSpec(memory_space=pltpu.VMEM)
+    return pl.pallas_call(
+        functools.partial(prepare_kernel, half=n_rows // 2, terms=2.0 * n_cols),
+        out_shape=(
+            jax.ShapeDtypeStruct((tiles.shape[0], 2 * tiles.shape[1]), jnp.int32),
+            jax.ShapeDtypeStruct((8, 128), jnp.float32),
+            jax.ShapeDtypeStruct(tiles.shape, tiles.dtype),
+            jax.ShapeDtypeStruct(cores.shape, cores.dtype),
+            jax.ShapeDtypeStruct(factor.shape, factor.dtype),
+        ),
+        in_specs=[smem, smem, smem, vmem, vmem, vmem],
+        out_specs=(smem, vmem, vmem, vmem, vmem),
+        compiler_params=params(),
+        cost_estimate=cost(2.0),
+        name="prepare",
+    )(rows, cols, counts, tiles, cores, factor)
+
+
+def first_kernel(places_ref, tiles_ref, factors_ref, panel_ref, cores_ref,
+                 direct_ref, back_ref, acc_ref, turned_ref, sums_ref, *, bits_c):
     relations, slots = tiles_ref.shape[0], tiles_ref.shape[1]
     tile = tiles_ref.shape[2]
-    panels = len(panel_refs)
-    my_row = lax.axis_index("rows")
-    my_col = lax.axis_index("cols")
+    panels = panel_ref.shape[0] // tile
     sums_ref[...] = jnp.zeros_like(sums_ref)
     for k in range(relations):
         core = cores_ref[k]
         for i in range(panels):
-            rotated = dot(panel_refs[i][...], core).astype(jnp.bfloat16)
+            rotated = dot(panel_ref[i * tile:(i + 1) * tile, :], core).astype(jnp.bfloat16)
             turned_ref[i] = rotated.T
         acc_ref[...] = jnp.zeros_like(acc_ref)
         for s in range(slots):
-            live = s < counts_ref[k, 0, 0]
             values = tiles_ref[k, s]
-            values = jnp.where(live, values, jnp.zeros_like(values))
-            col = cols_ref[k, 0, s] ^ my_row
-            col = (col & 1) * half + (col >> 1)
-            row = rows_ref[k, 0, s] ^ my_col
+            col = places_ref[k, s]
+            row = places_ref[k, slots + s]
             acc_ref[row] += dot(values, factors_ref[col])
             sums_ref[col] += dot(turned_ref[row], values)
         for i in range(panels):
@@ -141,19 +209,19 @@
         back_ref[g] = sums_ref[g].T
 
 
-def first_pass(rows, cols, counts, tiles, factors, panel, cores):
-    relations, slots, tile, _ = tiles.shape
+def first_pass(places, tiles, factors, panel, cores):
+    tile = tiles.shape[2]
     rank = cores.shape[-1]
     n_rows, n_cols = lax.axis_size("rows"), lax.axis_size("cols")
     smem = pl.BlockSpec(memory_space=pltpu.SMEM)
     vmem = pl.BlockSpec(memory_space=pltpu.VMEM)
     return pl.pallas_call(
-        functools.partial(first_kernel, bits_c=bits_of("cols"), half=n_rows // 2),
+        functools.partial(first_kernel, bits_c=bits_of("cols")),
         out_shape=(
             jax.ShapeDtypeStruct((n_cols, tile, rank), jnp.float32),
             jax.ShapeDtypeStruct((n_rows, tile, rank), jnp.float32),
         ),
-        in_specs=[smem, smem, smem, vmem, vmem, vmem] + [vmem] * len(panel),
+        in_specs=[smem, vmem, vmem, vmem, vmem],
         out_specs=(vmem, vmem),
         scratch_shapes=[
             pltpu.VMEM((n_cols, tile, rank), jnp.float32),
@@ -161,30 +229,27 @@
             pltpu.VMEM((n_rows, rank, tile), jnp.float32),
         ],
         compiler_params=params(),
+        cost_estimate=cost(4.8),
         name="first_pass",
-    )(rows, cols, counts, tiles, factors.reshape(n_rows, tile, rank), cores, *panel)
-
-
-def second_kernel(rows_ref, cols_ref, counts_ref, tiles_ref, factors_ref, *refs, bits_c, half):
-    panel_refs = refs[:-4]
-    out_ref, turned_ref, upper_ref, picked_ref = refs[-4:]
+    )(places, tiles, factors.reshape(n_rows, tile, rank), panel, cores)
+
+
+def second_kernel(places_ref, tiles_ref, factors_ref, panel_ref,
+                  out_ref, turned_ref, upper_ref, picked_ref, *, bits_c):
     relations, slots = tiles_ref.shape[0], tiles_ref.shape[1]
     tile = tiles_ref.shape[2]
-    panels = len(panel_refs)
+    panels = panel_ref.shape[0] // tile
     pieces = out_ref.shape[0] // relations
     height = out_ref.shape[2]
     my_row = lax.axis_index("rows")
     my_col = lax.axis_index("cols")
     for i in range(panels):
-        turned_ref[i] = panel_refs[i][...].T
+        turned_ref[i] = panel_ref[i * tile:(i + 1) * tile, :].T
     for k in range(relations):
         for s in range(slots):
-            live = s < counts_ref[k, 0, 0]
             values = tiles_ref[k, s]
-            values = jnp.where(live, values, jnp.zeros_like(values))
-            col = cols_ref[k, 0, s] ^ my_row
-            col = (col & 1) * half + (col >> 1)
-            row = rows_ref[k, 0, s] ^ my_col
+            col = places_ref[k, s]
+            row = places_ref[k, slots + s]
             upper_ref[:, s * tile:(s + 1) * tile] = dot(turned_ref[row], values).astype(jnp.bfloat16)
             picked_ref[s * tile:(s + 1) * tile, :] = factors_ref[col]
         core = dot(upper_ref[...], picked_ref[...])
@@ -195,18 +260,18 @@
                 out_ref[place, h ^ (my_row & 1)] = core[begin:begin + height, :]
 
 
-def second_pass(rows, cols, counts, tiles, factors, panel):
+def second_pass(places, tiles, factors, panel):
     relations, slots, tile, _ = tiles.shape
-    rank = panel[0].shape[-1]
+    rank = panel.shape[-1]
     n_rows, n_cols = lax.axis_size("rows"), lax.axis_size("cols")
     smem = pl.BlockSpec(memory_space=pltpu.SMEM)
     vmem = pl.BlockSpec(memory_space=pltpu.VMEM)
     return pl.pallas_call(
-        functools.partial(second_kernel, bits_c=bits_of("cols"), half=n_rows // 2),
+        functools.partial(second_kernel, bits_c=bits_of("cols")),
         out_shape=jax.ShapeDtypeStruct(
             (n_cols, 2, relations * rank // n_cols // 2, rank), jnp.float32
         ),
-        in_specs=[smem, smem, smem, vmem, vmem] + [vmem] * len(panel),
+        in_specs=[smem, vmem, vmem, vmem],
         out_specs=vmem,
         scratch_shapes=[
             pltpu.VMEM((n_cols, rank, tile), jnp.bfloat16),
@@ -214,8 +279,9 @@
             pltpu.VMEM((slots * tile, rank), jnp.bfloat16),
         ],
         compiler_params=params(),
+        cost_estimate=cost(2.8),
         name="second_pass",
-    )(rows, cols, counts, tiles, factors.reshape(n_rows, tile, rank), *panel)
+    )(places, tiles, factors.reshape(n_rows, tile, rank), panel)
 
 
 def split(x, terms):
@@ -271,7 +337,7 @@
     return jnp.where(rows >= lanes, z, 0.0)
 
 
-def system_kernel(mine_ref, other_ref, cores_ref, out_ref, z_ref):
+def system_kernel(mine_ref, other_ref, cores_ref, z_ref):
     size = z_ref.shape[0]
     side = size // 2
     upper = mine_ref[1] + other_ref[1]
@@ -291,27 +357,17 @@
             middle = jnp.concatenate(split(middle, 3), axis=1)
             total = total + dot(middle, jnp.concatenate([right] * 3, axis=0))
     z_ref[...] = total
-    eliminate(z_ref, 0, size // 32, 32, 16)
-    lower = lower_of(z_ref[...])
-    high, mid, low = split(lower, 3)
+    eliminate(z_ref, 0, size // 128, 32, 16)
+
+
+def inverse_kernel(in_ref, out_ref, z_ref):
+    size = z_ref.shape[0]
+    z_ref[...] = in_ref[...]
+    eliminate(z_ref, size // 128, size // 32, 32, 16)
+    high, mid, low = split(lower_of(z_ref[...]), 3)
     left = jnp.concatenate([high, high, mid, mid, high, low], axis=0)
     right = jnp.concatenate([high, mid, high, mid, low, high], axis=0)
     out_ref[...] = dot(left, right, ((0,), (0,)))
-
-
-def system_inverse(mine, other, cores):
-    rank = cores.shape[-1]
-    vmem = pl.BlockSpec(memory_space=pltpu.VMEM)
-    return pl.pallas_call(
-        system_kernel,
-        out_shape=jax.ShapeDtypeStruct((rank, rank), jnp.float32),
-        in_specs=[vmem] * 3,
-        out_specs=vmem,
-        scratch_shapes=[pltpu.VMEM((rank, rank), jnp.float32)],
-        compiler_params=params(),
-        cost_estimate=pl.CostEstimate(flops=9_000_000_000, bytes_accessed=1_500_000, transcendentals=0),
-        name="system_inverse",
-    )(mine, other, cores)
 
 
 def begin_kernel(mine_ref, other_ref, out_ref):
@@ -330,15 +386,16 @@
     eliminate(out_ref, size // 64, size // 32, 32, 16)
 
 
-def half_eliminate(kernel, name, rank, *args):
+def square_call(kernel, name, microseconds, rank, *args, scratch=False):
     vmem = pl.BlockSpec(memory_space=pltpu.VMEM)
     return pl.pallas_call(
         kernel,
         out_shape=jax.ShapeDtypeStruct((rank, rank), jnp.float32),
         in_specs=[vmem] * len(args),
         out_specs=vmem,
+        scratch_shapes=[pltpu.VMEM((rank, rank), jnp.float32)] if scratch else [],
         compiler_params=params(),
-        cost_estimate=pl.CostEstimate(flops=3_500_000_000, bytes_accessed=500_000, transcendentals=0),
+        cost_estimate=cost(microseconds),
         name=name,
     )(*args)
 
@@ -377,6 +434,7 @@
         out_specs=vmem,
         scratch_shapes=[pltpu.VMEM((2 * near.shape[0],) + near.shape[1:], jnp.float32)],
         compiler_params=params(),
+        cost_estimate=cost(2.3),
         name="whiten",
     )(z, factor.reshape(1), near, far)
 
@@ -392,22 +450,24 @@
     rank = factor.shape[1]
     n_rows, n_cols = lax.axis_size("rows"), lax.axis_size("cols")
     half = n_rows // 2
-    magnitude = jnp.abs(cores.astype(jnp.float32))
-    reach = jnp.maximum(jnp.max(jnp.sum(magnitude, 1)), jnp.max(jnp.sum(magnitude, 2)))
-    scale = f16_top / (2.0 * n_cols * relations * slots * product_bound * reach + 1e-20)
-
-    factors, gram = gram_of(gather_rows(factor))
+    places, scale, tiles, cores, own = prepare(
+        tile_rows, tile_cols, tile_counts, tile_values, cores, factor
+    )
+    scale = scale[0, 0]
+
+    factors, gram = gram_of([own] + gather_rows(factor)[1:])
     panel = gather_cols(factor)
     gram_pair = pair_of_sums(gram)
-    direct, back = first_pass(tile_rows, tile_cols, tile_counts, tile_values, factors, panel, cores)
-    inverse = system_inverse(*gram_pair, cores)
+    direct, back = first_pass(places, tiles, after(factors, gram_pair[0]), panel, cores)
+    direct, back = after((direct, back), gram_pair)
+    system = square_call(system_kernel, "system", 5.5, rank, *gram_pair, cores)
     parts = []
     for begin in range(half, 0, -half // 2):
         begin = begin - half // 2
         end = begin + half // 2
         give = half_of(back[half + begin:half + end], scale)
         parts = [back[begin:end] + swap(give, "rows", 1).astype(jnp.float32) / scale] + parts
-    packed = [half_of(part, scale) for part in parts]
+    packed = [after(half_of(part, scale), system) for part in parts]
     received = [
         swap(packed[i // (half // 2)][i % (half // 2)], "rows", 2 * i).astype(jnp.float32)
         for i in range(1, half)
@@ -415,31 +475,40 @@
     numerator = (
         scatter_cols(direct, scale)[0] + parts[0][0] + functools.reduce(jnp.add, received) / scale
     )
+    inverse = square_call(inverse_kernel, "inverse", 4.0, rank, system, scratch=True)
     factor_new = dot(numerator, inverse, precision=lax.Precision.HIGHEST).astype(jnp.bfloat16)
 
     factors_new, gram_new = gram_of(gather_rows(factor_new))
     panel_new = gather_cols(factor_new)
     gram_pair = pair_of_sums(gram_new)
+    core = second_pass(places, tiles, factors_new, panel_new)
+    keep, give = jnp.split(after(core, gram_pair[0]), 2, axis=0)
+    core = keep + swap(give, "cols", 1)
+    z = square_call(begin_kernel, "begin", 3.3, rank, *gram_pair)
+    bits = bits_of("cols")
+    slots_left = [2 * reversed_slot(p, bits - 1) for p in range(n_cols // 2)]
+    plane = [(h, p) for p in range(n_cols // 2) for h in range(2) if (h, p) != (0, 0)]
+    core = core[0, 0] + functools.reduce(
+        jnp.add, [swap_both(core[p, h], h, slots_left[p]) for h, p in plane]
+    )
     longest = jnp.max(gram_pair[0] + gram_pair[1])
     tiles_in_all = n_rows * n_cols
     scale_core = f16_top / (2.0 * slots * tile * value_bound * tiles_in_all * longest + 1e-30)
-    core = second_pass(tile_rows, tile_cols, tile_counts, tile_values, factors_new, panel_new)
-    core = scatter_cols(core, scale_core)[0]
-    z = half_eliminate(begin_kernel, "begin", rank, *gram_pair)
-    core = core[0] + swap(half_of(core[1], scale_core), "rows", 1).astype(jnp.float32) / scale_core
-    packed = half_of(core, scale_core)
+    packed = after(half_of(core, scale_core), z)
     core = tree_sum(
         [packed.astype(jnp.float32)]
         + [swap(packed, "rows", 2 * i).astype(jnp.float32) for i in range(1, half)]
     )
-    z = half_eliminate(end_kernel, "end", rank, z)
-    core = core.astype(jnp.float16)[None]
-    core = jnp.concatenate([core, swap(core, "rows", 1)], axis=0)[None]
-    for b in reversed(range(1, bits_of("cols"))):
-        core = jnp.concatenate([core, swap(core, "cols", 1 << b)], axis=0)
-    far = swap(core, "cols", 1)
+    z = square_call(end_kernel, "end", 2.9, rank, z)
+    core = after(core.astype(jnp.float16), z)
+    found = {(h, p): swap_both(core, h, slots_left[p]) for h, p in plane}
+    found[(0, 0)] = core
+    near = jnp.stack(
+        [jnp.stack([found[(h, p)] for h in range(2)]) for p in range(n_cols // 2)]
+    )
+    far = swap(near, "cols", 1)
     cores_new = whiten(
-        z, 1.0 / scale_core, core.astype(jnp.float32), far.astype(jnp.float32), relations
+        z, 1.0 / scale_core, near.astype(jnp.float32), far.astype(jnp.float32), relations
     )
     return (factor_new, cores_new)
 

time: 119 us -> 107 us (0.90)
  waiting for transfers between devices: 34 us -> 24.3 us
  starting transfers between devices: 45.2 us -> 41 us
  Pallas kernels: 26.2 us -> 27.7 us
  between operations: 3.04 us -> 1.72 us
    ppermute x40 -> x36, waiting for transfers between devices: 34 us -> 21.7 us  [swap(): return lax.ppermute(x, axis, [(i, i ^ mask) for i in range(size)])]
    ppermute x40 -> x36, starting transfers between devices: 45.2 us -> 37.4 us  [swap(): return lax.ppermute(x, axis, [(i, i ^ mask) for i in range(size)])]
    ppermute x0 -> x2, starting transfers between devices: none -> 3.57 us  [swap_both(): lax.ppermute(x, ('rows', 'cols'), [(i, i ^ mask) for i in range(size)])]
    ppermute x0 -> x2, waiting for transfers between devices: none -> 2.64 us  [swap_both(): lax.ppermute(x, ('rows', 'cols'), [(i, i ^ mask) for i in range(size)])]
    convert_element_type x6 -> x5, other arithmetic: 0.2 us -> 2.8 us  [half_of(): return (x * scale).astype(jnp.float16)]
    pallas_call x7 -> x9, Pallas kernels: 24 us -> 25.4 us  [the longest x4 15.2 us: square_call(): pl.pallas_call(kernel, out_shape=jax.ShapeDtypeStruct((rank, rank), jnp.f...]
    reduce_sum x1 -> x0, other arithmetic: 1.27 us -> none  [local(): jnp.sum(magnitude, 2)]
    reduce_max x2 -> x0, other arithmetic: 1.2 us -> none  [the longest x1 0.6 us: local(): jnp.max(jnp.sum(magnitude, 1))]
  transfers between devices with their start and end apart: 40 -> 38, of which waited for: 19 -> 16; matrix products, arithmetic and copies ran while one was open for 4% -> 5% of each run, Pallas kernels for 14% -> 24%
where the time goes in v1:
time: 107 us; the launch traced here: 106 us
  starting transfers between devices  41 us (38%)
  Pallas kernels  27.7 us (26%)
  waiting for transfers between devices  24.3 us (23%)
  local copies, waits for them, and re-layouts  6.03 us (6%)
  other arithmetic  4.75 us (4%)
  between operations  1.72 us (2%)
    ppermute x36, starting transfers between devices, swap(): return lax.ppermute(x, axis, [(i, i ^ mask) for i in range(size)])  37.4 us
    ppermute x36, waiting for transfers between devices, swap(): return lax.ppermute(x, axis, [(i, i ^ mask) for i in range(size)])  21.7 us
    pallas_call x4, Pallas kernels, square_call(): pl.pallas_call(kernel, out_shape=jax.ShapeDtypeStruct((rank, rank), jnp.f...  15.2 us
    unnamed x13, local copies, waits for them, and re-layouts  5.4 us
    pallas_call x1, Pallas kernels, first_pass(): pl.pallas_call(functools.partial(first_kernel, bits_c=bits_of('cols')), o...  4.83 us
    ppermute x2, starting transfers between devices, swap_both(): lax.ppermute(x, ('rows', 'cols'), [(i, i ^ mask) for i in range(size)])  3.57 us
    convert_element_type x5, other arithmetic, half_of(): return (x * scale).astype(jnp.float16)  2.8 us
    pallas_call x1, Pallas kernels, second_pass(): pl.pallas_call(functools.partial(second_kernel, bits_c=bits_of('cols')),...  2.79 us
  transfers between devices with their start and end apart: 38, of which 16 were waited for; matrix products, arithmetic and copies ran while one was open for 5% of the time, Pallas kernels for 24%

profile of v1, /device:TPU:0, one launch (start us, length us, event | category | flops | bytes accessed | tf_op | source)
XLA Modules:
  0.0 106.4 jit_solution(7475786563966291062)
XLA Ops:
  0.6 3.1 %collective-permute-start = (bf16[128,256]{1,0:T(8,128)(2,1)}, bf16[128,256]{1,0:T(8,128)(2,1)S(1)}, u32[]{:S(2)}, u32[]{:S(2)}) collective-permute-start(bf16[128,256]{1,0:T(8,128)(2,1)} %factor_ref.1), channel_id=1, source_target_pairs={{0,8},{4,12},{8,0},{12,4},{16,24},{20,28},{24,16},{28,20},{1,9},{5... | collective-permute-start | bytes 196616 | tf_op jit(solution)/shard_map/ppermute | solution.py:22
  3.7 2.6 %collective-permute-start.1 = (bf16[128,256]{1,0:T(8,128)(2,1)}, bf16[128,256]{1,0:T(8,128)(2,1)S(1)}, u32[]{:S(2)}, u32[]{:S(2)}) collective-permute-start(bf16[128,256]{1,0:T(8,128)(2,1)} %factor_ref.1), channel_id=1, source_target_pairs={{0,16},{4,20},{8,24},{12,28},{16,0},{20,4},{24,8},{28,12},{1,17},{... | collective-permute-start | bytes 196616 | tf_op jit(solution)/shard_map/ppermute | solution.py:22
  6.3 1.7 %collective-permute-start.3 = (bf16[128,256]{1,0:T(8,128)(2,1)}, bf16[128,256]{1,0:T(8,128)(2,1)S(1)}, u32[]{:S(2)}, u32[]{:S(2)}) collective-permute-start(bf16[128,256]{1,0:T(8,128)(2,1)} %factor_ref.1), channel_id=1, source_target_pairs={{0,4},{4,0},{8,12},{12,8},{16,20},{20,16},{24,28},{28,24},{1,5},{5... | collective-permute-start | bytes 196616 | tf_op jit(solution)/shard_map/ppermute | solution.py:22
  8.1 0.7 copy.8.counts_ref
  8.8 2.4 %collective-permute-done.1.refs_2_ = bf16[128,256]{1,0:T(8,128)(2,1)S(1)} collective-permute-done((bf16[128,256]{1,0:T(8,128)(2,1)}, bf16[128,256]{1,0:T(8,128)(2,1)S(1)}, u32[]{:S(2)}, u32[]{:S(2)}) %collective-permute-start.1) | collective-permute-done | bytes 65568 | tf_op jit(solution)/shard_map/ppermute | solution.py:22
  11.2 1.6 %collective-permute-start.4 = (bf16[256,256]{1,0:T(8,128)(2,1)S(1)}, bf16[256,256]{1,0:T(8,128)(2,1)S(1)}, u32[]{:S(2)}, u32[]{:S(2)}) collective-permute-start(bf16[256,256]{1,0:T(8,128)(2,1)S(1)} %pad_maximum_fusion.3), channel_id=1, source_target_pairs={{0,4},{4,0},{8,12},{12,8},{16,20},{20,16},{24,28},{28,24},{1,5},{5... | collective-permute-start | bytes 393224 | tf_op jit(solution)/shard_map/ppermute | solution.py:22
  12.8 0.8 pad_maximum_fusion.4
  13.7 1.6 %collective-permute-start.8 = (bf16[256,256]{1,0:T(8,128)(2,1)S(1)}, bf16[256,256]{1,0:T(8,128)(2,1)S(1)}, u32[]{:S(2)}, u32[]{:S(2)}) collective-permute-start(bf16[256,256]{1,0:T(8,128)(2,1)S(1)} %pad_maximum_fusion.4), channel_id=1, source_target_pairs={{0,2},{1,3},{2,0},{3,1},{4,6},{5,7},{6,4},{7,5},{8,10},{9,11},{10,... | collective-permute-start | bytes 393224 | tf_op jit(solution)/shard_map/ppermute | solution.py:22
  15.7 0.8 copy-done
  16.6 1.4 %copy-done.2 = bf16[4,12,128,128]{3,2,1,0:T(8,128)(2,1)S(1)} copy-done((bf16[4,12,128,128]{3,2,1,0:T(8,128)(2,1)S(1)}, bf16[4,12,128,128]{3,2,1,0:T(8,128)(2,1)}, u32[]{:S(2)}) %copy-start.2) | copy-done | bytes 1572888
  18.0 1.0 copy-done.3
  20.4 1.8 %prepare.1 = (s32[4,24]{1,0:T(4,128)S(1)}, f32[8,128]{1,0:T(8,128)S(1)}, bf16[4,12,128,128]{3,2,1,0:T(8,128)(2,1)S(1)}, bf16[4,256,256]{2,1,0:T(8,128)(2,1)S(1)}, bf16[128,256]{1,0:T(8,128)(2,1)S(1)}) custom-call(s32[4,1,12]{2,1,0:T(1,128)S(1)} %copy-done.4, s32[4,1,12]{2,1,0:T(1,128)S(1)} %copy-done.5, s32[4,1,1]{2,1,0:T(1,128)S(1)} %copy.8.counts_ref, ...), custom_call_target="tpu_custom_call" | custom-call | flops 2200000000 | bytes 100000 | tf_op jit(solution)/shard_map/prepare/pallas_call | solution.py:163
  23.2 0.9 collective-permute-done.6
  24.8 4.8 %first_pass.1 = (f32[4,128,256]{2,1,0:T(8,128)S(1)}, f32[8,128,256]{2,1,0:T(8,128)S(1)}) custom-call(s32[4,24]{1,0:T(4,128)S(1)} %get-tuple-element.21.places_ref, bf16[4,12,128,128]{3,2,1,0:T(8,128)(2,1)S(1)} %get-tuple-element.22.tiles_ref, bf16[8,128,256]{2,1,0:T(8,128)(2,1)S(1)} %bitcast.38, bf16[512,256]{1,0:T(8,128)(2,1)S(1)} %pad_maximum_fusion.panel_ref, ...), custom_call_target="tpu_custom_call" | custom-call | flops 5280000000 | bytes 100000 | tf_op jit(solution)/shard_map/first_pass/pallas_call | solution.py:218
  29.6 1.6 %collective-permute-done.9.other_ref = f32[3,128,128]{2,1,0:T(8,128)S(1)} collective-permute-done((f32[3,128,128]{2,1,0:T(8,128)S(1)}, f32[3,128,128]{2,1,0:T(8,128)S(1)}, u32[]{:S(2)}, u32[]{:S(2)}) %collective-permute-start.9) | collective-permute-done | bytes 196640 | tf_op jit(solution)/shard_map/ppermute | solution.py:22
  32.0 1.6 %collective-permute-start.14 = (f16[2,128,256]{2,1,0:T(8,128)(2,1)S(1)}, f16[2,128,256]{2,1,0:T(8,128)(2,1)S(1)}, u32[]{:S(2)}, u32[]{:S(2)}) collective-permute-start(f16[2,128,256]{2,1,0:T(8,128)(2,1)S(1)} %multiply_convert_fusion.1), channel_id=1, source_target_pairs={{0,4},{4,0},{8,12},{12,8},{16,20},{20,16},{24,28},{28,24},{1,5},{5... | collective-permute-start | bytes 393224 | tf_op jit(solution)/shard_map/ppermute | solution.py:22
  33.5 3.8 %system.1.in_ref = f32[256,256]{1,0:T(8,128)S(1)} custom-call(f32[3,128,128]{2,1,0:T(8,128)S(1)} %add.60.mine_ref, f32[3,128,128]{2,1,0:T(8,128)S(1)} %collective-permute-done.9.other_ref, bf16[4,256,256]{2,1,0:T(8,128)(2,1)S(1)} %get-tuple-element.27.cores_ref), custom_call_target="tpu_custom_call" | custom-call | flops 6049999872 | bytes 100000 | tf_op jit(solution)/shard_map/system/pallas_call | solution.py:391
  37.9 0.7 multiply_convert_fusion
  38.7 1.6 %collective-permute-start.12 = (f16[2,128,256]{2,1,0:T(8,128)(2,1)S(1)}, f16[2,128,256]{2,1,0:T(8,128)(2,1)S(1)}, u32[]{:S(2)}, u32[]{:S(2)}) collective-permute-start(f16[2,128,256]{2,1,0:T(8,128)(2,1)S(1)} %get-tuple-element.43), channel_id=1, source_target_pairs={{0,4},{4,0},{8,12},{12,8},{16,20},{20,16},{24,28},{28,24},{1,5},{5... | collective-permute-start | bytes 393224 | tf_op jit(solution)/shard_map/ppermute | solution.py:22
  40.9 2.7 %collective-permute-start.16 = (f16[128,256]{1,0:T(8,128)(2,1)S(1)}, f16[128,256]{1,0:T(8,128)(2,1)S(1)}, u32[]{:S(2)}, u32[]{:S(2)}) collective-permute-start(f16[128,256]{1,0:T(8,128)(2,1)S(1)} %get-tuple-element.50), channel_id=1, source_target_pairs={{0,24},{4,28},{8,16},{12,20},{16,8},{20,12},{24,0},{28,4},{1,25},{... | collective-permute-start | bytes 196616 | tf_op jit(solution)/shard_map/ppermute | solution.py:22
  44.9 0.7 multiply_convert_fusion.2
  46.2 5.2 %inverse.1 = f32[256,256]{1,0:T(8,128)S(1)} custom-call(f32[256,256]{1,0:T(8,128)S(1)} %system.1.in_ref), custom_call_target="tpu_custom_call" | custom-call | flops 4400000000 | bytes 100000 | tf_op jit(solution)/shard_map/inverse/pallas_call | solution.py:391
  51.4 1.0 convolution_convert_fusion.refs_0_
  52.4 1.6 %collective-permute-start.17 = (bf16[128,256]{1,0:T(8,128)(2,1)S(1)}, bf16[128,256]{1,0:T(8,128)(2,1)S(1)}, u32[]{:S(2)}, u32[]{:S(2)}) collective-permute-start(bf16[128,256]{1,0:T(8,128)(2,1)S(1)} %convolution_convert_fusion.refs_0_), channel_id=1, source_target_pairs={{0,8},{4,12},{8,0},{12,4},{16,24},{20,28},{24,16},{28,20},{1,9},{5... | collective-permute-start | bytes 196616 | tf_op jit(solution)/shard_map/ppermute | solution.py:22
  54.0 1.9 %collective-permute-start.18 = (bf16[128,256]{1,0:T(8,128)(2,1)S(1)}, bf16[128,256]{1,0:T(8,128)(2,1)S(1)}, u32[]{:S(2)}, u32[]{:S(2)}) collective-permute-start(bf16[128,256]{1,0:T(8,128)(2,1)S(1)} %convolution_convert_fusion.refs_0_), channel_id=1, source_target_pairs={{0,16},{4,20},{8,24},{12,28},{16,0},{20,4},{24,8},{28,12},{1,17},{... | collective-permute-start | bytes 196616 | tf_op jit(solution)/shard_map/ppermute | solution.py:22
  55.9 0.9 collective-permute-start.19
  56.8 3.5 %collective-permute-done.18.refs_2_ = bf16[128,256]{1,0:T(8,128)(2,1)S(1)} collective-permute-done((bf16[128,256]{1,0:T(8,128)(2,1)S(1)}, bf16[128,256]{1,0:T(8,128)(2,1)S(1)}, u32[]{:S(2)}, u32[]{:S(2)}) %collective-permute-start.18) | collective-permute-done | bytes 65568 | tf_op jit(solution)/shard_map/ppermute | solution.py:22
  60.4 2.0 %collective-permute-start.26 = (bf16[256,256]{1,0:T(8,128)(2,1)S(1)}, bf16[256,256]{1,0:T(8,128)(2,1)S(1)}, u32[]{:S(2)}, u32[]{:S(2)}) collective-permute-start(bf16[256,256]{1,0:T(8,128)(2,1)S(1)} %pad_maximum_fusion.6), channel_id=1, source_target_pairs={{0,2},{1,3},{2,0},{3,1},{4,6},{5,7},{6,4},{7,5},{8,10},{9,11},{10,... | collective-permute-start | bytes 393224 | tf_op jit(solution)/shard_map/ppermute | solution.py:22
  62.5 1.7 %collective-permute-start.20 = (bf16[128,256]{1,0:T(8,128)(2,1)S(1)}, bf16[128,256]{1,0:T(8,128)(2,1)S(1)}, u32[]{:S(2)}, u32[]{:S(2)}) collective-permute-start(bf16[128,256]{1,0:T(8,128)(2,1)S(1)} %convolution_convert_fusion.refs_0_), channel_id=1, source_target_pairs={{0,4},{4,0},{8,12},{12,8},{16,20},{20,16},{24,28},{28,24},{1,5},{5... | collective-permute-start | bytes 196616 | tf_op jit(solution)/shard_map/ppermute | solution.py:22
  64.5 2.3 %collective-permute-done.20.refs_4_ = bf16[128,256]{1,0:T(8,128)(2,1)S(1)} collective-permute-done((bf16[128,256]{1,0:T(8,128)(2,1)S(1)}, bf16[128,256]{1,0:T(8,128)(2,1)S(1)}, u32[]{:S(2)}, u32[]{:S(2)}) %collective-permute-start.20) | collective-permute-done | bytes 65568 | tf_op jit(solution)/shard_map/ppermute | solution.py:22
  66.8 1.6 %collective-permute-done.22.refs_6_ = bf16[128,256]{1,0:T(8,128)(2,1)S(1)} collective-permute-done((bf16[128,256]{1,0:T(8,128)(2,1)S(1)}, bf16[128,256]{1,0:T(8,128)(2,1)S(1)}, u32[]{:S(2)}, u32[]{:S(2)}) %collective-permute-start.22) | collective-permute-done | bytes 65568 | tf_op jit(solution)/shard_map/ppermute | solution.py:22
  68.9 2.8 %second_pass.1 = f32[4,2,128,256]{3,2,1,0:T(8,128)S(1)} custom-call(s32[4,24]{1,0:T(4,128)S(1)} %get-tuple-element.21.places_ref, bf16[4,12,128,128]{3,2,1,0:T(8,128)(2,1)S(1)} %get-tuple-element.22.tiles_ref, bf16[8,128,256]{2,1,0:T(8,128)(2,1)S(1)} %bitcast.39, bf16[512,256]{1,0:T(8,128)(2,1)S(1)} %pad_maximum_fusion.1.panel_ref), custom_call_target="tpu_custom_call" | custom-call | flops 3080000000 | bytes 100000 | tf_op jit(solution)/shard_map/second_pass/pallas_call | solution.py:269
  72.3 0.7 collective-permute-start.24
  73.0 0.8 collective-permute-done.27
  74.0 0.8 collective-permute-start.28
  75.2 2.3 %collective-permute-start.30 = (f32[128,256]{1,0:T(8,128)S(1)}, f32[128,256]{1,0:T(8,128)S(1)}, u32[]{:S(2)}, u32[]{:S(2)}) collective-permute-start(f32[128,256]{1,0:T(8,128)S(1)} %get-tuple-element.45), channel_id=1, source_target_pairs={{0,6},{1,7},{2,4},{3,5},{4,2},{5,3},{6,0},{7,1},{8,14},{9,15},{10,... | collective-permute-start | bytes 393224 | tf_op jit(solution)/shard_map/ppermute | solution.py:33
  77.6 2.5 %collective-permute-done.24.other_ref = f32[3,128,128]{2,1,0:T(8,128)S(1)} collective-permute-done((f32[3,128,128]{2,1,0:T(8,128)S(1)}, f32[3,128,128]{2,1,0:T(8,128)S(1)}, u32[]{:S(2)}, u32[]{:S(2)}) %collective-permute-start.24) | collective-permute-done | bytes 196640 | tf_op jit(solution)/shard_map/ppermute | solution.py:22
  80.1 3.3 %begin.1.in_ref = f32[256,256]{1,0:T(8,128)S(1)} custom-call(f32[3,128,128]{2,1,0:T(8,128)S(1)} %add.70.mine_ref, f32[3,128,128]{2,1,0:T(8,128)S(1)} %collective-permute-done.24.other_ref), custom_call_target="tpu_custom_call" | custom-call | flops 3630000128 | bytes 100000 | tf_op jit(solution)/shard_map/begin/pallas_call | solution.py:391
  85.6 3.2 %collective-permute-start.32 = (f16[128,256]{1,0:T(8,128)(2,1)S(1)}, f16[128,256]{1,0:T(8,128)(2,1)S(1)}, u32[]{:S(2)}, u32[]{:S(2)}) collective-permute-start(f16[128,256]{1,0:T(8,128)(2,1)S(1)} %fusion.2), channel_id=1, source_target_pairs={{0,16},{4,20},{8,24},{12,28},{16,0},{20,4},{24,8},{28,12},{1,17},{... | collective-permute-start | bytes 196616 | tf_op jit(solution)/shard_map/ppermute | solution.py:22
  89.5 3.0 %end.1.z_ref = f32[256,256]{1,0:T(8,128)S(1)} custom-call(f32[256,256]{1,0:T(8,128)S(1)} %begin.1.in_ref), custom_call_target="tpu_custom_call" | custom-call | flops 3190000128 | bytes 100000 | tf_op jit(solution)/shard_map/end/pallas_call | solution.py:391
  92.8 2.0 %collective-permute-done.33 = f16[128,256]{1,0:T(8,128)(2,1)S(1)} collective-permute-done((f16[128,256]{1,0:T(8,128)(2,1)S(1)}, f16[128,256]{1,0:T(8,128)(2,1)S(1)}, u32[]{:S(2)}, u32[]{:S(2)}) %collective-permute-start.33) | collective-permute-done | bytes 65568 | tf_op jit(solution)/shard_map/ppermute | solution.py:22
  94.9 0.8 collective-permute-start.34
  95.7 1.5 %collective-permute-start.35 = (f16[128,256]{1,0:T(8,128)(2,1)S(1)}, f16[128,256]{1,0:T(8,128)(2,1)S(1)}, u32[]{:S(2)}, u32[]{:S(2)}) collective-permute-start(f16[128,256]{1,0:T(8,128)(2,1)S(1)} %add_convert_fusion), channel_id=1, source_target_pairs={{0,2},{1,3},{2,0},{3,1},{4,6},{5,7},{6,4},{7,5},{8,10},{9,11},{10,... | collective-permute-start | bytes 196616 | tf_op jit(solution)/shard_map/ppermute | solution.py:22
  97.2 1.3 %collective-permute-start.36 = (f16[128,256]{1,0:T(8,128)(2,1)S(1)}, f16[128,256]{1,0:T(8,128)(2,1)S(1)}, u32[]{:S(2)}, u32[]{:S(2)}) collective-permute-start(f16[128,256]{1,0:T(8,128)(2,1)S(1)} %add_convert_fusion), channel_id=1, source_target_pairs={{0,6},{1,7},{2,4},{3,5},{4,2},{5,3},{6,0},{7,1},{8,14},{9,15},{10,... | collective-permute-start | bytes 196616 | tf_op jit(solution)/shard_map/ppermute | solution.py:33
  98.5 0.8 collective-permute-done.34
  99.9 2.4 %collective-permute-done.36 = f16[128,256]{1,0:T(8,128)(2,1)S(1)} collective-permute-done((f16[128,256]{1,0:T(8,128)(2,1)S(1)}, f16[128,256]{1,0:T(8,128)(2,1)S(1)}, u32[]{:S(2)}, u32[]{:S(2)}) %collective-permute-start.36) | collective-permute-done | bytes 65568 | tf_op jit(solution)/shard_map/ppermute | solution.py:33
  102.6 1.5 %collective-permute-done.37 = f16[2,2,128,256]{3,2,1,0:T(8,128)(2,1)S(1)} collective-permute-done((f16[2,2,128,256]{3,2,1,0:T(8,128)(2,1)S(1)}, f16[2,2,128,256]{3,2,1,0:T(8,128)(2,1)S(1)}, u32[]{:S(2)}, u32[]{:S(2)}) %collective-permute-start.37) | collective-permute-done | bytes 262176 | tf_op jit(solution)/shard_map/ppermute | solution.py:22
  104.1 2.3 %whiten.1 = f32[4,256,256]{2,1,0:T(8,128)} custom-call(f32[256,256]{1,0:T(8,128)S(1)} %end.1.z_ref, f32[1]{0:T(128)} %bitcast.6.factor_ref, f32[2,2,128,256]{3,2,1,0:T(8,128)S(1)} %get-tuple-element.48.near_ref, f32[2,2,128,256]{3,2,1,0:T(8,128)S(1)} %convert_element_type.79.far_ref), custom_call_target="tpu_custom_call" | custom-call | flops 2529999872 | bytes 100000 | tf_op jit(solution)/shard_map/whiten/pallas_call | solution.py:430
  (79 shorter events, 13.0 us)
Async XLA Ops:
  0.6 8.2 %collective-permute-start = (bf16[128,256]{1,0:T(8,128)(2,1)}, bf16[128,256]{1,0:T(8,128)(2,1)S(1)}, u32[]{:S(2)}, u32[]{:S(2)}) collective-permute-start(bf16[128,256]{1,0:T(8,128)(2,1)} %factor_ref.1), channel_id=1, source_target_pairs={{0,8},{4,12},{8,0},{12,4},{16,24},{20,28},{24,16},{28,20},{1,9},{5... | collective-permute-start | bytes 196616 | tf_op jit(solution)/shard_map/ppermute | solution.py:22
  3.7 7.5 %collective-permute-start.1 = (bf16[128,256]{1,0:T(8,128)(2,1)}, bf16[128,256]{1,0:T(8,128)(2,1)S(1)}, u32[]{:S(2)}, u32[]{:S(2)}) collective-permute-start(bf16[128,256]{1,0:T(8,128)(2,1)} %factor_ref.1), channel_id=1, source_target_pairs={{0,16},{4,20},{8,24},{12,28},{16,0},{20,4},{24,8},{28,12},{1,17},{... | collective-permute-start | bytes 196616 | tf_op jit(solution)/shard_map/ppermute | solution.py:22
  6.3 8.9 %collective-permute-start.2 = (bf16[128,256]{1,0:T(8,128)(2,1)}, bf16[128,256]{1,0:T(8,128)(2,1)S(1)}, u32[]{:S(2)}, u32[]{:S(2)}) collective-permute-start(bf16[128,256]{1,0:T(8,128)(2,1)} %factor_ref.1), channel_id=1, source_target_pairs={{0,24},{4,28},{8,16},{12,20},{16,8},{20,12},{24,0},{28,4},{1,25},{... | collective-permute-start | bytes 196616 | tf_op jit(solution)/shard_map/ppermute | solution.py:22
  6.3 15.9 %collective-permute-start.3 = (bf16[128,256]{1,0:T(8,128)(2,1)}, bf16[128,256]{1,0:T(8,128)(2,1)S(1)}, u32[]{:S(2)}, u32[]{:S(2)}) collective-permute-start(bf16[128,256]{1,0:T(8,128)(2,1)} %factor_ref.1), channel_id=1, source_target_pairs={{0,4},{4,0},{8,12},{12,8},{16,20},{20,16},{24,28},{28,24},{1,5},{5... | collective-permute-start | bytes 196616 | tf_op jit(solution)/shard_map/ppermute | solution.py:22
  8.1 4.8 %collective-permute-start.7 = (bf16[128,256]{1,0:T(8,128)(2,1)}, bf16[128,256]{1,0:T(8,128)(2,1)S(1)}, u32[]{:S(2)}, u32[]{:S(2)}) collective-permute-start(bf16[128,256]{1,0:T(8,128)(2,1)} %factor_ref.1), channel_id=1, source_target_pairs={{0,1},{1,0},{2,3},{3,2},{4,5},{5,4},{6,7},{7,6},{8,9},{9,8},{10,11... | collective-permute-start | bytes 196616 | tf_op jit(solution)/shard_map/ppermute | solution.py:22
  11.2 11.0 %collective-permute-start.4 = (bf16[256,256]{1,0:T(8,128)(2,1)S(1)}, bf16[256,256]{1,0:T(8,128)(2,1)S(1)}, u32[]{:S(2)}, u32[]{:S(2)}) collective-permute-start(bf16[256,256]{1,0:T(8,128)(2,1)S(1)} %pad_maximum_fusion.3), channel_id=1, source_target_pairs={{0,4},{4,0},{8,12},{12,8},{16,20},{20,16},{24,28},{28,24},{1,5},{5... | collective-permute-start | bytes 393224 | tf_op jit(solution)/shard_map/ppermute | solution.py:22
  13.7 9.6 %collective-permute-start.8 = (bf16[256,256]{1,0:T(8,128)(2,1)S(1)}, bf16[256,256]{1,0:T(8,128)(2,1)S(1)}, u32[]{:S(2)}, u32[]{:S(2)}) collective-permute-start(bf16[256,256]{1,0:T(8,128)(2,1)S(1)} %pad_maximum_fusion.4), channel_id=1, source_target_pairs={{0,2},{1,3},{2,0},{3,1},{4,6},{5,7},{6,4},{7,5},{8,10},{9,11},{10,... | collective-permute-start | bytes 393224 | tf_op jit(solution)/shard_map/ppermute | solution.py:22
  15.2 7.0 %collective-permute-start.5 = (bf16[128,256]{1,0:T(8,128)(2,1)S(1)}, bf16[128,256]{1,0:T(8,128)(2,1)S(1)}, u32[]{:S(2)}, u32[]{:S(2)}) collective-permute-start(bf16[128,256]{1,0:T(8,128)(2,1)S(1)} %collective-permute-done.2.refs_3_), channel_id=1, source_target_pairs={{0,4},{4,0},{8,12},{12,8},{16,20},{20,16},{24,28},{28,24},{1,5},{5... | collective-permute-start | bytes 196616 | tf_op jit(solution)/shard_map/ppermute | solution.py:22
  15.7 0.8 copy-start
  16.6 1.4 %copy-start.2 = (bf16[4,12,128,128]{3,2,1,0:T(8,128)(2,1)S(1)}, bf16[4,12,128,128]{3,2,1,0:T(8,128)(2,1)}, u32[]{:S(2)}) copy-start(bf16[4,12,128,128]{3,2,1,0:T(8,128)(2,1)} %tiles_ref.1) | copy-start | bytes 4718596
  18.0 1.0 copy-start.3
  19.0 0.7 copy-start.4
  19.7 0.7 copy-start.5
  22.6 1.5 %collective-permute-start.6 = (f32[3,128,128]{2,1,0:T(8,128)S(1)}, f32[3,128,128]{2,1,0:T(8,128)S(1)}, u32[]{:S(2)}, u32[]{:S(2)}) collective-permute-start(f32[3,128,128]{2,1,0:T(8,128)S(1)} %get-tuple-element.25), channel_id=1, source_target_pairs={{0,1},{1,0},{2,3},{3,2},{4,5},{5,4},{6,7},{7,6},{8,9},{9,8},{10,11... | collective-permute-start | bytes 589832 | tf_op jit(solution)/shard_map/ppermute | solution.py:22
  24.2 7.0 %collective-permute-start.9 = (f32[3,128,128]{2,1,0:T(8,128)S(1)}, f32[3,128,128]{2,1,0:T(8,128)S(1)}, u32[]{:S(2)}, u32[]{:S(2)}) collective-permute-start(f32[3,128,128]{2,1,0:T(8,128)S(1)} %add.60.mine_ref), channel_id=1, source_target_pairs={{0,2},{1,3},{2,0},{3,1},{4,6},{5,7},{6,4},{7,5},{8,10},{9,11},{10,... | collective-permute-start | bytes 589832 | tf_op jit(solution)/shard_map/ppermute | solution.py:22
  31.2 12.4 %collective-permute-start.10 = (f32[2,128,256]{2,1,0:T(8,128)S(1)}, f32[2,128,256]{2,1,0:T(8,128)S(1)}, u32[]{:S(2)}, u32[]{:S(2)}) collective-permute-start(f32[2,128,256]{2,1,0:T(8,128)S(1)} %split.19), channel_id=1, source_target_pairs={{0,1},{1,0},{2,3},{3,2},{4,5},{5,4},{6,7},{7,6},{8,9},{9,8},{10,11... | collective-permute-start | bytes 786440 | tf_op jit(solution)/shard_map/ppermute | solution.py:22
  32.0 6.0 %collective-permute-start.14 = (f16[2,128,256]{2,1,0:T(8,128)(2,1)S(1)}, f16[2,128,256]{2,1,0:T(8,128)(2,1)S(1)}, u32[]{:S(2)}, u32[]{:S(2)}) collective-permute-start(f16[2,128,256]{2,1,0:T(8,128)(2,1)S(1)} %multiply_convert_fusion.1), channel_id=1, source_target_pairs={{0,4},{4,0},{8,12},{12,8},{16,20},{20,16},{24,28},{28,24},{1,5},{5... | collective-permute-start | bytes 393224 | tf_op jit(solution)/shard_map/ppermute | solution.py:22
  38.7 6.2 %collective-permute-start.12 = (f16[2,128,256]{2,1,0:T(8,128)(2,1)S(1)}, f16[2,128,256]{2,1,0:T(8,128)(2,1)S(1)}, u32[]{:S(2)}, u32[]{:S(2)}) collective-permute-start(f16[2,128,256]{2,1,0:T(8,128)(2,1)S(1)} %get-tuple-element.43), channel_id=1, source_target_pairs={{0,4},{4,0},{8,12},{12,8},{16,20},{20,16},{24,28},{28,24},{1,5},{5... | collective-permute-start | bytes 393224 | tf_op jit(solution)/shard_map/ppermute | solution.py:22
  40.3 11.1 %collective-permute-start.15 = (f16[128,256]{1,0:T(8,128)(2,1)S(1)}, f16[128,256]{1,0:T(8,128)(2,1)S(1)}, u32[]{:S(2)}, u32[]{:S(2)}) collective-permute-start(f16[128,256]{1,0:T(8,128)(2,1)S(1)} %get-tuple-element.49), channel_id=1, source_target_pairs={{0,16},{4,20},{8,24},{12,28},{16,0},{20,4},{24,8},{28,12},{1,17},{... | collective-permute-start | bytes 196616 | tf_op jit(solution)/shard_map/ppermute | solution.py:22
  40.9 10.4 %collective-permute-start.16 = (f16[128,256]{1,0:T(8,128)(2,1)S(1)}, f16[128,256]{1,0:T(8,128)(2,1)S(1)}, u32[]{:S(2)}, u32[]{:S(2)}) collective-permute-start(f16[128,256]{1,0:T(8,128)(2,1)S(1)} %get-tuple-element.50), channel_id=1, source_target_pairs={{0,24},{4,28},{8,16},{12,20},{16,8},{20,12},{24,0},{28,4},{1,25},{... | collective-permute-start | bytes 196616 | tf_op jit(solution)/shard_map/ppermute | solution.py:22
  44.3 7.1 %collective-permute-start.11 = (f16[1,128,256]{2,1,0:T(8,128)(2,1)S(1)}, f16[1,128,256]{2,1,0:T(8,128)(2,1)S(1)}, u32[]{:S(2)}, u32[]{:S(2)}) collective-permute-start(f16[1,128,256]{2,1,0:T(8,128)(2,1)S(1)} %fusion.6), channel_id=1, source_target_pairs={{0,2},{1,3},{2,0},{3,1},{4,6},{5,7},{6,4},{7,5},{8,10},{9,11},{10,... | collective-permute-start | bytes 196616 | tf_op jit(solution)/shard_map/ppermute | solution.py:22
  45.6 5.7 %collective-permute-start.13 = (f16[128,256]{1,0:T(8,128)(2,1)S(1)}, f16[128,256]{1,0:T(8,128)(2,1)S(1)}, u32[]{:S(2)}, u32[]{:S(2)}) collective-permute-start(f16[128,256]{1,0:T(8,128)(2,1)S(1)} %slice_bitcast_fusion.6), channel_id=1, source_target_pairs={{0,8},{4,12},{8,0},{12,4},{16,24},{20,28},{24,16},{28,20},{1,9},{5... | collective-permute-start | bytes 196616 | tf_op jit(solution)/shard_map/ppermute | solution.py:22
  52.3 19.4 %copy-start.1 = (bf16[128,256]{1,0:T(8,128)(2,1)}, bf16[128,256]{1,0:T(8,128)(2,1)S(1)}, u32[]{:S(2)}) copy-start(bf16[128,256]{1,0:T(8,128)(2,1)S(1)} %convolution_convert_fusion.refs_0_) | copy-start | bytes 196612
  52.4 4.5 %collective-permute-start.17 = (bf16[128,256]{1,0:T(8,128)(2,1)S(1)}, bf16[128,256]{1,0:T(8,128)(2,1)S(1)}, u32[]{:S(2)}, u32[]{:S(2)}) collective-permute-start(bf16[128,256]{1,0:T(8,128)(2,1)S(1)} %convolution_convert_fusion.refs_0_), channel_id=1, source_target_pairs={{0,8},{4,12},{8,0},{12,4},{16,24},{20,28},{24,16},{28,20},{1,9},{5... | collective-permute-start | bytes 196616 | tf_op jit(solution)/shard_map/ppermute | solution.py:22
  54.0 6.4 %collective-permute-start.18 = (bf16[128,256]{1,0:T(8,128)(2,1)S(1)}, bf16[128,256]{1,0:T(8,128)(2,1)S(1)}, u32[]{:S(2)}, u32[]{:S(2)}) collective-permute-start(bf16[128,256]{1,0:T(8,128)(2,1)S(1)} %convolution_convert_fusion.refs_0_), channel_id=1, source_target_pairs={{0,16},{4,20},{8,24},{12,28},{16,0},{20,4},{24,8},{28,12},{1,17},{... | collective-permute-start | bytes 196616 | tf_op jit(solution)/shard_map/ppermute | solution.py:22
  55.9 4.5 %collective-permute-start.25 = (bf16[128,256]{1,0:T(8,128)(2,1)S(1)}, bf16[128,256]{1,0:T(8,128)(2,1)S(1)}, u32[]{:S(2)}, u32[]{:S(2)}) collective-permute-start(bf16[128,256]{1,0:T(8,128)(2,1)S(1)} %convolution_convert_fusion.refs_0_), channel_id=1, source_target_pairs={{0,1},{1,0},{2,3},{3,2},{4,5},{5,4},{6,7},{7,6},{8,9},{9,8},{10,11... | collective-permute-start | bytes 196616 | tf_op jit(solution)/shard_map/ppermute | solution.py:22
  55.9 8.2 %collective-permute-start.19 = (bf16[128,256]{1,0:T(8,128)(2,1)S(1)}, bf16[128,256]{1,0:T(8,128)(2,1)S(1)}, u32[]{:S(2)}, u32[]{:S(2)}) collective-permute-start(bf16[128,256]{1,0:T(8,128)(2,1)S(1)} %convolution_convert_fusion.refs_0_), channel_id=1, source_target_pairs={{0,24},{4,28},{8,16},{12,20},{16,8},{20,12},{24,0},{28,4},{1,25},{... | collective-permute-start | bytes 196616 | tf_op jit(solution)/shard_map/ppermute | solution.py:22
  60.3 8.1 %collective-permute-start.21 = (bf16[256,256]{1,0:T(8,128)(2,1)S(1)}, bf16[256,256]{1,0:T(8,128)(2,1)S(1)}, u32[]{:S(2)}, u32[]{:S(2)}) collective-permute-start(bf16[256,256]{1,0:T(8,128)(2,1)S(1)} %pad_maximum_fusion.5), channel_id=1, source_target_pairs={{0,4},{4,0},{8,12},{12,8},{16,20},{20,16},{24,28},{28,24},{1,5},{5... | collective-permute-start | bytes 393224 | tf_op jit(solution)/shard_map/ppermute | solution.py:22
  60.4 8.4 %collective-permute-start.26 = (bf16[256,256]{1,0:T(8,128)(2,1)S(1)}, bf16[256,256]{1,0:T(8,128)(2,1)S(1)}, u32[]{:S(2)}, u32[]{:S(2)}) collective-permute-start(bf16[256,256]{1,0:T(8,128)(2,1)S(1)} %pad_maximum_fusion.6), channel_id=1, source_target_pairs={{0,2},{1,3},{2,0},{3,1},{4,6},{5,7},{6,4},{7,5},{8,10},{9,11},{10,... | collective-permute-start | bytes 393224 | tf_op jit(solution)/shard_map/ppermute | solution.py:22
  62.5 4.3 %collective-permute-start.20 = (bf16[128,256]{1,0:T(8,128)(2,1)S(1)}, bf16[128,256]{1,0:T(8,128)(2,1)S(1)}, u32[]{:S(2)}, u32[]{:S(2)}) collective-permute-start(bf16[128,256]{1,0:T(8,128)(2,1)S(1)} %convolution_convert_fusion.refs_0_), channel_id=1, source_target_pairs={{0,4},{4,0},{8,12},{12,8},{16,20},{20,16},{24,28},{28,24},{1,5},{5... | collective-permute-start | bytes 196616 | tf_op jit(solution)/shard_map/ppermute | solution.py:22
  64.1 4.3 %collective-permute-start.22 = (bf16[128,256]{1,0:T(8,128)(2,1)S(1)}, bf16[128,256]{1,0:T(8,128)(2,1)S(1)}, u32[]{:S(2)}, u32[]{:S(2)}) collective-permute-start(bf16[128,256]{1,0:T(8,128)(2,1)S(1)} %collective-permute-done.19.refs_3_), channel_id=1, source_target_pairs={{0,4},{4,0},{8,12},{12,8},{16,20},{20,16},{24,28},{28,24},{1,5},{5... | collective-permute-start | bytes 196616 | tf_op jit(solution)/shard_map/ppermute | solution.py:22
  68.8 2.9 %collective-permute-start.23 = (f32[3,128,128]{2,1,0:T(8,128)S(1)}, f32[3,128,128]{2,1,0:T(8,128)S(1)}, u32[]{:S(2)}, u32[]{:S(2)}) collective-permute-start(f32[3,128,128]{2,1,0:T(8,128)S(1)} %get-tuple-element.35), channel_id=1, source_target_pairs={{0,1},{1,0},{2,3},{3,2},{4,5},{5,4},{6,7},{7,6},{8,9},{9,8},{10,11... | collective-permute-start | bytes 589832 | tf_op jit(solution)/shard_map/ppermute | solution.py:22
  71.8 2.1 %collective-permute-start.27 = (f32[2,2,128,256]{3,2,1,0:T(8,128)S(1)}, f32[2,2,128,256]{3,2,1,0:T(8,128)S(1)}, u32[]{:S(2)}, u32[]{:S(2)}) collective-permute-start(f32[2,2,128,256]{3,2,1,0:T(8,128)S(1)} %split.23), channel_id=1, source_target_pairs={{0,1},{1,0},{2,3},{3,2},{4,5},{5,4},{6,7},{7,6},{8,9},{9,8},{10,11... | collective-permute-start | bytes 1572872 | tf_op jit(solution)/shard_map/ppermute | solution.py:22
  72.3 7.8 %collective-permute-start.24 = (f32[3,128,128]{2,1,0:T(8,128)S(1)}, f32[3,128,128]{2,1,0:T(8,128)S(1)}, u32[]{:S(2)}, u32[]{:S(2)}) collective-permute-start(f32[3,128,128]{2,1,0:T(8,128)S(1)} %add.70.mine_ref), channel_id=1, source_target_pairs={{0,2},{1,3},{2,0},{3,1},{4,6},{5,7},{6,4},{7,5},{8,10},{9,11},{10,... | collective-permute-start | bytes 589832 | tf_op jit(solution)/shard_map/ppermute | solution.py:22
  74.0 10.7 %collective-permute-start.28 = (f32[128,256]{1,0:T(8,128)S(1)}, f32[128,256]{1,0:T(8,128)S(1)}, u32[]{:S(2)}, u32[]{:S(2)}) collective-permute-start(f32[128,256]{1,0:T(8,128)S(1)} %get-tuple-element.46), channel_id=1, source_target_pairs={{0,4},{4,0},{8,12},{12,8},{16,20},{20,16},{24,28},{28,24},{1,5},{5... | collective-permute-start | bytes 393224 | tf_op jit(solution)/shard_map/ppermute | solution.py:22
  74.8 10.0 %collective-permute-start.29 = (f32[128,256]{1,0:T(8,128)S(1)}, f32[128,256]{1,0:T(8,128)S(1)}, u32[]{:S(2)}, u32[]{:S(2)}) collective-permute-start(f32[128,256]{1,0:T(8,128)S(1)} %get-tuple-element.44), channel_id=1, source_target_pairs={{0,2},{1,3},{2,0},{3,1},{4,6},{5,7},{6,4},{7,5},{8,10},{9,11},{10,... | collective-permute-start | bytes 393224 | tf_op jit(solution)/shard_map/ppermute | solution.py:22
  75.2 9.7 %collective-permute-start.30 = (f32[128,256]{1,0:T(8,128)S(1)}, f32[128,256]{1,0:T(8,128)S(1)}, u32[]{:S(2)}, u32[]{:S(2)}) collective-permute-start(f32[128,256]{1,0:T(8,128)S(1)} %get-tuple-element.45), channel_id=1, source_target_pairs={{0,6},{1,7},{2,4},{3,5},{4,2},{5,3},{6,0},{7,1},{8,14},{9,15},{10,... | collective-permute-start | bytes 393224 | tf_op jit(solution)/shard_map/ppermute | solution.py:33
  85.0 7.4 %collective-permute-start.31 = (f16[128,256]{1,0:T(8,128)(2,1)S(1)}, f16[128,256]{1,0:T(8,128)(2,1)S(1)}, u32[]{:S(2)}, u32[]{:S(2)}) collective-permute-start(f16[128,256]{1,0:T(8,128)(2,1)S(1)} %fusion.2), channel_id=1, source_target_pairs={{0,8},{4,12},{8,0},{12,4},{16,24},{20,28},{24,16},{28,20},{1,9},{5... | collective-permute-start | bytes 196616 | tf_op jit(solution)/shard_map/ppermute | solution.py:22
  85.6 7.2 %collective-permute-start.32 = (f16[128,256]{1,0:T(8,128)(2,1)S(1)}, f16[128,256]{1,0:T(8,128)(2,1)S(1)}, u32[]{:S(2)}, u32[]{:S(2)}) collective-permute-start(f16[128,256]{1,0:T(8,128)(2,1)S(1)} %fusion.2), channel_id=1, source_target_pairs={{0,16},{4,20},{8,24},{12,28},{16,0},{20,4},{24,8},{28,12},{1,17},{... | collective-permute-start | bytes 196616 | tf_op jit(solution)/shard_map/ppermute | solution.py:22
  88.8 6.1 %collective-permute-start.33 = (f16[128,256]{1,0:T(8,128)(2,1)S(1)}, f16[128,256]{1,0:T(8,128)(2,1)S(1)}, u32[]{:S(2)}, u32[]{:S(2)}) collective-permute-start(f16[128,256]{1,0:T(8,128)(2,1)S(1)} %fusion.2), channel_id=1, source_target_pairs={{0,24},{4,28},{8,16},{12,20},{16,8},{20,12},{24,0},{28,4},{1,25},{... | collective-permute-start | bytes 196616 | tf_op jit(solution)/shard_map/ppermute | solution.py:22
  94.9 4.3 %collective-permute-start.34 = (f16[128,256]{1,0:T(8,128)(2,1)S(1)}, f16[128,256]{1,0:T(8,128)(2,1)S(1)}, u32[]{:S(2)}, u32[]{:S(2)}) collective-permute-start(f16[128,256]{1,0:T(8,128)(2,1)S(1)} %add_convert_fusion), channel_id=1, source_target_pairs={{0,4},{4,0},{8,12},{12,8},{16,20},{20,16},{24,28},{28,24},{1,5},{5... | collective-permute-start | bytes 196616 | tf_op jit(solution)/shard_map/ppermute | solution.py:22
  95.7 4.3 %collective-permute-start.35 = (f16[128,256]{1,0:T(8,128)(2,1)S(1)}, f16[128,256]{1,0:T(8,128)(2,1)S(1)}, u32[]{:S(2)}, u32[]{:S(2)}) collective-permute-start(f16[128,256]{1,0:T(8,128)(2,1)S(1)} %add_convert_fusion), channel_id=1, source_target_pairs={{0,2},{1,3},{2,0},{3,1},{4,6},{5,7},{6,4},{7,5},{8,10},{9,11},{10,... | collective-permute-start | bytes 196616 | tf_op jit(solution)/shard_map/ppermute | solution.py:22
  97.2 5.2 %collective-permute-start.36 = (f16[128,256]{1,0:T(8,128)(2,1)S(1)}, f16[128,256]{1,0:T(8,128)(2,1)S(1)}, u32[]{:S(2)}, u32[]{:S(2)}) collective-permute-start(f16[128,256]{1,0:T(8,128)(2,1)S(1)} %add_convert_fusion), channel_id=1, source_target_pairs={{0,6},{1,7},{2,4},{3,5},{4,2},{5,3},{6,0},{7,1},{8,14},{9,15},{10,... | collective-permute-start | bytes 196616 | tf_op jit(solution)/shard_map/ppermute | solution.py:33
  102.5 1.6 %collective-permute-start.37 = (f16[2,2,128,256]{3,2,1,0:T(8,128)(2,1)S(1)}, f16[2,2,128,256]{3,2,1,0:T(8,128)(2,1)S(1)}, u32[]{:S(2)}, u32[]{:S(2)}) collective-permute-start(f16[2,2,128,256]{3,2,1,0:T(8,128)(2,1)S(1)} %get-tuple-element.47), channel_id=1, source_target_pairs={{0,1},{1,0},{2,3},{3,2},{4,5},{5,4},{6,7},{7,6},{8,9},{9,8},{10,11... | collective-permute-start | bytes 786440 | tf_op jit(solution)/shard_map/ppermute | solution.py:22

commit v2 on v1

--- a/solution.py
+++ b/solution.py
@@ -60,15 +60,13 @@
     return x
 
 
-def gather_rows(x):
+def gather_rows(x, first=None):
     half = lax.axis_size("rows") // 2
+    even = [swap(x, "rows", 2 * i) for i in range(1, half)]
     across = swap(x, "rows", 1)
-    even = [swap(x, "rows", 2 * i) for i in range(1, half)]
-    middle = half // 2
-    odd = [
-        swap(jnp.concatenate(part, axis=0), "rows", 1) for part in (even[:middle], even[middle:])
-    ]
-    return [x] + even + [across] + odd
+    if first is not None:
+        even = after(even, first)
+    return [x] + even + [across] + [swap(p, "rows", 1) for p in even]
 
 
 def tree_sum(parts):
@@ -77,17 +75,13 @@
     return parts[0]
 
 
-def half_of(x, scale):
-    return (x * scale).astype(jnp.float16)
-
-
-def scatter_cols(x, scale):
+def scatter_cols(x):
     for b in range(bits_of("cols")):
         keep, give = jnp.split(x, 2, axis=0)
         if b == 0:
             x = keep + swap(give, "cols", 1)
         else:
-            x = keep + swap(half_of(give, scale), "cols", 1 << b).astype(jnp.float32) / scale
+            x = keep + swap(give.astype(jnp.float16), "cols", 1 << b).astype(jnp.float32)
     return x
 
 
@@ -130,54 +124,83 @@
     return factors, gram
 
 
-def prepare_kernel(rows_ref, cols_ref, counts_ref, tiles_ref, cores_ref, factor_ref,
-                   places_ref, scale_ref, live_ref, copied_ref, own_ref, *, half, terms):
+def prepare_kernel(rows_hbm, cols_hbm, counts_ref, tiles_hbm, cores_hbm, factor_hbm,
+                   places_ref, scale_ref, tiles_ref, copied_ref, own_ref,
+                   rows_ref, cols_ref, sems, *, half, terms):
     relations, slots = tiles_ref.shape[0], tiles_ref.shape[1]
     my_row = lax.axis_index("rows")
     my_col = lax.axis_index("cols")
-    own_ref[...] = factor_ref[...]
+    copies = [
+        pltpu.make_async_copy(source, target, sems.at[i])
+        for i, (source, target) in enumerate(
+            (
+                (cores_hbm, copied_ref),
+                (rows_hbm, rows_ref),
+                (cols_hbm, cols_ref),
+                (tiles_hbm, tiles_ref),
+                (factor_hbm, own_ref),
+            )
+        )
+    ]
+    for copy in copies:
+        copy.start()
+    copies[0].wait()
     reach = jnp.zeros((1, 1), jnp.float32)
     for k in range(relations):
-        core = cores_ref[k]
-        copied_ref[k] = core
-        size = jnp.abs(core.astype(jnp.float32))
+        size = jnp.abs(copied_ref[k].astype(jnp.float32))
         for axis in (0, 1):
             sums = jnp.sum(size, axis=axis, keepdims=True)
             reach = jnp.maximum(reach, jnp.max(sums, axis=1 - axis, keepdims=True))
+    scale_ref[...] = jnp.broadcast_to(
+        f16_top / (terms * relations * slots * product_bound * reach + 1e-20), scale_ref.shape
+    )
+    for copy in copies[1:]:
+        copy.wait()
+    for k in range(relations):
         for s in range(slots):
-            live = s < counts_ref[k, 0, 0]
-            values = tiles_ref[k, s]
-            live_ref[k, s] = jnp.where(live, values, jnp.zeros_like(values))
             col = cols_ref[k, 0, s] ^ my_row
             places_ref[k, s] = (col & 1) * half + (col >> 1)
             places_ref[k, slots + s] = rows_ref[k, 0, s] ^ my_col
-    scale_ref[...] = jnp.broadcast_to(
-        f16_top / (terms * relations * slots * product_bound * reach + 1e-20), scale_ref.shape
-    )
+
+            @pl.when(s >= counts_ref[k, 0, 0])
+            def _():
+                tiles_ref[k, s] = jnp.zeros(tiles_ref.shape[2:], tiles_ref.dtype)
+
+
+def stay(x):
+    return pltpu.with_memory_space_constraint(x, pltpu.HBM)
 
 
 def prepare(rows, cols, counts, tiles, cores, factor):
     n_rows, n_cols = lax.axis_size("rows"), lax.axis_size("cols")
     smem = pl.BlockSpec(memory_space=pltpu.SMEM)
     vmem = pl.BlockSpec(memory_space=pltpu.VMEM)
+    anywhere = pl.BlockSpec(memory_space=pltpu.HBM)
     return pl.pallas_call(
         functools.partial(prepare_kernel, half=n_rows // 2, terms=2.0 * n_cols),
         out_shape=(
             jax.ShapeDtypeStruct((tiles.shape[0], 2 * tiles.shape[1]), jnp.int32),
-            jax.ShapeDtypeStruct((8, 128), jnp.float32),
+            jax.ShapeDtypeStruct((1, cores.shape[-1]), jnp.float32),
             jax.ShapeDtypeStruct(tiles.shape, tiles.dtype),
             jax.ShapeDtypeStruct(cores.shape, cores.dtype),
             jax.ShapeDtypeStruct(factor.shape, factor.dtype),
         ),
-        in_specs=[smem, smem, smem, vmem, vmem, vmem],
+        in_specs=[anywhere, anywhere, smem, anywhere, anywhere, anywhere],
         out_specs=(smem, vmem, vmem, vmem, vmem),
+        scratch_shapes=[
+            pltpu.SMEM(rows.shape, jnp.int32),
+            pltpu.SMEM(cols.shape, jnp.int32),
+            pltpu.SemaphoreType.DMA((5,)),
+        ],
         compiler_params=params(),
         cost_estimate=cost(2.0),
         name="prepare",
-    )(rows, cols, counts, tiles, cores, factor)
-
-
-def first_kernel(places_ref, tiles_ref, factors_ref, panel_ref, cores_ref,
+    )(
+        stay(rows), stay(cols), counts, stay(tiles), stay(cores), stay(factor)
+    )
+
+
+def first_kernel(places_ref, scale_ref, tiles_ref, factors_ref, panel_ref, cores_ref,
                  direct_ref, back_ref, acc_ref, turned_ref, sums_ref, *, bits_c):
     relations, slots = tiles_ref.shape[0], tiles_ref.shape[1]
     tile = tiles_ref.shape[2]
@@ -200,16 +223,17 @@
             high = whole.astype(jnp.bfloat16)
             low = (whole - high.astype(jnp.float32)).astype(jnp.bfloat16)
             part = dot(high, core, ((1,), (1,))) + dot(low, core, ((1,), (1,)))
+            part = part * scale_ref[...]
             place = reversed_slot(i, bits_c)
             if k == 0:
                 direct_ref[place] = part
             else:
                 direct_ref[place] += part
     for g in range(sums_ref.shape[0]):
-        back_ref[g] = sums_ref[g].T
-
-
-def first_pass(places, tiles, factors, panel, cores):
+        back_ref[g] = sums_ref[g].T * scale_ref[...]
+
+
+def first_pass(places, scale, tiles, factors, panel, cores):
     tile = tiles.shape[2]
     rank = cores.shape[-1]
     n_rows, n_cols = lax.axis_size("rows"), lax.axis_size("cols")
@@ -221,7 +245,7 @@
             jax.ShapeDtypeStruct((n_cols, tile, rank), jnp.float32),
             jax.ShapeDtypeStruct((n_rows, tile, rank), jnp.float32),
         ),
-        in_specs=[smem, vmem, vmem, vmem, vmem],
+        in_specs=[smem, vmem, vmem, vmem, vmem, vmem],
         out_specs=(vmem, vmem),
         scratch_shapes=[
             pltpu.VMEM((n_cols, tile, rank), jnp.float32),
@@ -231,7 +255,7 @@
         compiler_params=params(),
         cost_estimate=cost(4.8),
         name="first_pass",
-    )(places, tiles, factors.reshape(n_rows, tile, rank), panel, cores)
+    )(places, scale, tiles, factors.reshape(n_rows, tile, rank), panel, cores)
 
 
 def second_kernel(places_ref, tiles_ref, factors_ref, panel_ref,
@@ -296,29 +320,46 @@
 def eliminate(z_ref, begin, end, block, sub):
     size = z_ref.shape[0]
     wide = size // 128
+    groups = block // 8
+    rows = lax.broadcasted_iota(jnp.int32, (8, 128), 0)
+    rows_wide = lax.broadcasted_iota(jnp.int32, (8, size), 0)
+    lanes = lax.broadcasted_iota(jnp.int32, (8, size), 1)
     for p in range(begin, end):
         o = p * block
-        panel = z_ref[o:o + block, :]
-        rows = lax.broadcasted_iota(jnp.int32, (block, 128), 0)
-        rows_wide = lax.broadcasted_iota(jnp.int32, (block, size), 0)
-        lanes = lax.broadcasted_iota(jnp.int32, (block, size), 1)
+        panel = [z_ref[o + 8 * g:o + 8 * g + 8, :] for g in range(groups)]
         for q in range(block // sub):
             first = o + q * sub
+            start = q * sub // 8
             cols = [
-                jnp.broadcast_to(panel[:, first + m:first + m + 1], (block, 128))
+                {
+                    g: jnp.broadcast_to(panel[g][:, first + m:first + m + 1], (8, 128))
+                    for g in range(start, groups)
+                }
                 for m in range(sub)
             ]
             for m in range(sub):
                 j = q * sub + m
-                root = lax.rsqrt(cols[m][j:j + 1, :])
-                factors = jnp.where(rows > j, cols[m] * root, 0.0)
+                own, i = j // 8, j % 8
+                root = lax.rsqrt(cols[m][own][i:i + 1, :])
+                factors = {g: cols[m][g] * root for g in range(own, groups)}
+                factors[own] = jnp.where(rows > i, factors[own], 0.0)
                 for t in range(m + 1, sub):
-                    cols[t] = cols[t] - factors * (cols[t][j:j + 1, :] * root)
-                unit = jnp.where(rows_wide == j, 1.0, 0.0)
-                panel = jnp.where(lanes == o + j, unit, panel)
-                line = panel[j:j + 1, :] * jnp.concatenate([root] * wide, axis=1)
-                factors = jnp.concatenate([factors] * wide, axis=1)
-                panel = jnp.where(rows_wide == j, line, panel - factors * line)
+                    line = cols[t][own][i:i + 1, :] * root
+                    for g in range(own, groups):
+                        cols[t][g] = cols[t][g] - factors[g] * line
+                pivot = lanes == o + j
+                panel[own] = jnp.where(pivot, jnp.where(rows_wide == i, 1.0, 0.0), panel[own])
+                line = panel[own][i:i + 1, :] * jnp.concatenate([root] * wide, axis=1)
+                for g in range(own, groups):
+                    factor = jnp.concatenate([factors[g]] * wide, axis=1)
+                    if g > own:
+                        panel[g] = jnp.where(pivot, 0.0, panel[g])
+                    panel[g] = panel[g] - factor * line
+                panel[own] = jnp.where(rows_wide == i, line, panel[own])
+        panel = jnp.concatenate(panel, axis=0)
+        below = lax.broadcasted_iota(jnp.int32, (block, size), 0) + o
+        across = lax.broadcasted_iota(jnp.int32, (block, size), 1)
+        panel = jnp.where((across > below) & (across < o + block), 0.0, panel)
         z_ref[o:o + block, :] = panel
         rest = size - o - block
         if rest:
@@ -326,8 +367,8 @@
             left = jnp.concatenate([high, high, mid, mid, high, low], axis=0)[:, o + block:]
             right = jnp.concatenate([high, mid, high, mid, low, high], axis=0)
             change = dot(left, right, ((0,), (0,)))
-            lanes = lax.broadcasted_iota(jnp.int32, (rest, size), 1)
-            done = (lanes >= o) & (lanes < o + block)
+            spread = lax.broadcasted_iota(jnp.int32, (rest, size), 1)
+            done = (spread >= o) & (spread < o + block)
             z_ref[o + block:, :] = jnp.where(done, 0.0, z_ref[o + block:, :]) - change
 
 
@@ -357,17 +398,39 @@
             middle = jnp.concatenate(split(middle, 3), axis=1)
             total = total + dot(middle, jnp.concatenate([right] * 3, axis=0))
     z_ref[...] = total
-    eliminate(z_ref, 0, size // 128, 32, 16)
-
-
-def inverse_kernel(in_ref, out_ref, z_ref):
+    eliminate(z_ref, 0, 3 * size // 256, 32, 16)
+
+
+def inverse_kernel(in_ref, scale_ref, out_ref, z_ref):
     size = z_ref.shape[0]
     z_ref[...] = in_ref[...]
-    eliminate(z_ref, size // 128, size // 32, 32, 16)
+    eliminate(z_ref, 3 * size // 256, size // 32, 32, 16)
     high, mid, low = split(lower_of(z_ref[...]), 3)
     left = jnp.concatenate([high, high, mid, mid, high, low], axis=0)
     right = jnp.concatenate([high, mid, high, mid, low, high], axis=0)
-    out_ref[...] = dot(left, right, ((0,), (0,)))
+    out_ref[...] = dot(left, right, ((0,), (0,))) / scale_ref[...]
+
+
+def scale_kernel(mine_ref, other_ref, scale_ref, back_ref, *, bound):
+    largest = jnp.max(mine_ref[...] + other_ref[...], axis=0)
+    largest = jnp.max(jnp.max(largest, axis=0, keepdims=True), axis=1, keepdims=True)
+    scale = f16_top / (bound * jnp.broadcast_to(largest, scale_ref.shape) + 1e-30)
+    scale_ref[...] = scale
+    back_ref[...] = 1.0 / scale
+
+
+def core_scale(pair, rank, bound):
+    vmem = pl.BlockSpec(memory_space=pltpu.VMEM)
+    vector = jax.ShapeDtypeStruct((1, rank), jnp.float32)
+    return pl.pallas_call(
+        functools.partial(scale_kernel, bound=bound),
+        out_shape=(vector, vector),
+        in_specs=[vmem, vmem],
+        out_specs=(vmem, vmem),
+        compiler_params=params(),
+        cost_estimate=cost(0.5),
+        name="core_scale",
+    )(*pair)
 
 
 def begin_kernel(mine_ref, other_ref, out_ref):
@@ -400,43 +463,76 @@
     )(*args)
 
 
-def whiten_kernel(z_ref, factor_ref, near_ref, far_ref, out_ref, core_ref, *, bits_c):
-    relations, rank = out_ref.shape[0], out_ref.shape[1]
-    halves = near_ref.shape[0]
-    pieces = 2 * halves // relations
-    height = near_ref.shape[2]
-    my_col = lax.axis_index("cols")
-    my_row = lax.axis_index("rows")
-    core_ref[:halves] = near_ref[...]
-    core_ref[halves:] = far_ref[...]
+def whitened(left, right, core):
+    first, rest = split(core, 2)
+    middle = dot(left, jnp.concatenate([first, rest, first], axis=0))
+    first, rest = split(middle, 2)
+    return dot(jnp.concatenate([first, first, rest], axis=1), right, ((1,), (1,)))
+
+
+def whiten_parts(z_ref):
     high, low = split(lower_of(z_ref[...]), 2)
     left = jnp.concatenate([high, high, low], axis=1)
     right = jnp.concatenate([high, low, high], axis=1)
+    return left, right
+
+
+def whiten_kernel(z_ref, factor_ref, near_ref, far_ref, out_ref, core_ref, *, bits_c):
+    relations, halves = out_ref.shape[0], near_ref.shape[0]
+    pieces = 2 * halves // relations
+    my_col = lax.axis_index("cols")
+    my_row = lax.axis_index("rows")
+    left, right = whiten_parts(z_ref)
+    core_ref[:halves] = near_ref[...]
+    core_ref[halves:] = far_ref[...]
     for k in range(relations):
         parts = []
         for p in range(pieces):
             place = reversed_slot((k * pieces + p) ^ my_col, bits_c)
             parts += [core_ref[place, h ^ (my_row & 1)] for h in range(2)]
-        core = jnp.concatenate(parts, axis=0) * factor_ref[0]
-        first, rest = split(core, 2)
-        middle = dot(left, jnp.concatenate([first, rest, first], axis=0))
-        first, rest = split(middle, 2)
-        out_ref[k] = dot(jnp.concatenate([first, first, rest], axis=1), right, ((1,), (1,)))
+        core = jnp.concatenate(parts, axis=0) * factor_ref[...]
+        out_ref[k] = whitened(left, right, core)
+
+
+def half_whiten_kernel(z_ref, factor_ref, core_ref, *refs, bits_c):
+    out_ref = refs[-1]
+    my_col = lax.axis_index("cols")
+    my_row = lax.axis_index("rows")
+    left, right = whiten_parts(z_ref)
+    for p in range(core_ref.shape[0]):
+        slot = 2 * reversed_slot(p, bits_c - 1)
+        parts = [core_ref[p, h ^ (my_row & 1)] for h in range(2)]
+        core = jnp.concatenate(parts, axis=0) * factor_ref[...]
+        result = whitened(left, right, core)
+        if len(refs) == 1:
+            out_ref[p] = result
+        else:
+            out_ref[slot ^ my_col] = refs[0][p]
+            out_ref[(slot + 1) ^ my_col] = result
 
 
 def whiten(z, factor, near, far, relations):
     rank = z.shape[0]
+    halves = near.shape[0]
     vmem = pl.BlockSpec(memory_space=pltpu.VMEM)
-    return pl.pallas_call(
-        functools.partial(whiten_kernel, bits_c=bits_of("cols")),
-        out_shape=jax.ShapeDtypeStruct((relations, rank, rank), jnp.float32),
-        in_specs=[vmem, pl.BlockSpec(memory_space=pltpu.SMEM), vmem, vmem],
-        out_specs=vmem,
-        scratch_shapes=[pltpu.VMEM((2 * near.shape[0],) + near.shape[1:], jnp.float32)],
-        compiler_params=params(),
-        cost_estimate=cost(2.3),
-        name="whiten",
-    )(z, factor.reshape(1), near, far)
+
+    def call(kernel, count, microseconds, *args, scratch=()):
+        return pl.pallas_call(
+            functools.partial(kernel, bits_c=bits_of("cols")),
+            out_shape=jax.ShapeDtypeStruct((count, rank, rank), jnp.float32),
+            in_specs=[vmem] * (2 + len(args)),
+            out_specs=vmem,
+            scratch_shapes=scratch,
+            compiler_params=params(),
+            cost_estimate=cost(microseconds),
+            name="whiten",
+        )(z, factor, *args)
+
+    if 2 * halves != relations:
+        scratch = [pltpu.VMEM((2 * halves,) + near.shape[1:], jnp.float32)]
+        return call(whiten_kernel, relations, 2.3, near, far, scratch=scratch)
+    first = call(half_whiten_kernel, halves, 1.2, near)
+    return call(half_whiten_kernel, relations, 1.2, far, first)
 
 
 def pair_of_sums(x):
@@ -453,29 +549,25 @@
     places, scale, tiles, cores, own = prepare(
         tile_rows, tile_cols, tile_counts, tile_values, cores, factor
     )
-    scale = scale[0, 0]
-
-    factors, gram = gram_of([own] + gather_rows(factor)[1:])
+
+    factors, gram = gram_of([own] + gather_rows(factor, own)[1:])
     panel = gather_cols(factor)
     gram_pair = pair_of_sums(gram)
-    direct, back = first_pass(places, tiles, after(factors, gram_pair[0]), panel, cores)
+    direct, back = first_pass(places, scale, tiles, after(factors, gram_pair[0]), panel, cores)
     direct, back = after((direct, back), gram_pair)
-    system = square_call(system_kernel, "system", 5.5, rank, *gram_pair, cores)
-    parts = []
-    for begin in range(half, 0, -half // 2):
-        begin = begin - half // 2
-        end = begin + half // 2
-        give = half_of(back[half + begin:half + end], scale)
-        parts = [back[begin:end] + swap(give, "rows", 1).astype(jnp.float32) / scale] + parts
-    packed = [after(half_of(part, scale), system) for part in parts]
-    received = [
-        swap(packed[i // (half // 2)][i % (half // 2)], "rows", 2 * i).astype(jnp.float32)
-        for i in range(1, half)
+    system = square_call(system_kernel, "system", 3.8, rank, *gram_pair, cores)
+    middle = half + half // 2
+    far = swap(back[middle:].astype(jnp.float16), "rows", 1).astype(jnp.float32)
+    close = swap(back[half:middle].astype(jnp.float16), "rows", 1).astype(jnp.float32)
+    far = back[half // 2:half] + far
+    close = back[:half // 2] + close
+    packed = [
+        after(x[i].astype(jnp.float16), system) for x in (close, far) for i in range(half // 2)
     ]
-    numerator = (
-        scatter_cols(direct, scale)[0] + parts[0][0] + functools.reduce(jnp.add, received) / scale
-    )
-    inverse = square_call(inverse_kernel, "inverse", 4.0, rank, system, scratch=True)
+    packed[half - 1] = after(packed[half - 1], close)
+    received = [swap(packed[i], "rows", 2 * i).astype(jnp.float32) for i in range(1, half)]
+    numerator = scatter_cols(direct)[0] + close[0] + functools.reduce(jnp.add, received)
+    inverse = square_call(inverse_kernel, "inverse", 5.2, rank, system, scale, scratch=True)
     factor_new = dot(numerator, inverse, precision=lax.Precision.HIGHEST).astype(jnp.bfloat16)
 
     factors_new, gram_new = gram_of(gather_rows(factor_new))
@@ -484,31 +576,31 @@
     core = second_pass(places, tiles, factors_new, panel_new)
     keep, give = jnp.split(after(core, gram_pair[0]), 2, axis=0)
     core = keep + swap(give, "cols", 1)
-    z = square_call(begin_kernel, "begin", 3.3, rank, *gram_pair)
     bits = bits_of("cols")
     slots_left = [2 * reversed_slot(p, bits - 1) for p in range(n_cols // 2)]
     plane = [(h, p) for p in range(n_cols // 2) for h in range(2) if (h, p) != (0, 0)]
     core = core[0, 0] + functools.reduce(
         jnp.add, [swap_both(core[p, h], h, slots_left[p]) for h, p in plane]
     )
-    longest = jnp.max(gram_pair[0] + gram_pair[1])
-    tiles_in_all = n_rows * n_cols
-    scale_core = f16_top / (2.0 * slots * tile * value_bound * tiles_in_all * longest + 1e-30)
-    packed = after(half_of(core, scale_core), z)
+    bound = 2.0 * slots * tile * value_bound * n_rows * n_cols
+    scale_core, unit_core = core_scale(gram_pair, rank, bound)
+    z = square_call(begin_kernel, "begin", 3.3, rank, *gram_pair)
+    packed = (core * scale_core).astype(jnp.float16)
     core = tree_sum(
         [packed.astype(jnp.float32)]
         + [swap(packed, "rows", 2 * i).astype(jnp.float32) for i in range(1, half)]
     )
-    z = square_call(end_kernel, "end", 2.9, rank, z)
     core = after(core.astype(jnp.float16), z)
     found = {(h, p): swap_both(core, h, slots_left[p]) for h, p in plane}
+    z = square_call(end_kernel, "end", 2.9, rank, after(z, found[plane[0]]))
     found[(0, 0)] = core
     near = jnp.stack(
         [jnp.stack([found[(h, p)] for h in range(2)]) for p in range(n_cols // 2)]
     )
+    near = after(near, z)
     far = swap(near, "cols", 1)
     cores_new = whiten(
-        z, 1.0 / scale_core, near.astype(jnp.float32), far.astype(jnp.float32), relations
+        z, unit_core, near.astype(jnp.float32), far.astype(jnp.float32), relations
     )
     return (factor_new, cores_new)
 

time: 107 us -> 99.4 us (0.929)
  local copies, waits for them, and re-layouts: 6.03 us -> 0.91 us
  other arithmetic: 4.75 us -> 0.69 us
  starting transfers between devices: 41 us -> 44.2 us
  Pallas kernels: 27.7 us -> 29.3 us
  waiting for transfers between devices: 24.3 us -> 22.8 us
    unnamed x13 -> x5, local copies, waits for them, and re-layouts: 5.4 us -> 0.75 us
    convert_element_type x5 -> x3, other arithmetic: 2.8 us -> 0.09 us  [the longest x1 0.04 us: local(): near.astype(jnp.float32)]
    ppermute x36 -> x38, starting transfers between devices: 37.4 us -> 39.5 us  [swap(): return lax.ppermute(x, axis, [(i, i ^ mask) for i in range(size)])]
    pallas_call x1, Pallas kernels: 1.83 us -> 3.2 us  [prepare(): pl.pallas_call(functools.partial(prepare_kernel, half=n_rows // 2, terms=...]
    ppermute x2, starting transfers between devices: 3.57 us -> 4.7 us  [swap_both(): lax.ppermute(x, ('rows', 'cols'), [(i, i ^ mask) for i in range(size)])]
    ppermute x36 -> x38, waiting for transfers between devices: 21.7 us -> 20.9 us  [swap(): return lax.ppermute(x, axis, [(i, i ^ mask) for i in range(size)])]
    pallas_call x1 -> x3, Pallas kernels: 2.28 us -> 2.72 us  [the longest x2 2.61 us: call(): pl.pallas_call(functools.partial(kernel, bits_c=bits_of('cols')), out_sha...]
  transfers between devices with their start and end apart: 38 -> 40, of which waited for: 16 -> 20; matrix products, arithmetic and copies ran while one was open for 5% -> 1% of each run, Pallas kernels for 24% -> 28%
where the time goes in v2:
time: 99.4 us; the launch traced here: 99.3 us
  starting transfers between devices  44.2 us (44%)
  Pallas kernels  29.3 us (29%)
  waiting for transfers between devices  22.8 us (23%)
  between operations  1.02 us (1%)
    ppermute x38, starting transfers between devices, swap(): return lax.ppermute(x, axis, [(i, i ^ mask) for i in range(size)])  39.5 us
    ppermute x38, waiting for transfers between devices, swap(): return lax.ppermute(x, axis, [(i, i ^ mask) for i in range(size)])  20.9 us
    pallas_call x4, Pallas kernels, square_call(): pl.pallas_call(kernel, out_shape=jax.ShapeDtypeStruct((rank, rank), jnp.f...  15.1 us
    pallas_call x1, Pallas kernels, first_pass(): pl.pallas_call(functools.partial(first_kernel, bits_c=bits_of('cols')), o...  4.85 us
    ppermute x2, starting transfers between devices, swap_both(): lax.ppermute(x, ('rows', 'cols'), [(i, i ^ mask) for i in range(size)])  4.7 us
    pallas_call x1, Pallas kernels, prepare(): pl.pallas_call(functools.partial(prepare_kernel, half=n_rows // 2, terms=...  3.2 us
    pallas_call x1, Pallas kernels, second_pass(): pl.pallas_call(functools.partial(second_kernel, bits_c=bits_of('cols')),...  2.76 us
    pallas_call x2, Pallas kernels, call(): pl.pallas_call(functools.partial(kernel, bits_c=bits_of('cols')), out_sha...  2.61 us
  transfers between devices with their start and end apart: 40, of which 20 were waited for; matrix products, arithmetic and copies ran while one was open for 1% of the time, Pallas kernels for 28%

profile of v2, /device:TPU:0, one launch (start us, length us, event | category | flops | bytes accessed | tf_op | source)
XLA Modules:
  0.0 99.3 jit_solution(14934230915777991242)
XLA Ops:
  0.6 3.1 %collective-permute-start = (bf16[128,256]{1,0:T(8,128)(2,1)}, bf16[128,256]{1,0:T(8,128)(2,1)S(1)}, u32[]{:S(2)}, u32[]{:S(2)}) collective-permute-start(bf16[128,256]{1,0:T(8,128)(2,1)} %factor_hbm.1), channel_id=1, source_target_pairs={{0,8},{4,12},{8,0},{12,4},{16,24},{20,28},{24,16},{28,20},{1,9},{5... | collective-permute-start | bytes 196616 | tf_op jit(solution)/shard_map/ppermute | solution.py:22
  3.7 2.6 %collective-permute-start.1 = (bf16[128,256]{1,0:T(8,128)(2,1)}, bf16[128,256]{1,0:T(8,128)(2,1)S(1)}, u32[]{:S(2)}, u32[]{:S(2)}) collective-permute-start(bf16[128,256]{1,0:T(8,128)(2,1)} %factor_hbm.1), channel_id=1, source_target_pairs={{0,16},{4,20},{8,24},{12,28},{16,0},{20,4},{24,8},{28,12},{1,17},{... | collective-permute-start | bytes 196616 | tf_op jit(solution)/shard_map/ppermute | solution.py:22
  6.3 1.7 %collective-permute-start.3 = (bf16[128,256]{1,0:T(8,128)(2,1)}, bf16[128,256]{1,0:T(8,128)(2,1)S(1)}, u32[]{:S(2)}, u32[]{:S(2)}) collective-permute-start(bf16[128,256]{1,0:T(8,128)(2,1)} %factor_hbm.1), channel_id=1, source_target_pairs={{0,4},{4,0},{8,12},{12,8},{16,20},{20,16},{24,28},{28,24},{1,5},{5... | collective-permute-start | bytes 196616 | tf_op jit(solution)/shard_map/ppermute | solution.py:22
  8.1 0.7 copy.8.counts_ref
  8.8 3.2 %prepare.1 = (s32[4,24]{1,0:T(4,128)S(1)}, f32[1,256]{1,0:T(1,128)S(1)}, bf16[4,12,128,128]{3,2,1,0:T(8,128)(2,1)S(1)}, bf16[4,256,256]{2,1,0:T(8,128)(2,1)S(1)}, bf16[128,256]{1,0:T(8,128)(2,1)S(1)}) custom-call(s32[4,1,12]{2,1,0:T(1,128)} %rows_hbm.1, s32[4,1,12]{2,1,0:T(1,128)} %cols_hbm.1, s32[4,1,1]{2,1,0:T(1,128)S(1)} %copy.8.counts_ref, ...), custom_call_target="tpu_custom_call" | custom-call | flops 2200000000 | bytes 100000 | tf_op jit(solution)/shard_map/prepare/pallas_call | solution.py:179
  12.0 0.6 collective-permute-done.2.refs_3_
  12.6 1.5 %collective-permute-start.4 = (bf16[128,256]{1,0:T(8,128)(2,1)S(1)}, bf16[128,256]{1,0:T(8,128)(2,1)S(1)}, u32[]{:S(2)}, u32[]{:S(2)}) collective-permute-start(bf16[128,256]{1,0:T(8,128)(2,1)S(1)} %collective-permute-done.refs_1_), channel_id=1, source_target_pairs={{0,4},{4,0},{8,12},{12,8},{16,20},{20,16},{24,28},{28,24},{1,5},{5... | collective-permute-start | bytes 196616 | tf_op jit(solution)/shard_map/ppermute | solution.py:22
  14.6 1.5 %collective-permute-start.6 = (bf16[128,256]{1,0:T(8,128)(2,1)S(1)}, bf16[128,256]{1,0:T(8,128)(2,1)S(1)}, u32[]{:S(2)}, u32[]{:S(2)}) collective-permute-start(bf16[128,256]{1,0:T(8,128)(2,1)S(1)} %collective-permute-done.2.refs_3_), channel_id=1, source_target_pairs={{0,4},{4,0},{8,12},{12,8},{16,20},{20,16},{24,28},{28,24},{1,5},{5... | collective-permute-start | bytes 196616 | tf_op jit(solution)/shard_map/ppermute | solution.py:22
  16.2 1.6 %collective-permute-start.9 = (bf16[256,256]{1,0:T(8,128)(2,1)S(1)}, bf16[256,256]{1,0:T(8,128)(2,1)S(1)}, u32[]{:S(2)}, u32[]{:S(2)}) collective-permute-start(bf16[256,256]{1,0:T(8,128)(2,1)S(1)} %pad_maximum_fusion.3), channel_id=1, source_target_pairs={{0,2},{1,3},{2,0},{3,1},{4,6},{5,7},{6,4},{7,5},{8,10},{9,11},{10,... | collective-permute-start | bytes 393224 | tf_op jit(solution)/shard_map/ppermute | solution.py:22
  17.8 0.9 collective-permute-done.5.refs_6_
  18.7 0.7 collective-permute-done.6.refs_7_
  19.9 1.3 %collective-permute-done.9 = bf16[256,256]{1,0:T(8,128)(2,1)S(1)} collective-permute-done((bf16[256,256]{1,0:T(8,128)(2,1)S(1)}, bf16[256,256]{1,0:T(8,128)(2,1)S(1)}, u32[]{:S(2)}, u32[]{:S(2)}) %collective-permute-start.9) | collective-permute-done | bytes 131104 | tf_op jit(solution)/shard_map/ppermute | solution.py:22
  21.3 1.5 %collective-permute-start.10 = (f32[3,128,128]{2,1,0:T(8,128)S(1)}, f32[3,128,128]{2,1,0:T(8,128)S(1)}, u32[]{:S(2)}, u32[]{:S(2)}) collective-permute-start(f32[3,128,128]{2,1,0:T(8,128)S(1)} %add.54.mine_ref), channel_id=1, source_target_pairs={{0,2},{1,3},{2,0},{3,1},{4,6},{5,7},{6,4},{7,5},{8,10},{9,11},{10,... | collective-permute-start | bytes 589832 | tf_op jit(solution)/shard_map/ppermute | solution.py:22
  22.9 4.8 %first_pass.1 = (f32[4,128,256]{2,1,0:T(8,128)S(1)}, f32[8,128,256]{2,1,0:T(8,128)S(1)}) custom-call(s32[4,24]{1,0:T(4,128)S(1)} %get-tuple-element.29.places_ref, f32[1,256]{1,0:T(1,128)S(1)} %get-tuple-element.30.scale_ref, bf16[4,12,128,128]{3,2,1,0:T(8,128)(2,1)S(1)} %get-tuple-element.31.tiles_ref, bf16[8,128,256]{2,1,0:T(8,128)(2,1)S(1)} %bitcast.38, ...), custom_call_target="tpu_custom_call" | custom-call | flops 5280000000 | bytes 100000 | tf_op jit(solution)/shard_map/first_pass/pallas_call | solution.py:242
  27.7 0.6 collective-permute-done.10.other_ref
  28.5 1.1 %collective-permute-start.13 = (f16[2,128,256]{2,1,0:T(8,128)(2,1)S(1)}, f16[2,128,256]{2,1,0:T(8,128)(2,1)S(1)}, u32[]{:S(2)}, u32[]{:S(2)}) collective-permute-start(f16[2,128,256]{2,1,0:T(8,128)(2,1)S(1)} %get-tuple-element.62), channel_id=1, source_target_pairs={{0,4},{4,0},{8,12},{12,8},{16,20},{20,16},{24,28},{28,24},{1,5},{5... | collective-permute-start | bytes 393224 | tf_op jit(solution)/shard_map/ppermute | solution.py:22
  29.6 1.0 collective-permute-start.15
  30.7 4.6 %system.1.in_ref = f32[256,256]{1,0:T(8,128)S(1)} custom-call(f32[3,128,128]{2,1,0:T(8,128)S(1)} %add.54.mine_ref, f32[3,128,128]{2,1,0:T(8,128)S(1)} %collective-permute-done.10.other_ref, bf16[4,256,256]{2,1,0:T(8,128)(2,1)S(1)} %get-tuple-element.39.cores_ref), custom_call_target="tpu_custom_call" | custom-call | flops 4180000000 | bytes 100000 | tf_op jit(solution)/shard_map/system/pallas_call | solution.py:454
  35.3 0.8 collective-permute-done.15
  36.2 0.7 collective-permute-start.14
  36.9 3.6 %collective-permute-start.16 = (f16[128,256]{1,0:T(8,128)(2,1)S(1)}, f16[128,256]{1,0:T(8,128)(2,1)S(1)}, u32[]{:S(2)}, u32[]{:S(2)}) collective-permute-start(f16[128,256]{1,0:T(8,128)(2,1)S(1)} %get-tuple-element.45), channel_id=1, source_target_pairs={{0,16},{4,20},{8,24},{12,28},{16,0},{20,4},{24,8},{28,12},{1,17},{... | collective-permute-start | bytes 196616 | tf_op jit(solution)/shard_map/ppermute | solution.py:22
  40.8 1.5 %collective-permute-start.12 = (f16[1,128,256]{2,1,0:T(8,128)(2,1)S(1)}, f16[1,128,256]{2,1,0:T(8,128)(2,1)S(1)}, u32[]{:S(2)}, u32[]{:S(2)}) collective-permute-start(f16[1,128,256]{2,1,0:T(8,128)(2,1)S(1)} %slice_convert_fusion.1), channel_id=1, source_target_pairs={{0,2},{1,3},{2,0},{3,1},{4,6},{5,7},{6,4},{7,5},{8,10},{9,11},{10,... | collective-permute-start | bytes 196616 | tf_op jit(solution)/shard_map/ppermute | solution.py:22
  42.3 4.3 %inverse.1 = f32[256,256]{1,0:T(8,128)S(1)} custom-call(f32[256,256]{1,0:T(8,128)S(1)} %system.1.in_ref, f32[1,256]{1,0:T(1,128)S(1)} %get-tuple-element.30.scale_ref), custom_call_target="tpu_custom_call" | custom-call | flops 5720000000 | bytes 100000 | tf_op jit(solution)/shard_map/inverse/pallas_call | solution.py:454
  47.6 3.7 %collective-permute-start.19 = (bf16[128,256]{1,0:T(8,128)(2,1)S(1)}, bf16[128,256]{1,0:T(8,128)(2,1)S(1)}, u32[]{:S(2)}, u32[]{:S(2)}) collective-permute-start(bf16[128,256]{1,0:T(8,128)(2,1)S(1)} %convolution_convert_fusion.refs_0_), channel_id=1, source_target_pairs={{0,16},{4,20},{8,24},{12,28},{16,0},{20,4},{24,8},{28,12},{1,17},{... | collective-permute-start | bytes 196616 | tf_op jit(solution)/shard_map/ppermute | solution.py:22
  51.5 1.4 %collective-permute-start.28 = (bf16[256,256]{1,0:T(8,128)(2,1)S(1)}, bf16[256,256]{1,0:T(8,128)(2,1)S(1)}, u32[]{:S(2)}, u32[]{:S(2)}) collective-permute-start(bf16[256,256]{1,0:T(8,128)(2,1)S(1)} %pad_maximum_fusion.4), channel_id=1, source_target_pairs={{0,2},{1,3},{2,0},{3,1},{4,6},{5,7},{6,4},{7,5},{8,10},{9,11},{10,... | collective-permute-start | bytes 393224 | tf_op jit(solution)/shard_map/ppermute | solution.py:22
  53.5 1.5 %collective-permute-start.22 = (bf16[128,256]{1,0:T(8,128)(2,1)S(1)}, bf16[128,256]{1,0:T(8,128)(2,1)S(1)}, u32[]{:S(2)}, u32[]{:S(2)}) collective-permute-start(bf16[128,256]{1,0:T(8,128)(2,1)S(1)} %collective-permute-done.18.refs_1_), channel_id=1, source_target_pairs={{0,4},{4,0},{8,12},{12,8},{16,20},{20,16},{24,28},{28,24},{1,5},{5... | collective-permute-start | bytes 196616 | tf_op jit(solution)/shard_map/ppermute | solution.py:22
  56.0 1.4 %collective-permute-done.20.refs_3_ = bf16[128,256]{1,0:T(8,128)(2,1)S(1)} collective-permute-done((bf16[128,256]{1,0:T(8,128)(2,1)S(1)}, bf16[128,256]{1,0:T(8,128)(2,1)S(1)}, u32[]{:S(2)}, u32[]{:S(2)}) %collective-permute-start.20) | collective-permute-done | bytes 65568 | tf_op jit(solution)/shard_map/ppermute | solution.py:22
  58.5 1.7 %collective-permute-done.23.refs_6_ = bf16[128,256]{1,0:T(8,128)(2,1)S(1)} collective-permute-done((bf16[128,256]{1,0:T(8,128)(2,1)S(1)}, bf16[128,256]{1,0:T(8,128)(2,1)S(1)}, u32[]{:S(2)}, u32[]{:S(2)}) %collective-permute-start.23) | collective-permute-done | bytes 65568 | tf_op jit(solution)/shard_map/ppermute | solution.py:22
  60.2 1.5 %collective-permute-done.24.refs_7_ = bf16[128,256]{1,0:T(8,128)(2,1)S(1)} collective-permute-done((bf16[128,256]{1,0:T(8,128)(2,1)S(1)}, bf16[128,256]{1,0:T(8,128)(2,1)S(1)}, u32[]{:S(2)}, u32[]{:S(2)}) %collective-permute-start.24) | collective-permute-done | bytes 65568 | tf_op jit(solution)/shard_map/ppermute | solution.py:22
  62.2 2.8 %second_pass.1 = f32[4,2,128,256]{3,2,1,0:T(8,128)S(1)} custom-call(s32[4,24]{1,0:T(4,128)S(1)} %get-tuple-element.29.places_ref, bf16[4,12,128,128]{3,2,1,0:T(8,128)(2,1)S(1)} %get-tuple-element.31.tiles_ref, bf16[8,128,256]{2,1,0:T(8,128)(2,1)S(1)} %bitcast.39, bf16[512,256]{1,0:T(8,128)(2,1)S(1)} %pad_maximum_fusion.1.panel_ref), custom_call_target="tpu_custom_call" | custom-call | flops 3080000000 | bytes 100000 | tf_op jit(solution)/shard_map/second_pass/pallas_call | solution.py:293
  65.6 0.6 collective-permute-start.26
  66.2 1.0 collective-permute-done.29
  67.2 0.6 collective-permute-start.30
  68.3 2.5 %collective-permute-start.32 = (f32[128,256]{1,0:T(8,128)S(1)}, f32[128,256]{1,0:T(8,128)S(1)}, u32[]{:S(2)}, u32[]{:S(2)}) collective-permute-start(f32[128,256]{1,0:T(8,128)S(1)} %get-tuple-element.59), channel_id=1, source_target_pairs={{0,6},{1,7},{2,4},{3,5},{4,2},{5,3},{6,0},{7,1},{8,14},{9,15},{10,... | collective-permute-start | bytes 393224 | tf_op jit(solution)/shard_map/ppermute | solution.py:33
  70.8 2.5 %collective-permute-done.26.other_ref = f32[3,128,128]{2,1,0:T(8,128)S(1)} collective-permute-done((f32[3,128,128]{2,1,0:T(8,128)S(1)}, f32[3,128,128]{2,1,0:T(8,128)S(1)}, u32[]{:S(2)}, u32[]{:S(2)}) %collective-permute-start.26) | collective-permute-done | bytes 196640 | tf_op jit(solution)/shard_map/ppermute | solution.py:22
  73.5 2.7 %collective-permute-done.31 = f32[128,256]{1,0:T(8,128)S(1)} collective-permute-done((f32[128,256]{1,0:T(8,128)S(1)}, f32[128,256]{1,0:T(8,128)S(1)}, u32[]{:S(2)}, u32[]{:S(2)}) %collective-permute-start.31) | collective-permute-done | bytes 131104 | tf_op jit(solution)/shard_map/ppermute | solution.py:22
  76.2 1.9 %collective-permute-done.32 = f32[128,256]{1,0:T(8,128)S(1)} collective-permute-done((f32[128,256]{1,0:T(8,128)S(1)}, f32[128,256]{1,0:T(8,128)S(1)}, u32[]{:S(2)}, u32[]{:S(2)}) %collective-permute-start.32) | collective-permute-done | bytes 131104 | tf_op jit(solution)/shard_map/ppermute | solution.py:33
  78.1 1.1 %collective-permute-start.33 = (f16[128,256]{1,0:T(8,128)(2,1)S(1)}, f16[128,256]{1,0:T(8,128)(2,1)S(1)}, u32[]{:S(2)}, u32[]{:S(2)}) collective-permute-start(f16[128,256]{1,0:T(8,128)(2,1)S(1)} %fusion.2), channel_id=1, source_target_pairs={{0,8},{4,12},{8,0},{12,4},{16,24},{20,28},{24,16},{28,20},{1,9},{5... | collective-permute-start | bytes 196616 | tf_op jit(solution)/shard_map/ppermute | solution.py:22
  79.2 3.0 %collective-permute-start.34 = (f16[128,256]{1,0:T(8,128)(2,1)S(1)}, f16[128,256]{1,0:T(8,128)(2,1)S(1)}, u32[]{:S(2)}, u32[]{:S(2)}) collective-permute-start(f16[128,256]{1,0:T(8,128)(2,1)S(1)} %fusion.2), channel_id=1, source_target_pairs={{0,16},{4,20},{8,24},{12,28},{16,0},{20,4},{24,8},{28,12},{1,17},{... | collective-permute-start | bytes 196616 | tf_op jit(solution)/shard_map/ppermute | solution.py:22
  82.5 3.2 %begin.1.in_ref = f32[256,256]{1,0:T(8,128)S(1)} custom-call(f32[3,128,128]{2,1,0:T(8,128)S(1)} %add.64.mine_ref, f32[3,128,128]{2,1,0:T(8,128)S(1)} %collective-permute-done.26.other_ref), custom_call_target="tpu_custom_call" | custom-call | flops 3630000128 | bytes 100000 | tf_op jit(solution)/shard_map/begin/pallas_call | solution.py:454
  86.3 2.0 %collective-permute-done.35 = f16[128,256]{1,0:T(8,128)(2,1)S(1)} collective-permute-done((f16[128,256]{1,0:T(8,128)(2,1)S(1)}, f16[128,256]{1,0:T(8,128)(2,1)S(1)}, u32[]{:S(2)}, u32[]{:S(2)}) %collective-permute-start.35) | collective-permute-done | bytes 65568 | tf_op jit(solution)/shard_map/ppermute | solution.py:22
  88.4 0.8 collective-permute-start.36
  89.7 2.2 %collective-permute-start.38 = (f16[128,256]{1,0:T(8,128)(2,1)S(1)}, f16[128,256]{1,0:T(8,128)(2,1)S(1)}, u32[]{:S(2)}, u32[]{:S(2)}) collective-permute-start(f16[128,256]{1,0:T(8,128)(2,1)S(1)} %add_convert_fusion.1), channel_id=1, source_target_pairs={{0,6},{1,7},{2,4},{3,5},{4,2},{5,3},{6,0},{7,1},{8,14},{9,15},{10,... | collective-permute-start | bytes 196616 | tf_op jit(solution)/shard_map/ppermute | solution.py:33
  91.9 0.8 collective-permute-done.36
  92.7 2.9 %end.1.z_ref = f32[256,256]{1,0:T(8,128)S(1)} custom-call(f32[256,256]{1,0:T(8,128)S(1)} %begin.1.in_ref), custom_call_target="tpu_custom_call" | custom-call | flops 3190000128 | bytes 100000 | tf_op jit(solution)/shard_map/end/pallas_call | solution.py:454
  96.0 0.8 whiten.2.refs_0_
  96.8 0.7 collective-permute-done.39
  97.5 1.8 %whiten.3 = f32[4,256,256]{2,1,0:T(8,128)} custom-call(f32[256,256]{1,0:T(8,128)S(1)} %end.1.z_ref, f32[1,256]{1,0:T(1,128)S(1)} %get-tuple-element.54.factor_ref, f32[2,2,128,256]{3,2,1,0:T(8,128)S(1)} %convert_element_type.76.core_ref, f32[2,256,256]{2,1,0:T(8,128)S(1)} %whiten.2.refs_0_), custom_call_target="tpu_custom_call" | custom-call | flops 1320000000 | bytes 100000 | tf_op jit(solution)/shard_map/whiten/pallas_call | solution.py:520
  (74 shorter events, 8.9 us)
Async XLA Ops:
  0.6 11.4 %collective-permute-start = (bf16[128,256]{1,0:T(8,128)(2,1)}, bf16[128,256]{1,0:T(8,128)(2,1)S(1)}, u32[]{:S(2)}, u32[]{:S(2)}) collective-permute-start(bf16[128,256]{1,0:T(8,128)(2,1)} %factor_hbm.1), channel_id=1, source_target_pairs={{0,8},{4,12},{8,0},{12,4},{16,24},{20,28},{24,16},{28,20},{1,9},{5... | collective-permute-start | bytes 196616 | tf_op jit(solution)/shard_map/ppermute | solution.py:22
  3.7 8.3 %collective-permute-start.1 = (bf16[128,256]{1,0:T(8,128)(2,1)}, bf16[128,256]{1,0:T(8,128)(2,1)S(1)}, u32[]{:S(2)}, u32[]{:S(2)}) collective-permute-start(bf16[128,256]{1,0:T(8,128)(2,1)} %factor_hbm.1), channel_id=1, source_target_pairs={{0,16},{4,20},{8,24},{12,28},{16,0},{20,4},{24,8},{28,12},{1,17},{... | collective-permute-start | bytes 196616 | tf_op jit(solution)/shard_map/ppermute | solution.py:22
  6.3 6.3 %collective-permute-start.2 = (bf16[128,256]{1,0:T(8,128)(2,1)}, bf16[128,256]{1,0:T(8,128)(2,1)S(1)}, u32[]{:S(2)}, u32[]{:S(2)}) collective-permute-start(bf16[128,256]{1,0:T(8,128)(2,1)} %factor_hbm.1), channel_id=1, source_target_pairs={{0,24},{4,28},{8,16},{12,20},{16,8},{20,12},{24,0},{28,4},{1,25},{... | collective-permute-start | bytes 196616 | tf_op jit(solution)/shard_map/ppermute | solution.py:22
  6.3 11.5 %collective-permute-start.3 = (bf16[128,256]{1,0:T(8,128)(2,1)}, bf16[128,256]{1,0:T(8,128)(2,1)S(1)}, u32[]{:S(2)}, u32[]{:S(2)}) collective-permute-start(bf16[128,256]{1,0:T(8,128)(2,1)} %factor_hbm.1), channel_id=1, source_target_pairs={{0,4},{4,0},{8,12},{12,8},{16,20},{20,16},{24,28},{28,24},{1,5},{5... | collective-permute-start | bytes 196616 | tf_op jit(solution)/shard_map/ppermute | solution.py:22
  8.1 8.1 %collective-permute-start.8 = (bf16[128,256]{1,0:T(8,128)(2,1)}, bf16[128,256]{1,0:T(8,128)(2,1)S(1)}, u32[]{:S(2)}, u32[]{:S(2)}) collective-permute-start(bf16[128,256]{1,0:T(8,128)(2,1)} %factor_hbm.1), channel_id=1, source_target_pairs={{0,1},{1,0},{2,3},{3,2},{4,5},{5,4},{6,7},{7,6},{8,9},{9,8},{10,11... | collective-permute-start | bytes 196616 | tf_op jit(solution)/shard_map/ppermute | solution.py:22
  8.8 7.4 %copy-start.1 = (bf16[128,256]{1,0:T(8,128)(2,1)S(1)}, bf16[128,256]{1,0:T(8,128)(2,1)}, u32[]{:S(2)}) copy-start(bf16[128,256]{1,0:T(8,128)(2,1)} %factor_hbm.1) | copy-start | bytes 196612
  12.6 5.2 %collective-permute-start.4 = (bf16[128,256]{1,0:T(8,128)(2,1)S(1)}, bf16[128,256]{1,0:T(8,128)(2,1)S(1)}, u32[]{:S(2)}, u32[]{:S(2)}) collective-permute-start(bf16[128,256]{1,0:T(8,128)(2,1)S(1)} %collective-permute-done.refs_1_), channel_id=1, source_target_pairs={{0,4},{4,0},{8,12},{12,8},{16,20},{20,16},{24,28},{28,24},{1,5},{5... | collective-permute-start | bytes 196616 | tf_op jit(solution)/shard_map/ppermute | solution.py:22
  14.1 4.6 %collective-permute-start.5 = (bf16[128,256]{1,0:T(8,128)(2,1)S(1)}, bf16[128,256]{1,0:T(8,128)(2,1)S(1)}, u32[]{:S(2)}, u32[]{:S(2)}) collective-permute-start(bf16[128,256]{1,0:T(8,128)(2,1)S(1)} %collective-permute-done.1.refs_2_), channel_id=1, source_target_pairs={{0,4},{4,0},{8,12},{12,8},{16,20},{20,16},{24,28},{28,24},{1,5},{5... | collective-permute-start | bytes 196616 | tf_op jit(solution)/shard_map/ppermute | solution.py:22
  14.6 4.8 %collective-permute-start.6 = (bf16[128,256]{1,0:T(8,128)(2,1)S(1)}, bf16[128,256]{1,0:T(8,128)(2,1)S(1)}, u32[]{:S(2)}, u32[]{:S(2)}) collective-permute-start(bf16[128,256]{1,0:T(8,128)(2,1)S(1)} %collective-permute-done.2.refs_3_), channel_id=1, source_target_pairs={{0,4},{4,0},{8,12},{12,8},{16,20},{20,16},{24,28},{28,24},{1,5},{5... | collective-permute-start | bytes 196616 | tf_op jit(solution)/shard_map/ppermute | solution.py:22
  16.2 5.0 %collective-permute-start.9 = (bf16[256,256]{1,0:T(8,128)(2,1)S(1)}, bf16[256,256]{1,0:T(8,128)(2,1)S(1)}, u32[]{:S(2)}, u32[]{:S(2)}) collective-permute-start(bf16[256,256]{1,0:T(8,128)(2,1)S(1)} %pad_maximum_fusion.3), channel_id=1, source_target_pairs={{0,2},{1,3},{2,0},{3,1},{4,6},{5,7},{6,4},{7,5},{8,10},{9,11},{10,... | collective-permute-start | bytes 393224 | tf_op jit(solution)/shard_map/ppermute | solution.py:22
  19.8 1.5 %collective-permute-start.7 = (f32[3,128,128]{2,1,0:T(8,128)S(1)}, f32[3,128,128]{2,1,0:T(8,128)S(1)}, u32[]{:S(2)}, u32[]{:S(2)}) collective-permute-start(f32[3,128,128]{2,1,0:T(8,128)S(1)} %get-tuple-element.37), channel_id=1, source_target_pairs={{0,1},{1,0},{2,3},{3,2},{4,5},{5,4},{6,7},{7,6},{8,9},{9,8},{10,11... | collective-permute-start | bytes 589832 | tf_op jit(solution)/shard_map/ppermute | solution.py:22
  21.3 7.0 %collective-permute-start.10 = (f32[3,128,128]{2,1,0:T(8,128)S(1)}, f32[3,128,128]{2,1,0:T(8,128)S(1)}, u32[]{:S(2)}, u32[]{:S(2)}) collective-permute-start(f32[3,128,128]{2,1,0:T(8,128)S(1)} %add.54.mine_ref), channel_id=1, source_target_pairs={{0,2},{1,3},{2,0},{3,1},{4,6},{5,7},{6,4},{7,5},{8,10},{9,11},{10,... | collective-permute-start | bytes 589832 | tf_op jit(solution)/shard_map/ppermute | solution.py:22
  28.5 6.8 %collective-permute-start.13 = (f16[2,128,256]{2,1,0:T(8,128)(2,1)S(1)}, f16[2,128,256]{2,1,0:T(8,128)(2,1)S(1)}, u32[]{:S(2)}, u32[]{:S(2)}) collective-permute-start(f16[2,128,256]{2,1,0:T(8,128)(2,1)S(1)} %get-tuple-element.62), channel_id=1, source_target_pairs={{0,4},{4,0},{8,12},{12,8},{16,20},{20,16},{24,28},{28,24},{1,5},{5... | collective-permute-start | bytes 393224 | tf_op jit(solution)/shard_map/ppermute | solution.py:22
  29.6 6.5 %collective-permute-start.15 = (f16[2,128,256]{2,1,0:T(8,128)(2,1)S(1)}, f16[2,128,256]{2,1,0:T(8,128)(2,1)S(1)}, u32[]{:S(2)}, u32[]{:S(2)}) collective-permute-start(f16[2,128,256]{2,1,0:T(8,128)(2,1)S(1)} %get-tuple-element.61), channel_id=1, source_target_pairs={{0,4},{4,0},{8,12},{12,8},{16,20},{20,16},{24,28},{28,24},{1,5},{5... | collective-permute-start | bytes 393224 | tf_op jit(solution)/shard_map/ppermute | solution.py:22
  30.6 10.1 %collective-permute-start.11 = (f32[2,128,256]{2,1,0:T(8,128)S(1)}, f32[2,128,256]{2,1,0:T(8,128)S(1)}, u32[]{:S(2)}, u32[]{:S(2)}) collective-permute-start(f32[2,128,256]{2,1,0:T(8,128)S(1)} %split.20), channel_id=1, source_target_pairs={{0,1},{1,0},{2,3},{3,2},{4,5},{5,4},{6,7},{7,6},{8,9},{9,8},{10,11... | collective-permute-start | bytes 786440 | tf_op jit(solution)/shard_map/ppermute | solution.py:22
  36.2 10.4 %collective-permute-start.14 = (f16[128,256]{1,0:T(8,128)(2,1)S(1)}, f16[128,256]{1,0:T(8,128)(2,1)S(1)}, u32[]{:S(2)}, u32[]{:S(2)}) collective-permute-start(f16[128,256]{1,0:T(8,128)(2,1)S(1)} %fusion.12), channel_id=1, source_target_pairs={{0,8},{4,12},{8,0},{12,4},{16,24},{20,28},{24,16},{28,20},{1,9},{5... | collective-permute-start | bytes 196616 | tf_op jit(solution)/shard_map/ppermute | solution.py:22
  36.9 9.8 %collective-permute-start.16 = (f16[128,256]{1,0:T(8,128)(2,1)S(1)}, f16[128,256]{1,0:T(8,128)(2,1)S(1)}, u32[]{:S(2)}, u32[]{:S(2)}) collective-permute-start(f16[128,256]{1,0:T(8,128)(2,1)S(1)} %get-tuple-element.45), channel_id=1, source_target_pairs={{0,16},{4,20},{8,24},{12,28},{16,0},{20,4},{24,8},{28,12},{1,17},{... | collective-permute-start | bytes 196616 | tf_op jit(solution)/shard_map/ppermute | solution.py:22
  40.5 6.1 %collective-permute-start.17 = (f16[128,256]{1,0:T(8,128)(2,1)S(1)}, f16[128,256]{1,0:T(8,128)(2,1)S(1)}, u32[]{:S(2)}, u32[]{:S(2)}) collective-permute-start(f16[128,256]{1,0:T(8,128)(2,1)S(1)} %get-tuple-element.47), channel_id=1, source_target_pairs={{0,24},{4,28},{8,16},{12,20},{16,8},{20,12},{24,0},{28,4},{1,25},{... | collective-permute-start | bytes 196616 | tf_op jit(solution)/shard_map/ppermute | solution.py:22
  40.8 5.9 %collective-permute-start.12 = (f16[1,128,256]{2,1,0:T(8,128)(2,1)S(1)}, f16[1,128,256]{2,1,0:T(8,128)(2,1)S(1)}, u32[]{:S(2)}, u32[]{:S(2)}) collective-permute-start(f16[1,128,256]{2,1,0:T(8,128)(2,1)S(1)} %slice_convert_fusion.1), channel_id=1, source_target_pairs={{0,2},{1,3},{2,0},{3,1},{4,6},{5,7},{6,4},{7,5},{8,10},{9,11},{10,... | collective-permute-start | bytes 196616 | tf_op jit(solution)/shard_map/ppermute | solution.py:22
  47.0 18.0 %copy-start = (bf16[128,256]{1,0:T(8,128)(2,1)}, bf16[128,256]{1,0:T(8,128)(2,1)S(1)}, u32[]{:S(2)}) copy-start(bf16[128,256]{1,0:T(8,128)(2,1)S(1)} %convolution_convert_fusion.refs_0_) | copy-start | bytes 196612
  47.0 4.5 %collective-permute-start.27 = (bf16[128,256]{1,0:T(8,128)(2,1)S(1)}, bf16[128,256]{1,0:T(8,128)(2,1)S(1)}, u32[]{:S(2)}, u32[]{:S(2)}) collective-permute-start(bf16[128,256]{1,0:T(8,128)(2,1)S(1)} %convolution_convert_fusion.refs_0_), channel_id=1, source_target_pairs={{0,1},{1,0},{2,3},{3,2},{4,5},{5,4},{6,7},{7,6},{8,9},{9,8},{10,11... | collective-permute-start | bytes 196616 | tf_op jit(solution)/shard_map/ppermute | solution.py:22
  47.1 6.4 %collective-permute-start.18 = (bf16[128,256]{1,0:T(8,128)(2,1)S(1)}, bf16[128,256]{1,0:T(8,128)(2,1)S(1)}, u32[]{:S(2)}, u32[]{:S(2)}) collective-permute-start(bf16[128,256]{1,0:T(8,128)(2,1)S(1)} %convolution_convert_fusion.refs_0_), channel_id=1, source_target_pairs={{0,8},{4,12},{8,0},{12,4},{16,24},{20,28},{24,16},{28,20},{1,9},{5... | collective-permute-start | bytes 196616 | tf_op jit(solution)/shard_map/ppermute | solution.py:22
  47.6 8.0 %collective-permute-start.19 = (bf16[128,256]{1,0:T(8,128)(2,1)S(1)}, bf16[128,256]{1,0:T(8,128)(2,1)S(1)}, u32[]{:S(2)}, u32[]{:S(2)}) collective-permute-start(bf16[128,256]{1,0:T(8,128)(2,1)S(1)} %convolution_convert_fusion.refs_0_), channel_id=1, source_target_pairs={{0,16},{4,20},{8,24},{12,28},{16,0},{20,4},{24,8},{28,12},{1,17},{... | collective-permute-start | bytes 196616 | tf_op jit(solution)/shard_map/ppermute | solution.py:22
  51.3 6.1 %collective-permute-start.20 = (bf16[128,256]{1,0:T(8,128)(2,1)S(1)}, bf16[128,256]{1,0:T(8,128)(2,1)S(1)}, u32[]{:S(2)}, u32[]{:S(2)}) collective-permute-start(bf16[128,256]{1,0:T(8,128)(2,1)S(1)} %convolution_convert_fusion.refs_0_), channel_id=1, source_target_pairs={{0,24},{4,28},{8,16},{12,20},{16,8},{20,12},{24,0},{28,4},{1,25},{... | collective-permute-start | bytes 196616 | tf_op jit(solution)/shard_map/ppermute | solution.py:22
  51.5 10.6 %collective-permute-start.28 = (bf16[256,256]{1,0:T(8,128)(2,1)S(1)}, bf16[256,256]{1,0:T(8,128)(2,1)S(1)}, u32[]{:S(2)}, u32[]{:S(2)}) collective-permute-start(bf16[256,256]{1,0:T(8,128)(2,1)S(1)} %pad_maximum_fusion.4), channel_id=1, source_target_pairs={{0,2},{1,3},{2,0},{3,1},{4,6},{5,7},{6,4},{7,5},{8,10},{9,11},{10,... | collective-permute-start | bytes 393224 | tf_op jit(solution)/shard_map/ppermute | solution.py:22
  53.0 4.9 %collective-permute-start.21 = (bf16[128,256]{1,0:T(8,128)(2,1)S(1)}, bf16[128,256]{1,0:T(8,128)(2,1)S(1)}, u32[]{:S(2)}, u32[]{:S(2)}) collective-permute-start(bf16[128,256]{1,0:T(8,128)(2,1)S(1)} %convolution_convert_fusion.refs_0_), channel_id=1, source_target_pairs={{0,4},{4,0},{8,12},{12,8},{16,20},{20,16},{24,28},{28,24},{1,5},{5... | collective-permute-start | bytes 196616 | tf_op jit(solution)/shard_map/ppermute | solution.py:22
  53.5 5.0 %collective-permute-start.22 = (bf16[128,256]{1,0:T(8,128)(2,1)S(1)}, bf16[128,256]{1,0:T(8,128)(2,1)S(1)}, u32[]{:S(2)}, u32[]{:S(2)}) collective-permute-start(bf16[128,256]{1,0:T(8,128)(2,1)S(1)} %collective-permute-done.18.refs_1_), channel_id=1, source_target_pairs={{0,4},{4,0},{8,12},{12,8},{16,20},{20,16},{24,28},{28,24},{1,5},{5... | collective-permute-start | bytes 196616 | tf_op jit(solution)/shard_map/ppermute | solution.py:22
  55.5 4.7 %collective-permute-start.23 = (bf16[128,256]{1,0:T(8,128)(2,1)S(1)}, bf16[128,256]{1,0:T(8,128)(2,1)S(1)}, u32[]{:S(2)}, u32[]{:S(2)}) collective-permute-start(bf16[128,256]{1,0:T(8,128)(2,1)S(1)} %collective-permute-done.19.refs_2_), channel_id=1, source_target_pairs={{0,4},{4,0},{8,12},{12,8},{16,20},{20,16},{24,28},{28,24},{1,5},{5... | collective-permute-start | bytes 196616 | tf_op jit(solution)/shard_map/ppermute | solution.py:22
  57.4 4.3 %collective-permute-start.24 = (bf16[128,256]{1,0:T(8,128)(2,1)S(1)}, bf16[128,256]{1,0:T(8,128)(2,1)S(1)}, u32[]{:S(2)}, u32[]{:S(2)}) collective-permute-start(bf16[128,256]{1,0:T(8,128)(2,1)S(1)} %collective-permute-done.20.refs_3_), channel_id=1, source_target_pairs={{0,4},{4,0},{8,12},{12,8},{16,20},{20,16},{24,28},{28,24},{1,5},{5... | collective-permute-start | bytes 196616 | tf_op jit(solution)/shard_map/ppermute | solution.py:22
  62.1 2.9 %collective-permute-start.25 = (f32[3,128,128]{2,1,0:T(8,128)S(1)}, f32[3,128,128]{2,1,0:T(8,128)S(1)}, u32[]{:S(2)}, u32[]{:S(2)}) collective-permute-start(f32[3,128,128]{2,1,0:T(8,128)S(1)} %get-tuple-element.48), channel_id=1, source_target_pairs={{0,1},{1,0},{2,3},{3,2},{4,5},{5,4},{6,7},{7,6},{8,9},{9,8},{10,11... | collective-permute-start | bytes 589832 | tf_op jit(solution)/shard_map/ppermute | solution.py:22
  65.1 2.1 %collective-permute-start.29 = (f32[2,2,128,256]{3,2,1,0:T(8,128)S(1)}, f32[2,2,128,256]{3,2,1,0:T(8,128)S(1)}, u32[]{:S(2)}, u32[]{:S(2)}) collective-permute-start(f32[2,2,128,256]{3,2,1,0:T(8,128)S(1)} %split.24), channel_id=1, source_target_pairs={{0,1},{1,0},{2,3},{3,2},{4,5},{5,4},{6,7},{7,6},{8,9},{9,8},{10,11... | collective-permute-start | bytes 1572872 | tf_op jit(solution)/shard_map/ppermute | solution.py:22
  65.6 7.8 %collective-permute-start.26 = (f32[3,128,128]{2,1,0:T(8,128)S(1)}, f32[3,128,128]{2,1,0:T(8,128)S(1)}, u32[]{:S(2)}, u32[]{:S(2)}) collective-permute-start(f32[3,128,128]{2,1,0:T(8,128)S(1)} %add.64.mine_ref), channel_id=1, source_target_pairs={{0,2},{1,3},{2,0},{3,1},{4,6},{5,7},{6,4},{7,5},{8,10},{9,11},{10,... | collective-permute-start | bytes 589832 | tf_op jit(solution)/shard_map/ppermute | solution.py:22
  67.2 6.2 %collective-permute-start.30 = (f32[128,256]{1,0:T(8,128)S(1)}, f32[128,256]{1,0:T(8,128)S(1)}, u32[]{:S(2)}, u32[]{:S(2)}) collective-permute-start(f32[128,256]{1,0:T(8,128)S(1)} %get-tuple-element.60), channel_id=1, source_target_pairs={{0,4},{4,0},{8,12},{12,8},{16,20},{20,16},{24,28},{28,24},{1,5},{5... | collective-permute-start | bytes 393224 | tf_op jit(solution)/shard_map/ppermute | solution.py:22
  67.8 8.3 %collective-permute-start.31 = (f32[128,256]{1,0:T(8,128)S(1)}, f32[128,256]{1,0:T(8,128)S(1)}, u32[]{:S(2)}, u32[]{:S(2)}) collective-permute-start(f32[128,256]{1,0:T(8,128)S(1)} %get-tuple-element.58), channel_id=1, source_target_pairs={{0,2},{1,3},{2,0},{3,1},{4,6},{5,7},{6,4},{7,5},{8,10},{9,11},{10,... | collective-permute-start | bytes 393224 | tf_op jit(solution)/shard_map/ppermute | solution.py:22
  68.3 9.7 %collective-permute-start.32 = (f32[128,256]{1,0:T(8,128)S(1)}, f32[128,256]{1,0:T(8,128)S(1)}, u32[]{:S(2)}, u32[]{:S(2)}) collective-permute-start(f32[128,256]{1,0:T(8,128)S(1)} %get-tuple-element.59), channel_id=1, source_target_pairs={{0,6},{1,7},{2,4},{3,5},{4,2},{5,3},{6,0},{7,1},{8,14},{9,15},{10,... | collective-permute-start | bytes 393224 | tf_op jit(solution)/shard_map/ppermute | solution.py:33
  78.1 7.7 %collective-permute-start.33 = (f16[128,256]{1,0:T(8,128)(2,1)S(1)}, f16[128,256]{1,0:T(8,128)(2,1)S(1)}, u32[]{:S(2)}, u32[]{:S(2)}) collective-permute-start(f16[128,256]{1,0:T(8,128)(2,1)S(1)} %fusion.2), channel_id=1, source_target_pairs={{0,8},{4,12},{8,0},{12,4},{16,24},{20,28},{24,16},{28,20},{1,9},{5... | collective-permute-start | bytes 196616 | tf_op jit(solution)/shard_map/ppermute | solution.py:22
  79.2 7.0 %collective-permute-start.34 = (f16[128,256]{1,0:T(8,128)(2,1)S(1)}, f16[128,256]{1,0:T(8,128)(2,1)S(1)}, u32[]{:S(2)}, u32[]{:S(2)}) collective-permute-start(f16[128,256]{1,0:T(8,128)(2,1)S(1)} %fusion.2), channel_id=1, source_target_pairs={{0,16},{4,20},{8,24},{12,28},{16,0},{20,4},{24,8},{28,12},{1,17},{... | collective-permute-start | bytes 196616 | tf_op jit(solution)/shard_map/ppermute | solution.py:22
  82.2 6.1 %collective-permute-start.35 = (f16[128,256]{1,0:T(8,128)(2,1)S(1)}, f16[128,256]{1,0:T(8,128)(2,1)S(1)}, u32[]{:S(2)}, u32[]{:S(2)}) collective-permute-start(f16[128,256]{1,0:T(8,128)(2,1)S(1)} %fusion.2), channel_id=1, source_target_pairs={{0,24},{4,28},{8,16},{12,20},{16,8},{20,12},{24,0},{28,4},{1,25},{... | collective-permute-start | bytes 196616 | tf_op jit(solution)/shard_map/ppermute | solution.py:22
  88.4 4.3 %collective-permute-start.36 = (f16[128,256]{1,0:T(8,128)(2,1)S(1)}, f16[128,256]{1,0:T(8,128)(2,1)S(1)}, u32[]{:S(2)}, u32[]{:S(2)}) collective-permute-start(f16[128,256]{1,0:T(8,128)(2,1)S(1)} %add_convert_fusion.1), channel_id=1, source_target_pairs={{0,4},{4,0},{8,12},{12,8},{16,20},{20,16},{24,28},{28,24},{1,5},{5... | collective-permute-start | bytes 196616 | tf_op jit(solution)/shard_map/ppermute | solution.py:22
  89.1 6.6 %collective-permute-start.37 = (f16[128,256]{1,0:T(8,128)(2,1)S(1)}, f16[128,256]{1,0:T(8,128)(2,1)S(1)}, u32[]{:S(2)}, u32[]{:S(2)}) collective-permute-start(f16[128,256]{1,0:T(8,128)(2,1)S(1)} %add_convert_fusion.1), channel_id=1, source_target_pairs={{0,2},{1,3},{2,0},{3,1},{4,6},{5,7},{6,4},{7,5},{8,10},{9,11},{10,... | collective-permute-start | bytes 196616 | tf_op jit(solution)/shard_map/ppermute | solution.py:22
  89.7 6.0 %collective-permute-start.38 = (f16[128,256]{1,0:T(8,128)(2,1)S(1)}, f16[128,256]{1,0:T(8,128)(2,1)S(1)}, u32[]{:S(2)}, u32[]{:S(2)}) collective-permute-start(f16[128,256]{1,0:T(8,128)(2,1)S(1)} %add_convert_fusion.1), channel_id=1, source_target_pairs={{0,6},{1,7},{2,4},{3,5},{4,2},{5,3},{6,0},{7,1},{8,14},{9,15},{10,... | collective-permute-start | bytes 196616 | tf_op jit(solution)/shard_map/ppermute | solution.py:33
  95.8 1.6 %collective-permute-start.39 = (f16[2,2,128,256]{3,2,1,0:T(8,128)(2,1)S(1)}, f16[2,2,128,256]{3,2,1,0:T(8,128)(2,1)S(1)}, u32[]{:S(2)}, u32[]{:S(2)}) collective-permute-start(f16[2,2,128,256]{3,2,1,0:T(8,128)(2,1)S(1)} %pad_maximum_fusion.2), channel_id=1, source_target_pairs={{0,1},{1,0},{2,3},{3,2},{4,5},{5,4},{6,7},{7,6},{8,9},{9,8},{10,11... | collective-permute-start | bytes 786440 | tf_op jit(solution)/shard_map/ppermute | solution.py:22

commit v3 on v2

--- a/solution.py
+++ b/solution.py
@@ -8,9 +8,9 @@
 from jax.sharding import PartitionSpec as P
 
 ridge_weight = 0.1
-value_bound = 160.0
 product_bound = 672.0
 f16_top = 30000.0
+extra_rows = 16
 
 
 def params():
@@ -411,26 +411,72 @@
     out_ref[...] = dot(left, right, ((0,), (0,))) / scale_ref[...]
 
 
-def scale_kernel(mine_ref, other_ref, scale_ref, back_ref, *, bound):
-    largest = jnp.max(mine_ref[...] + other_ref[...], axis=0)
-    largest = jnp.max(jnp.max(largest, axis=0, keepdims=True), axis=1, keepdims=True)
-    scale = f16_top / (bound * jnp.broadcast_to(largest, scale_ref.shape) + 1e-30)
-    scale_ref[...] = scale
-    back_ref[...] = 1.0 / scale
-
-
-def core_scale(pair, rank, bound):
-    vmem = pl.BlockSpec(memory_space=pltpu.VMEM)
-    vector = jax.ShapeDtypeStruct((1, rank), jnp.float32)
+def power_of_two(exponent):
+    left = jnp.abs(exponent)
+    result = jnp.ones_like(exponent)
+    for b in reversed(range(7)):
+        taken = left >= float(1 << b)
+        step = jnp.where(exponent < 0.0, 0.5 ** (1 << b), 2.0 ** (1 << b))
+        result = jnp.where(taken, result * step, result)
+        left = jnp.where(taken, left - float(1 << b), left)
+    return result
+
+
+def packed_block(x):
+    top = jnp.maximum(jnp.max(jnp.abs(x), axis=0, keepdims=True), 1e-30)
+    exponent = jnp.clip(jnp.ceil(jnp.log2(top)), -100.0, 126.0)
+    exponents = jnp.broadcast_to(exponent, (extra_rows, x.shape[1]))
+    return jnp.concatenate([x * power_of_two(-exponent), exponents], axis=0)
+
+
+def unpacked_block(x):
+    height = x.shape[0] - extra_rows
+    return x[:height] * power_of_two(x[height:height + 1])
+
+
+def plane_kernel(keep_ref, other_ref, own_ref, packed_ref):
+    own_ref[...] = keep_ref[0, 0] + other_ref[0, 0]
+    for i in range(packed_ref.shape[0]):
+        p, h = (i + 1) // 2, (i + 1) % 2
+        packed_ref[i] = packed_block(keep_ref[p, h] + other_ref[p, h])
+
+
+def pack_plane(keep, other):
+    pieces, _, height, rank = keep.shape
+    vmem = pl.BlockSpec(memory_space=pltpu.VMEM)
     return pl.pallas_call(
-        functools.partial(scale_kernel, bound=bound),
-        out_shape=(vector, vector),
+        plane_kernel,
+        out_shape=(
+            jax.ShapeDtypeStruct((height, rank), jnp.float32),
+            jax.ShapeDtypeStruct((2 * pieces - 1, height + extra_rows, rank), jnp.float32),
+        ),
         in_specs=[vmem, vmem],
         out_specs=(vmem, vmem),
         compiler_params=params(),
+        cost_estimate=cost(0.6),
+        name="pack_plane",
+    )(keep, other)
+
+
+def merge_kernel(*refs, plain):
+    parts = [ref[...] for ref in refs[:plain]]
+    parts += [unpacked_block(ref[...]) for ref in refs[plain:-1]]
+    refs[-1][...] = packed_block(tree_sum(parts))
+
+
+def merge(plain, packed):
+    args = list(plain) + [x.astype(jnp.float32) for x in packed]
+    vmem = pl.BlockSpec(memory_space=pltpu.VMEM)
+    merged = pl.pallas_call(
+        functools.partial(merge_kernel, plain=len(plain)),
+        out_shape=jax.ShapeDtypeStruct(args[-1].shape, jnp.float32),
+        in_specs=[vmem] * len(args),
+        out_specs=vmem,
+        compiler_params=params(),
         cost_estimate=cost(0.5),
-        name="core_scale",
-    )(*pair)
+        name="merge",
+    )(*args)
+    return lax.optimization_barrier(merged.astype(jnp.float16))
 
 
 def begin_kernel(mine_ref, other_ref, out_ref):
@@ -477,7 +523,7 @@
     return left, right
 
 
-def whiten_kernel(z_ref, factor_ref, near_ref, far_ref, out_ref, core_ref, *, bits_c):
+def whiten_kernel(z_ref, near_ref, far_ref, out_ref, core_ref, *, bits_c):
     relations, halves = out_ref.shape[0], near_ref.shape[0]
     pieces = 2 * halves // relations
     my_col = lax.axis_index("cols")
@@ -489,20 +535,20 @@
         parts = []
         for p in range(pieces):
             place = reversed_slot((k * pieces + p) ^ my_col, bits_c)
-            parts += [core_ref[place, h ^ (my_row & 1)] for h in range(2)]
-        core = jnp.concatenate(parts, axis=0) * factor_ref[...]
+            parts += [unpacked_block(core_ref[place, h ^ (my_row & 1)]) for h in range(2)]
+        core = jnp.concatenate(parts, axis=0)
         out_ref[k] = whitened(left, right, core)
 
 
-def half_whiten_kernel(z_ref, factor_ref, core_ref, *refs, bits_c):
+def half_whiten_kernel(z_ref, core_ref, *refs, bits_c):
     out_ref = refs[-1]
     my_col = lax.axis_index("cols")
     my_row = lax.axis_index("rows")
     left, right = whiten_parts(z_ref)
     for p in range(core_ref.shape[0]):
         slot = 2 * reversed_slot(p, bits_c - 1)
-        parts = [core_ref[p, h ^ (my_row & 1)] for h in range(2)]
-        core = jnp.concatenate(parts, axis=0) * factor_ref[...]
+        parts = [unpacked_block(core_ref[p, h ^ (my_row & 1)]) for h in range(2)]
+        core = jnp.concatenate(parts, axis=0)
         result = whitened(left, right, core)
         if len(refs) == 1:
             out_ref[p] = result
@@ -511,7 +557,7 @@
             out_ref[(slot + 1) ^ my_col] = result
 
 
-def whiten(z, factor, near, far, relations):
+def whiten(z, near, far, relations):
     rank = z.shape[0]
     halves = near.shape[0]
     vmem = pl.BlockSpec(memory_space=pltpu.VMEM)
@@ -520,13 +566,13 @@
         return pl.pallas_call(
             functools.partial(kernel, bits_c=bits_of("cols")),
             out_shape=jax.ShapeDtypeStruct((count, rank, rank), jnp.float32),
-            in_specs=[vmem] * (2 + len(args)),
+            in_specs=[vmem] * (1 + len(args)),
             out_specs=vmem,
             scratch_shapes=scratch,
             compiler_params=params(),
             cost_estimate=cost(microseconds),
             name="whiten",
-        )(z, factor, *args)
+        )(z, *args)
 
     if 2 * halves != relations:
         scratch = [pltpu.VMEM((2 * halves,) + near.shape[1:], jnp.float32)]
@@ -575,22 +621,18 @@
     gram_pair = pair_of_sums(gram_new)
     core = second_pass(places, tiles, factors_new, panel_new)
     keep, give = jnp.split(after(core, gram_pair[0]), 2, axis=0)
-    core = keep + swap(give, "cols", 1)
     bits = bits_of("cols")
     slots_left = [2 * reversed_slot(p, bits - 1) for p in range(n_cols // 2)]
     plane = [(h, p) for p in range(n_cols // 2) for h in range(2) if (h, p) != (0, 0)]
-    core = core[0, 0] + functools.reduce(
-        jnp.add, [swap_both(core[p, h], h, slots_left[p]) for h, p in plane]
-    )
-    bound = 2.0 * slots * tile * value_bound * n_rows * n_cols
-    scale_core, unit_core = core_scale(gram_pair, rank, bound)
+    core, packed = pack_plane(keep, swap(give, "cols", 1))
+    packed = packed.astype(jnp.float16)
+    core = merge(
+        [core],
+        [swap_both(packed[i], h, slots_left[p]) for i, (h, p) in enumerate(plane)],
+    )
     z = square_call(begin_kernel, "begin", 3.3, rank, *gram_pair)
-    packed = (core * scale_core).astype(jnp.float16)
-    core = tree_sum(
-        [packed.astype(jnp.float32)]
-        + [swap(packed, "rows", 2 * i).astype(jnp.float32) for i in range(1, half)]
-    )
-    core = after(core.astype(jnp.float16), z)
+    core = merge([], [core] + [swap(core, "rows", 2 * i) for i in range(1, half)])
+    core = after(core, z)
     found = {(h, p): swap_both(core, h, slots_left[p]) for h, p in plane}
     z = square_call(end_kernel, "end", 2.9, rank, after(z, found[plane[0]]))
     found[(0, 0)] = core
@@ -599,9 +641,7 @@
     )
     near = after(near, z)
     far = swap(near, "cols", 1)
-    cores_new = whiten(
-        z, unit_core, near.astype(jnp.float32), far.astype(jnp.float32), relations
-    )
+    cores_new = whiten(z, near.astype(jnp.float32), far.astype(jnp.float32), relations)
     return (factor_new, cores_new)
 
 

time: 99.4 us -> 97.5 us (0.981)
  waiting for transfers between devices: 22.8 us -> 20.7 us
    ppermute x2, waiting for transfers between devices: 1.88 us -> 0.71 us  [swap_both(): lax.ppermute(x, ('rows', 'cols'), [(i, i ^ mask) for i in range(size)])]
where the time goes in v3:
time: 97.5 us; the launch traced here: 97.3 us
  starting transfers between devices  44.1 us (45%)
  Pallas kernels  29.4 us (30%)
  waiting for transfers between devices  20.7 us (21%)
  between operations  1.08 us (1%)
    ppermute x38, starting transfers between devices, swap(): return lax.ppermute(x, axis, [(i, i ^ mask) for i in range(size)])  39.5 us
    ppermute x38, waiting for transfers between devices, swap(): return lax.ppermute(x, axis, [(i, i ^ mask) for i in range(size)])  20 us
    pallas_call x4, Pallas kernels, square_call(): pl.pallas_call(kernel, out_shape=jax.ShapeDtypeStruct((rank, rank), jnp.f...  15.1 us
    pallas_call x1, Pallas kernels, first_pass(): pl.pallas_call(functools.partial(first_kernel, bits_c=bits_of('cols')), o...  4.84 us
    ppermute x2, starting transfers between devices, swap_both(): lax.ppermute(x, ('rows', 'cols'), [(i, i ^ mask) for i in range(size)])  4.61 us
    pallas_call x1, Pallas kernels, prepare(): pl.pallas_call(functools.partial(prepare_kernel, half=n_rows // 2, terms=...  3 us
    pallas_call x1, Pallas kernels, second_pass(): pl.pallas_call(functools.partial(second_kernel, bits_c=bits_of('cols')),...  2.76 us
    pallas_call x2, Pallas kernels, call(): pl.pallas_call(functools.partial(kernel, bits_c=bits_of('cols')), out_sha...  2.64 us
  transfers between devices with their start and end apart: 40, of which 20 were waited for; matrix products, arithmetic and copies ran while one was open for 1% of the time, Pallas kernels for 28%

profile of v3, /device:TPU:0, one launch (start us, length us, event | category | flops | bytes accessed | tf_op | source)
XLA Modules:
  0.0 97.3 jit_solution(4781476399457278145)
XLA Ops:
  0.6 3.1 %collective-permute-start = (bf16[128,256]{1,0:T(8,128)(2,1)}, bf16[128,256]{1,0:T(8,128)(2,1)S(1)}, u32[]{:S(2)}, u32[]{:S(2)}) collective-permute-start(bf16[128,256]{1,0:T(8,128)(2,1)} %factor_hbm.1), channel_id=1, source_target_pairs={{0,8},{4,12},{8,0},{12,4},{16,24},{20,28},{24,16},{28,20},{1,9},{5... | collective-permute-start | bytes 196616 | tf_op jit(solution)/shard_map/ppermute | solution.py:22
  3.7 2.6 %collective-permute-start.1 = (bf16[128,256]{1,0:T(8,128)(2,1)}, bf16[128,256]{1,0:T(8,128)(2,1)S(1)}, u32[]{:S(2)}, u32[]{:S(2)}) collective-permute-start(bf16[128,256]{1,0:T(8,128)(2,1)} %factor_hbm.1), channel_id=1, source_target_pairs={{0,16},{4,20},{8,24},{12,28},{16,0},{20,4},{24,8},{28,12},{1,17},{... | collective-permute-start | bytes 196616 | tf_op jit(solution)/shard_map/ppermute | solution.py:22
  6.3 1.7 %collective-permute-start.3 = (bf16[128,256]{1,0:T(8,128)(2,1)}, bf16[128,256]{1,0:T(8,128)(2,1)S(1)}, u32[]{:S(2)}, u32[]{:S(2)}) collective-permute-start(bf16[128,256]{1,0:T(8,128)(2,1)} %factor_hbm.1), channel_id=1, source_target_pairs={{0,4},{4,0},{8,12},{12,8},{16,20},{20,16},{24,28},{28,24},{1,5},{5... | collective-permute-start | bytes 196616 | tf_op jit(solution)/shard_map/ppermute | solution.py:22
  8.1 0.7 copy.8.counts_ref
  8.8 3.0 %prepare.1 = (s32[4,24]{1,0:T(4,128)S(1)}, f32[1,256]{1,0:T(1,128)S(1)}, bf16[4,12,128,128]{3,2,1,0:T(8,128)(2,1)S(1)}, bf16[4,256,256]{2,1,0:T(8,128)(2,1)S(1)}, bf16[128,256]{1,0:T(8,128)(2,1)S(1)}) custom-call(s32[4,1,12]{2,1,0:T(1,128)} %rows_hbm.1, s32[4,1,12]{2,1,0:T(1,128)} %cols_hbm.1, s32[4,1,1]{2,1,0:T(1,128)S(1)} %copy.8.counts_ref, ...), custom_call_target="tpu_custom_call" | custom-call | flops 2200000000 | bytes 100000 | tf_op jit(solution)/shard_map/prepare/pallas_call | solution.py:179
  11.8 0.8 collective-permute-done.2.refs_3_
  12.6 1.5 %collective-permute-start.4 = (bf16[128,256]{1,0:T(8,128)(2,1)S(1)}, bf16[128,256]{1,0:T(8,128)(2,1)S(1)}, u32[]{:S(2)}, u32[]{:S(2)}) collective-permute-start(bf16[128,256]{1,0:T(8,128)(2,1)S(1)} %collective-permute-done.refs_1_), channel_id=1, source_target_pairs={{0,4},{4,0},{8,12},{12,8},{16,20},{20,16},{24,28},{28,24},{1,5},{5... | collective-permute-start | bytes 196616 | tf_op jit(solution)/shard_map/ppermute | solution.py:22
  14.6 1.5 %collective-permute-start.6 = (bf16[128,256]{1,0:T(8,128)(2,1)S(1)}, bf16[128,256]{1,0:T(8,128)(2,1)S(1)}, u32[]{:S(2)}, u32[]{:S(2)}) collective-permute-start(bf16[128,256]{1,0:T(8,128)(2,1)S(1)} %collective-permute-done.2.refs_3_), channel_id=1, source_target_pairs={{0,4},{4,0},{8,12},{12,8},{16,20},{20,16},{24,28},{28,24},{1,5},{5... | collective-permute-start | bytes 196616 | tf_op jit(solution)/shard_map/ppermute | solution.py:22
  16.2 1.6 %collective-permute-start.9 = (bf16[256,256]{1,0:T(8,128)(2,1)S(1)}, bf16[256,256]{1,0:T(8,128)(2,1)S(1)}, u32[]{:S(2)}, u32[]{:S(2)}) collective-permute-start(bf16[256,256]{1,0:T(8,128)(2,1)S(1)} %pad_maximum_fusion.3), channel_id=1, source_target_pairs={{0,2},{1,3},{2,0},{3,1},{4,6},{5,7},{6,4},{7,5},{8,10},{9,11},{10,... | collective-permute-start | bytes 393224 | tf_op jit(solution)/shard_map/ppermute | solution.py:22
  17.7 1.0 collective-permute-done.5.refs_6_
  18.7 0.7 collective-permute-done.6.refs_7_
  19.9 1.3 %collective-permute-done.9 = bf16[256,256]{1,0:T(8,128)(2,1)S(1)} collective-permute-done((bf16[256,256]{1,0:T(8,128)(2,1)S(1)}, bf16[256,256]{1,0:T(8,128)(2,1)S(1)}, u32[]{:S(2)}, u32[]{:S(2)}) %collective-permute-start.9) | collective-permute-done | bytes 131104 | tf_op jit(solution)/shard_map/ppermute | solution.py:22
  21.3 1.5 %collective-permute-start.10 = (f32[3,128,128]{2,1,0:T(8,128)S(1)}, f32[3,128,128]{2,1,0:T(8,128)S(1)}, u32[]{:S(2)}, u32[]{:S(2)}) collective-permute-start(f32[3,128,128]{2,1,0:T(8,128)S(1)} %add.33.mine_ref), channel_id=1, source_target_pairs={{0,2},{1,3},{2,0},{3,1},{4,6},{5,7},{6,4},{7,5},{8,10},{9,11},{10,... | collective-permute-start | bytes 589832 | tf_op jit(solution)/shard_map/ppermute | solution.py:22
  22.9 4.8 %first_pass.1 = (f32[4,128,256]{2,1,0:T(8,128)S(1)}, f32[8,128,256]{2,1,0:T(8,128)S(1)}) custom-call(s32[4,24]{1,0:T(4,128)S(1)} %get-tuple-element.29.places_ref, f32[1,256]{1,0:T(1,128)S(1)} %get-tuple-element.30.scale_ref, bf16[4,12,128,128]{3,2,1,0:T(8,128)(2,1)S(1)} %get-tuple-element.31.tiles_ref, bf16[8,128,256]{2,1,0:T(8,128)(2,1)S(1)} %bitcast.28, ...), custom_call_target="tpu_custom_call" | custom-call | flops 5280000000 | bytes 100000 | tf_op jit(solution)/shard_map/first_pass/pallas_call | solution.py:242
  27.7 0.6 collective-permute-done.10.other_ref
  28.5 1.1 %collective-permute-start.13 = (f16[2,128,256]{2,1,0:T(8,128)(2,1)S(1)}, f16[2,128,256]{2,1,0:T(8,128)(2,1)S(1)}, u32[]{:S(2)}, u32[]{:S(2)}) collective-permute-start(f16[2,128,256]{2,1,0:T(8,128)(2,1)S(1)} %get-tuple-element.61), channel_id=1, source_target_pairs={{0,4},{4,0},{8,12},{12,8},{16,20},{20,16},{24,28},{28,24},{1,5},{5... | collective-permute-start | bytes 393224 | tf_op jit(solution)/shard_map/ppermute | solution.py:22
  29.6 1.0 %collective-permute-start.15 = (f16[2,128,256]{2,1,0:T(8,128)(2,1)S(1)}, f16[2,128,256]{2,1,0:T(8,128)(2,1)S(1)}, u32[]{:S(2)}, u32[]{:S(2)}) collective-permute-start(f16[2,128,256]{2,1,0:T(8,128)(2,1)S(1)} %get-tuple-element.60), channel_id=1, source_target_pairs={{0,4},{4,0},{8,12},{12,8},{16,20},{20,16},{24,28},{28,24},{1,5},{5... | collective-permute-start | bytes 393224 | tf_op jit(solution)/shard_map/ppermute | solution.py:22
  30.7 4.6 %system.1.in_ref = f32[256,256]{1,0:T(8,128)S(1)} custom-call(f32[3,128,128]{2,1,0:T(8,128)S(1)} %add.33.mine_ref, f32[3,128,128]{2,1,0:T(8,128)S(1)} %collective-permute-done.10.other_ref, bf16[4,256,256]{2,1,0:T(8,128)(2,1)S(1)} %get-tuple-element.39.cores_ref), custom_call_target="tpu_custom_call" | custom-call | flops 4180000000 | bytes 100000 | tf_op jit(solution)/shard_map/system/pallas_call | solution.py:500
  35.3 0.8 collective-permute-done.15
  36.2 0.8 collective-permute-start.14
  36.9 3.5 %collective-permute-start.16 = (f16[128,256]{1,0:T(8,128)(2,1)S(1)}, f16[128,256]{1,0:T(8,128)(2,1)S(1)}, u32[]{:S(2)}, u32[]{:S(2)}) collective-permute-start(f16[128,256]{1,0:T(8,128)(2,1)S(1)} %get-tuple-element.45), channel_id=1, source_target_pairs={{0,16},{4,20},{8,24},{12,28},{16,0},{20,4},{24,8},{28,12},{1,17},{... | collective-permute-start | bytes 196616 | tf_op jit(solution)/shard_map/ppermute | solution.py:22
  40.8 1.5 %collective-permute-start.12 = (f16[1,128,256]{2,1,0:T(8,128)(2,1)S(1)}, f16[1,128,256]{2,1,0:T(8,128)(2,1)S(1)}, u32[]{:S(2)}, u32[]{:S(2)}) collective-permute-start(f16[1,128,256]{2,1,0:T(8,128)(2,1)S(1)} %slice_convert_fusion.1), channel_id=1, source_target_pairs={{0,2},{1,3},{2,0},{3,1},{4,6},{5,7},{6,4},{7,5},{8,10},{9,11},{10,... | collective-permute-start | bytes 196616 | tf_op jit(solution)/shard_map/ppermute | solution.py:22
  42.3 4.3 %inverse.1 = f32[256,256]{1,0:T(8,128)S(1)} custom-call(f32[256,256]{1,0:T(8,128)S(1)} %system.1.in_ref, f32[1,256]{1,0:T(1,128)S(1)} %get-tuple-element.30.scale_ref), custom_call_target="tpu_custom_call" | custom-call | flops 5720000000 | bytes 100000 | tf_op jit(solution)/shard_map/inverse/pallas_call | solution.py:500
  47.6 3.7 %collective-permute-start.19 = (bf16[128,256]{1,0:T(8,128)(2,1)S(1)}, bf16[128,256]{1,0:T(8,128)(2,1)S(1)}, u32[]{:S(2)}, u32[]{:S(2)}) collective-permute-start(bf16[128,256]{1,0:T(8,128)(2,1)S(1)} %convolution_convert_fusion.refs_0_), channel_id=1, source_target_pairs={{0,16},{4,20},{8,24},{12,28},{16,0},{20,4},{24,8},{28,12},{1,17},{... | collective-permute-start | bytes 196616 | tf_op jit(solution)/shard_map/ppermute | solution.py:22
  51.5 1.5 %collective-permute-start.28 = (bf16[256,256]{1,0:T(8,128)(2,1)S(1)}, bf16[256,256]{1,0:T(8,128)(2,1)S(1)}, u32[]{:S(2)}, u32[]{:S(2)}) collective-permute-start(bf16[256,256]{1,0:T(8,128)(2,1)S(1)} %pad_maximum_fusion.4), channel_id=1, source_target_pairs={{0,2},{1,3},{2,0},{3,1},{4,6},{5,7},{6,4},{7,5},{8,10},{9,11},{10,... | collective-permute-start | bytes 393224 | tf_op jit(solution)/shard_map/ppermute | solution.py:22
  53.5 1.5 %collective-permute-start.22 = (bf16[128,256]{1,0:T(8,128)(2,1)S(1)}, bf16[128,256]{1,0:T(8,128)(2,1)S(1)}, u32[]{:S(2)}, u32[]{:S(2)}) collective-permute-start(bf16[128,256]{1,0:T(8,128)(2,1)S(1)} %collective-permute-done.18.refs_1_), channel_id=1, source_target_pairs={{0,4},{4,0},{8,12},{12,8},{16,20},{20,16},{24,28},{28,24},{1,5},{5... | collective-permute-start | bytes 196616 | tf_op jit(solution)/shard_map/ppermute | solution.py:22
  56.0 1.4 %collective-permute-done.20.refs_3_ = bf16[128,256]{1,0:T(8,128)(2,1)S(1)} collective-permute-done((bf16[128,256]{1,0:T(8,128)(2,1)S(1)}, bf16[128,256]{1,0:T(8,128)(2,1)S(1)}, u32[]{:S(2)}, u32[]{:S(2)}) %collective-permute-start.20) | collective-permute-done | bytes 65568 | tf_op jit(solution)/shard_map/ppermute | solution.py:22
  58.5 1.7 %collective-permute-done.23.refs_6_ = bf16[128,256]{1,0:T(8,128)(2,1)S(1)} collective-permute-done((bf16[128,256]{1,0:T(8,128)(2,1)S(1)}, bf16[128,256]{1,0:T(8,128)(2,1)S(1)}, u32[]{:S(2)}, u32[]{:S(2)}) %collective-permute-start.23) | collective-permute-done | bytes 65568 | tf_op jit(solution)/shard_map/ppermute | solution.py:22
  60.2 1.5 %collective-permute-done.24.refs_7_ = bf16[128,256]{1,0:T(8,128)(2,1)S(1)} collective-permute-done((bf16[128,256]{1,0:T(8,128)(2,1)S(1)}, bf16[128,256]{1,0:T(8,128)(2,1)S(1)}, u32[]{:S(2)}, u32[]{:S(2)}) %collective-permute-start.24) | collective-permute-done | bytes 65568 | tf_op jit(solution)/shard_map/ppermute | solution.py:22
  62.2 2.8 %second_pass.1 = f32[4,2,128,256]{3,2,1,0:T(8,128)S(1)} custom-call(s32[4,24]{1,0:T(4,128)S(1)} %get-tuple-element.29.places_ref, bf16[4,12,128,128]{3,2,1,0:T(8,128)(2,1)S(1)} %get-tuple-element.31.tiles_ref, bf16[8,128,256]{2,1,0:T(8,128)(2,1)S(1)} %bitcast.29, bf16[512,256]{1,0:T(8,128)(2,1)S(1)} %pad_maximum_fusion.2.panel_ref), custom_call_target="tpu_custom_call" | custom-call | flops 3080000000 | bytes 100000 | tf_op jit(solution)/shard_map/second_pass/pallas_call | solution.py:293
  66.2 1.0 %collective-permute-done.29.other_ref = f32[2,2,128,256]{3,2,1,0:T(8,128)S(1)} collective-permute-done((f32[2,2,128,256]{3,2,1,0:T(8,128)S(1)}, f32[2,2,128,256]{3,2,1,0:T(8,128)S(1)}, u32[]{:S(2)}, u32[]{:S(2)}) %collective-permute-start.29) | collective-permute-done | bytes 524320 | tf_op jit(solution)/shard_map/ppermute | solution.py:22
  67.4 0.6 collective-permute-start.30
  68.5 2.4 %collective-permute-start.32 = (f16[144,256]{1,0:T(8,128)(2,1)S(1)}, f16[144,256]{1,0:T(8,128)(2,1)S(1)}, u32[]{:S(2)}, u32[]{:S(2)}) collective-permute-start(f16[144,256]{1,0:T(8,128)(2,1)S(1)} %get-tuple-element.62), channel_id=1, source_target_pairs={{0,6},{1,7},{2,4},{3,5},{4,2},{5,3},{6,0},{7,1},{8,14},{9,15},{10,... | collective-permute-start | bytes 221192 | tf_op jit(solution)/shard_map/ppermute | solution.py:33
  70.9 1.0 %collective-permute-done.30 = f16[144,256]{1,0:T(8,128)(2,1)S(1)} collective-permute-done((f16[144,256]{1,0:T(8,128)(2,1)S(1)}, f16[144,256]{1,0:T(8,128)(2,1)S(1)}, u32[]{:S(2)}, u32[]{:S(2)}) %collective-permute-start.30) | collective-permute-done | bytes 73760 | tf_op jit(solution)/shard_map/ppermute | solution.py:22
  72.0 2.9 %collective-permute-done.31 = f16[144,256]{1,0:T(8,128)(2,1)S(1)} collective-permute-done((f16[144,256]{1,0:T(8,128)(2,1)S(1)}, f16[144,256]{1,0:T(8,128)(2,1)S(1)}, u32[]{:S(2)}, u32[]{:S(2)}) %collective-permute-start.31) | collective-permute-done | bytes 73760 | tf_op jit(solution)/shard_map/ppermute | solution.py:22
  74.9 0.7 collective-permute-done.32
  75.8 1.1 %collective-permute-start.33 = (f16[144,256]{1,0:T(8,128)(2,1)S(1)}, f16[144,256]{1,0:T(8,128)(2,1)S(1)}, u32[]{:S(2)}, u32[]{:S(2)}) collective-permute-start(f16[144,256]{1,0:T(8,128)(2,1)S(1)} %convert_element_type.86), channel_id=1, source_target_pairs={{0,8},{4,12},{8,0},{12,4},{16,24},{20,28},{24,16},{28,20},{1,9},{5... | collective-permute-start | bytes 221192 | tf_op jit(solution)/shard_map/ppermute | solution.py:22
  76.9 3.0 %collective-permute-start.34 = (f16[144,256]{1,0:T(8,128)(2,1)S(1)}, f16[144,256]{1,0:T(8,128)(2,1)S(1)}, u32[]{:S(2)}, u32[]{:S(2)}) collective-permute-start(f16[144,256]{1,0:T(8,128)(2,1)S(1)} %convert_element_type.86), channel_id=1, source_target_pairs={{0,16},{4,20},{8,24},{12,28},{16,0},{20,4},{24,8},{28,12},{1,17},{... | collective-permute-start | bytes 221192 | tf_op jit(solution)/shard_map/ppermute | solution.py:22
  80.2 3.2 %begin.1.in_ref = f32[256,256]{1,0:T(8,128)S(1)} custom-call(f32[3,128,128]{2,1,0:T(8,128)S(1)} %add.43.mine_ref, f32[3,128,128]{2,1,0:T(8,128)S(1)} %collective-permute-done.26.other_ref), custom_call_target="tpu_custom_call" | custom-call | flops 3630000128 | bytes 100000 | tf_op jit(solution)/shard_map/begin/pallas_call | solution.py:500
  83.5 0.7 collective-permute-done.34
  84.2 1.9 %collective-permute-done.35 = f16[144,256]{1,0:T(8,128)(2,1)S(1)} collective-permute-done((f16[144,256]{1,0:T(8,128)(2,1)S(1)}, f16[144,256]{1,0:T(8,128)(2,1)S(1)}, u32[]{:S(2)}, u32[]{:S(2)}) %collective-permute-start.35) | collective-permute-done | bytes 73760 | tf_op jit(solution)/shard_map/ppermute | solution.py:22
  86.2 0.9 collective-permute-start.36
  87.6 2.2 %collective-permute-start.38 = (f16[144,256]{1,0:T(8,128)(2,1)S(1)}, f16[144,256]{1,0:T(8,128)(2,1)S(1)}, u32[]{:S(2)}, u32[]{:S(2)}) collective-permute-start(f16[144,256]{1,0:T(8,128)(2,1)S(1)} %convert_element_type.91), channel_id=1, source_target_pairs={{0,6},{1,7},{2,4},{3,5},{4,2},{5,3},{6,0},{7,1},{8,14},{9,15},{10,... | collective-permute-start | bytes 221192 | tf_op jit(solution)/shard_map/ppermute | solution.py:33
  89.8 0.9 collective-permute-done.36
  90.7 2.9 %end.1.z_ref = f32[256,256]{1,0:T(8,128)S(1)} custom-call(f32[256,256]{1,0:T(8,128)S(1)} %begin.1.in_ref), custom_call_target="tpu_custom_call" | custom-call | flops 3190000128 | bytes 100000 | tf_op jit(solution)/shard_map/end/pallas_call | solution.py:500
  93.9 0.8 whiten.2.refs_0_
  94.8 0.7 collective-permute-done.39
  95.5 1.8 %whiten.3 = f32[4,256,256]{2,1,0:T(8,128)} custom-call(f32[256,256]{1,0:T(8,128)S(1)} %end.1.z_ref, f32[2,2,144,256]{3,2,1,0:T(8,128)S(1)} %convert_element_type.92.core_ref, f32[2,256,256]{2,1,0:T(8,128)S(1)} %whiten.2.refs_0_), custom_call_target="tpu_custom_call" | custom-call | flops 1320000000 | bytes 100000 | tf_op jit(solution)/shard_map/whiten/pallas_call | solution.py:566
  (83 shorter events, 9.2 us)
Async XLA Ops:
  0.6 11.2 %collective-permute-start = (bf16[128,256]{1,0:T(8,128)(2,1)}, bf16[128,256]{1,0:T(8,128)(2,1)S(1)}, u32[]{:S(2)}, u32[]{:S(2)}) collective-permute-start(bf16[128,256]{1,0:T(8,128)(2,1)} %factor_hbm.1), channel_id=1, source_target_pairs={{0,8},{4,12},{8,0},{12,4},{16,24},{20,28},{24,16},{28,20},{1,9},{5... | collective-permute-start | bytes 196616 | tf_op jit(solution)/shard_map/ppermute | solution.py:22
  3.7 8.1 %collective-permute-start.1 = (bf16[128,256]{1,0:T(8,128)(2,1)}, bf16[128,256]{1,0:T(8,128)(2,1)S(1)}, u32[]{:S(2)}, u32[]{:S(2)}) collective-permute-start(bf16[128,256]{1,0:T(8,128)(2,1)} %factor_hbm.1), channel_id=1, source_target_pairs={{0,16},{4,20},{8,24},{12,28},{16,0},{20,4},{24,8},{28,12},{1,17},{... | collective-permute-start | bytes 196616 | tf_op jit(solution)/shard_map/ppermute | solution.py:22
  6.3 6.3 %collective-permute-start.2 = (bf16[128,256]{1,0:T(8,128)(2,1)}, bf16[128,256]{1,0:T(8,128)(2,1)S(1)}, u32[]{:S(2)}, u32[]{:S(2)}) collective-permute-start(bf16[128,256]{1,0:T(8,128)(2,1)} %factor_hbm.1), channel_id=1, source_target_pairs={{0,24},{4,28},{8,16},{12,20},{16,8},{20,12},{24,0},{28,4},{1,25},{... | collective-permute-start | bytes 196616 | tf_op jit(solution)/shard_map/ppermute | solution.py:22
  6.3 11.4 %collective-permute-start.3 = (bf16[128,256]{1,0:T(8,128)(2,1)}, bf16[128,256]{1,0:T(8,128)(2,1)S(1)}, u32[]{:S(2)}, u32[]{:S(2)}) collective-permute-start(bf16[128,256]{1,0:T(8,128)(2,1)} %factor_hbm.1), channel_id=1, source_target_pairs={{0,4},{4,0},{8,12},{12,8},{16,20},{20,16},{24,28},{28,24},{1,5},{5... | collective-permute-start | bytes 196616 | tf_op jit(solution)/shard_map/ppermute | solution.py:22
  8.1 8.1 %collective-permute-start.8 = (bf16[128,256]{1,0:T(8,128)(2,1)}, bf16[128,256]{1,0:T(8,128)(2,1)S(1)}, u32[]{:S(2)}, u32[]{:S(2)}) collective-permute-start(bf16[128,256]{1,0:T(8,128)(2,1)} %factor_hbm.1), channel_id=1, source_target_pairs={{0,1},{1,0},{2,3},{3,2},{4,5},{5,4},{6,7},{7,6},{8,9},{9,8},{10,11... | collective-permute-start | bytes 196616 | tf_op jit(solution)/shard_map/ppermute | solution.py:22
  8.8 7.4 %copy-start.1 = (bf16[128,256]{1,0:T(8,128)(2,1)S(1)}, bf16[128,256]{1,0:T(8,128)(2,1)}, u32[]{:S(2)}) copy-start(bf16[128,256]{1,0:T(8,128)(2,1)} %factor_hbm.1) | copy-start | bytes 196612
  12.6 5.1 %collective-permute-start.4 = (bf16[128,256]{1,0:T(8,128)(2,1)S(1)}, bf16[128,256]{1,0:T(8,128)(2,1)S(1)}, u32[]{:S(2)}, u32[]{:S(2)}) collective-permute-start(bf16[128,256]{1,0:T(8,128)(2,1)S(1)} %collective-permute-done.refs_1_), channel_id=1, source_target_pairs={{0,4},{4,0},{8,12},{12,8},{16,20},{20,16},{24,28},{28,24},{1,5},{5... | collective-permute-start | bytes 196616 | tf_op jit(solution)/shard_map/ppermute | solution.py:22
  14.1 4.6 %collective-permute-start.5 = (bf16[128,256]{1,0:T(8,128)(2,1)S(1)}, bf16[128,256]{1,0:T(8,128)(2,1)S(1)}, u32[]{:S(2)}, u32[]{:S(2)}) collective-permute-start(bf16[128,256]{1,0:T(8,128)(2,1)S(1)} %collective-permute-done.1.refs_2_), channel_id=1, source_target_pairs={{0,4},{4,0},{8,12},{12,8},{16,20},{20,16},{24,28},{28,24},{1,5},{5... | collective-permute-start | bytes 196616 | tf_op jit(solution)/shard_map/ppermute | solution.py:22
  14.6 4.8 %collective-permute-start.6 = (bf16[128,256]{1,0:T(8,128)(2,1)S(1)}, bf16[128,256]{1,0:T(8,128)(2,1)S(1)}, u32[]{:S(2)}, u32[]{:S(2)}) collective-permute-start(bf16[128,256]{1,0:T(8,128)(2,1)S(1)} %collective-permute-done.2.refs_3_), channel_id=1, source_target_pairs={{0,4},{4,0},{8,12},{12,8},{16,20},{20,16},{24,28},{28,24},{1,5},{5... | collective-permute-start | bytes 196616 | tf_op jit(solution)/shard_map/ppermute | solution.py:22
  16.2 5.0 %collective-permute-start.9 = (bf16[256,256]{1,0:T(8,128)(2,1)S(1)}, bf16[256,256]{1,0:T(8,128)(2,1)S(1)}, u32[]{:S(2)}, u32[]{:S(2)}) collective-permute-start(bf16[256,256]{1,0:T(8,128)(2,1)S(1)} %pad_maximum_fusion.3), channel_id=1, source_target_pairs={{0,2},{1,3},{2,0},{3,1},{4,6},{5,7},{6,4},{7,5},{8,10},{9,11},{10,... | collective-permute-start | bytes 393224 | tf_op jit(solution)/shard_map/ppermute | solution.py:22
  19.8 1.5 %collective-permute-start.7 = (f32[3,128,128]{2,1,0:T(8,128)S(1)}, f32[3,128,128]{2,1,0:T(8,128)S(1)}, u32[]{:S(2)}, u32[]{:S(2)}) collective-permute-start(f32[3,128,128]{2,1,0:T(8,128)S(1)} %get-tuple-element.37), channel_id=1, source_target_pairs={{0,1},{1,0},{2,3},{3,2},{4,5},{5,4},{6,7},{7,6},{8,9},{9,8},{10,11... | collective-permute-start | bytes 589832 | tf_op jit(solution)/shard_map/ppermute | solution.py:22
  21.3 7.0 %collective-permute-start.10 = (f32[3,128,128]{2,1,0:T(8,128)S(1)}, f32[3,128,128]{2,1,0:T(8,128)S(1)}, u32[]{:S(2)}, u32[]{:S(2)}) collective-permute-start(f32[3,128,128]{2,1,0:T(8,128)S(1)} %add.33.mine_ref), channel_id=1, source_target_pairs={{0,2},{1,3},{2,0},{3,1},{4,6},{5,7},{6,4},{7,5},{8,10},{9,11},{10,... | collective-permute-start | bytes 589832 | tf_op jit(solution)/shard_map/ppermute | solution.py:22
  28.5 6.8 %collective-permute-start.13 = (f16[2,128,256]{2,1,0:T(8,128)(2,1)S(1)}, f16[2,128,256]{2,1,0:T(8,128)(2,1)S(1)}, u32[]{:S(2)}, u32[]{:S(2)}) collective-permute-start(f16[2,128,256]{2,1,0:T(8,128)(2,1)S(1)} %get-tuple-element.61), channel_id=1, source_target_pairs={{0,4},{4,0},{8,12},{12,8},{16,20},{20,16},{24,28},{28,24},{1,5},{5... | collective-permute-start | bytes 393224 | tf_op jit(solution)/shard_map/ppermute | solution.py:22
  29.6 6.5 %collective-permute-start.15 = (f16[2,128,256]{2,1,0:T(8,128)(2,1)S(1)}, f16[2,128,256]{2,1,0:T(8,128)(2,1)S(1)}, u32[]{:S(2)}, u32[]{:S(2)}) collective-permute-start(f16[2,128,256]{2,1,0:T(8,128)(2,1)S(1)} %get-tuple-element.60), channel_id=1, source_target_pairs={{0,4},{4,0},{8,12},{12,8},{16,20},{20,16},{24,28},{28,24},{1,5},{5... | collective-permute-start | bytes 393224 | tf_op jit(solution)/shard_map/ppermute | solution.py:22
  30.6 10.1 %collective-permute-start.11 = (f32[2,128,256]{2,1,0:T(8,128)S(1)}, f32[2,128,256]{2,1,0:T(8,128)S(1)}, u32[]{:S(2)}, u32[]{:S(2)}) collective-permute-start(f32[2,128,256]{2,1,0:T(8,128)S(1)} %split.20), channel_id=1, source_target_pairs={{0,1},{1,0},{2,3},{3,2},{4,5},{5,4},{6,7},{7,6},{8,9},{9,8},{10,11... | collective-permute-start | bytes 786440 | tf_op jit(solution)/shard_map/ppermute | solution.py:22
  36.2 10.5 %collective-permute-start.14 = (f16[128,256]{1,0:T(8,128)(2,1)S(1)}, f16[128,256]{1,0:T(8,128)(2,1)S(1)}, u32[]{:S(2)}, u32[]{:S(2)}) collective-permute-start(f16[128,256]{1,0:T(8,128)(2,1)S(1)} %fusion.9), channel_id=1, source_target_pairs={{0,8},{4,12},{8,0},{12,4},{16,24},{20,28},{24,16},{28,20},{1,9},{5... | collective-permute-start | bytes 196616 | tf_op jit(solution)/shard_map/ppermute | solution.py:22
  36.9 9.7 %collective-permute-start.16 = (f16[128,256]{1,0:T(8,128)(2,1)S(1)}, f16[128,256]{1,0:T(8,128)(2,1)S(1)}, u32[]{:S(2)}, u32[]{:S(2)}) collective-permute-start(f16[128,256]{1,0:T(8,128)(2,1)S(1)} %get-tuple-element.45), channel_id=1, source_target_pairs={{0,16},{4,20},{8,24},{12,28},{16,0},{20,4},{24,8},{28,12},{1,17},{... | collective-permute-start | bytes 196616 | tf_op jit(solution)/shard_map/ppermute | solution.py:22
  40.5 6.2 %collective-permute-start.17 = (f16[128,256]{1,0:T(8,128)(2,1)S(1)}, f16[128,256]{1,0:T(8,128)(2,1)S(1)}, u32[]{:S(2)}, u32[]{:S(2)}) collective-permute-start(f16[128,256]{1,0:T(8,128)(2,1)S(1)} %get-tuple-element.47), channel_id=1, source_target_pairs={{0,24},{4,28},{8,16},{12,20},{16,8},{20,12},{24,0},{28,4},{1,25},{... | collective-permute-start | bytes 196616 | tf_op jit(solution)/shard_map/ppermute | solution.py:22
  40.8 5.9 %collective-permute-start.12 = (f16[1,128,256]{2,1,0:T(8,128)(2,1)S(1)}, f16[1,128,256]{2,1,0:T(8,128)(2,1)S(1)}, u32[]{:S(2)}, u32[]{:S(2)}) collective-permute-start(f16[1,128,256]{2,1,0:T(8,128)(2,1)S(1)} %slice_convert_fusion.1), channel_id=1, source_target_pairs={{0,2},{1,3},{2,0},{3,1},{4,6},{5,7},{6,4},{7,5},{8,10},{9,11},{10,... | collective-permute-start | bytes 196616 | tf_op jit(solution)/shard_map/ppermute | solution.py:22
  47.0 18.0 %copy-start = (bf16[128,256]{1,0:T(8,128)(2,1)}, bf16[128,256]{1,0:T(8,128)(2,1)S(1)}, u32[]{:S(2)}) copy-start(bf16[128,256]{1,0:T(8,128)(2,1)S(1)} %convolution_convert_fusion.refs_0_) | copy-start | bytes 196612
  47.0 4.5 %collective-permute-start.27 = (bf16[128,256]{1,0:T(8,128)(2,1)S(1)}, bf16[128,256]{1,0:T(8,128)(2,1)S(1)}, u32[]{:S(2)}, u32[]{:S(2)}) collective-permute-start(bf16[128,256]{1,0:T(8,128)(2,1)S(1)} %convolution_convert_fusion.refs_0_), channel_id=1, source_target_pairs={{0,1},{1,0},{2,3},{3,2},{4,5},{5,4},{6,7},{7,6},{8,9},{9,8},{10,11... | collective-permute-start | bytes 196616 | tf_op jit(solution)/shard_map/ppermute | solution.py:22
  47.1 6.4 %collective-permute-start.18 = (bf16[128,256]{1,0:T(8,128)(2,1)S(1)}, bf16[128,256]{1,0:T(8,128)(2,1)S(1)}, u32[]{:S(2)}, u32[]{:S(2)}) collective-permute-start(bf16[128,256]{1,0:T(8,128)(2,1)S(1)} %convolution_convert_fusion.refs_0_), channel_id=1, source_target_pairs={{0,8},{4,12},{8,0},{12,4},{16,24},{20,28},{24,16},{28,20},{1,9},{5... | collective-permute-start | bytes 196616 | tf_op jit(solution)/shard_map/ppermute | solution.py:22
  47.6 8.0 %collective-permute-start.19 = (bf16[128,256]{1,0:T(8,128)(2,1)S(1)}, bf16[128,256]{1,0:T(8,128)(2,1)S(1)}, u32[]{:S(2)}, u32[]{:S(2)}) collective-permute-start(bf16[128,256]{1,0:T(8,128)(2,1)S(1)} %convolution_convert_fusion.refs_0_), channel_id=1, source_target_pairs={{0,16},{4,20},{8,24},{12,28},{16,0},{20,4},{24,8},{28,12},{1,17},{... | collective-permute-start | bytes 196616 | tf_op jit(solution)/shard_map/ppermute | solution.py:22
  51.3 6.1 %collective-permute-start.20 = (bf16[128,256]{1,0:T(8,128)(2,1)S(1)}, bf16[128,256]{1,0:T(8,128)(2,1)S(1)}, u32[]{:S(2)}, u32[]{:S(2)}) collective-permute-start(bf16[128,256]{1,0:T(8,128)(2,1)S(1)} %convolution_convert_fusion.refs_0_), channel_id=1, source_target_pairs={{0,24},{4,28},{8,16},{12,20},{16,8},{20,12},{24,0},{28,4},{1,25},{... | collective-permute-start | bytes 196616 | tf_op jit(solution)/shard_map/ppermute | solution.py:22
  51.5 10.6 %collective-permute-start.28 = (bf16[256,256]{1,0:T(8,128)(2,1)S(1)}, bf16[256,256]{1,0:T(8,128)(2,1)S(1)}, u32[]{:S(2)}, u32[]{:S(2)}) collective-permute-start(bf16[256,256]{1,0:T(8,128)(2,1)S(1)} %pad_maximum_fusion.4), channel_id=1, source_target_pairs={{0,2},{1,3},{2,0},{3,1},{4,6},{5,7},{6,4},{7,5},{8,10},{9,11},{10,... | collective-permute-start | bytes 393224 | tf_op jit(solution)/shard_map/ppermute | solution.py:22
  53.0 4.9 %collective-permute-start.21 = (bf16[128,256]{1,0:T(8,128)(2,1)S(1)}, bf16[128,256]{1,0:T(8,128)(2,1)S(1)}, u32[]{:S(2)}, u32[]{:S(2)}) collective-permute-start(bf16[128,256]{1,0:T(8,128)(2,1)S(1)} %convolution_convert_fusion.refs_0_), channel_id=1, source_target_pairs={{0,4},{4,0},{8,12},{12,8},{16,20},{20,16},{24,28},{28,24},{1,5},{5... | collective-permute-start | bytes 196616 | tf_op jit(solution)/shard_map/ppermute | solution.py:22
  53.5 5.0 %collective-permute-start.22 = (bf16[128,256]{1,0:T(8,128)(2,1)S(1)}, bf16[128,256]{1,0:T(8,128)(2,1)S(1)}, u32[]{:S(2)}, u32[]{:S(2)}) collective-permute-start(bf16[128,256]{1,0:T(8,128)(2,1)S(1)} %collective-permute-done.18.refs_1_), channel_id=1, source_target_pairs={{0,4},{4,0},{8,12},{12,8},{16,20},{20,16},{24,28},{28,24},{1,5},{5... | collective-permute-start | bytes 196616 | tf_op jit(solution)/shard_map/ppermute | solution.py:22
  55.5 4.7 %collective-permute-start.23 = (bf16[128,256]{1,0:T(8,128)(2,1)S(1)}, bf16[128,256]{1,0:T(8,128)(2,1)S(1)}, u32[]{:S(2)}, u32[]{:S(2)}) collective-permute-start(bf16[128,256]{1,0:T(8,128)(2,1)S(1)} %collective-permute-done.19.refs_2_), channel_id=1, source_target_pairs={{0,4},{4,0},{8,12},{12,8},{16,20},{20,16},{24,28},{28,24},{1,5},{5... | collective-permute-start | bytes 196616 | tf_op jit(solution)/shard_map/ppermute | solution.py:22
  57.4 4.3 %collective-permute-start.24 = (bf16[128,256]{1,0:T(8,128)(2,1)S(1)}, bf16[128,256]{1,0:T(8,128)(2,1)S(1)}, u32[]{:S(2)}, u32[]{:S(2)}) collective-permute-start(bf16[128,256]{1,0:T(8,128)(2,1)S(1)} %collective-permute-done.20.refs_3_), channel_id=1, source_target_pairs={{0,4},{4,0},{8,12},{12,8},{16,20},{20,16},{24,28},{28,24},{1,5},{5... | collective-permute-start | bytes 196616 | tf_op jit(solution)/shard_map/ppermute | solution.py:22
  62.1 2.9 %collective-permute-start.25 = (f32[3,128,128]{2,1,0:T(8,128)S(1)}, f32[3,128,128]{2,1,0:T(8,128)S(1)}, u32[]{:S(2)}, u32[]{:S(2)}) collective-permute-start(f32[3,128,128]{2,1,0:T(8,128)S(1)} %get-tuple-element.48), channel_id=1, source_target_pairs={{0,1},{1,0},{2,3},{3,2},{4,5},{5,4},{6,7},{7,6},{8,9},{9,8},{10,11... | collective-permute-start | bytes 589832 | tf_op jit(solution)/shard_map/ppermute | solution.py:22
  65.1 2.1 %collective-permute-start.29 = (f32[2,2,128,256]{3,2,1,0:T(8,128)S(1)}, f32[2,2,128,256]{3,2,1,0:T(8,128)S(1)}, u32[]{:S(2)}, u32[]{:S(2)}) collective-permute-start(f32[2,2,128,256]{3,2,1,0:T(8,128)S(1)} %get-tuple-element.56), channel_id=1, source_target_pairs={{0,1},{1,0},{2,3},{3,2},{4,5},{5,4},{6,7},{7,6},{8,9},{9,8},{10,11... | collective-permute-start | bytes 1572872 | tf_op jit(solution)/shard_map/ppermute | solution.py:22
  65.6 14.6 %collective-permute-start.26 = (f32[3,128,128]{2,1,0:T(8,128)S(1)}, f32[3,128,128]{2,1,0:T(8,128)S(1)}, u32[]{:S(2)}, u32[]{:S(2)}) collective-permute-start(f32[3,128,128]{2,1,0:T(8,128)S(1)} %add.43.mine_ref), channel_id=1, source_target_pairs={{0,2},{1,3},{2,0},{3,1},{4,6},{5,7},{6,4},{7,5},{8,10},{9,11},{10,... | collective-permute-start | bytes 589832 | tf_op jit(solution)/shard_map/ppermute | solution.py:22
  67.4 4.6 %collective-permute-start.30 = (f16[144,256]{1,0:T(8,128)(2,1)S(1)}, f16[144,256]{1,0:T(8,128)(2,1)S(1)}, u32[]{:S(2)}, u32[]{:S(2)}) collective-permute-start(f16[144,256]{1,0:T(8,128)(2,1)S(1)} %get-tuple-element.64), channel_id=1, source_target_pairs={{0,4},{4,0},{8,12},{12,8},{16,20},{20,16},{24,28},{28,24},{1,5},{5... | collective-permute-start | bytes 221192 | tf_op jit(solution)/shard_map/ppermute | solution.py:22
  68.0 6.9 %collective-permute-start.31 = (f16[144,256]{1,0:T(8,128)(2,1)S(1)}, f16[144,256]{1,0:T(8,128)(2,1)S(1)}, u32[]{:S(2)}, u32[]{:S(2)}) collective-permute-start(f16[144,256]{1,0:T(8,128)(2,1)S(1)} %get-tuple-element.63), channel_id=1, source_target_pairs={{0,2},{1,3},{2,0},{3,1},{4,6},{5,7},{6,4},{7,5},{8,10},{9,11},{10,... | collective-permute-start | bytes 221192 | tf_op jit(solution)/shard_map/ppermute | solution.py:22
  68.5 7.1 %collective-permute-start.32 = (f16[144,256]{1,0:T(8,128)(2,1)S(1)}, f16[144,256]{1,0:T(8,128)(2,1)S(1)}, u32[]{:S(2)}, u32[]{:S(2)}) collective-permute-start(f16[144,256]{1,0:T(8,128)(2,1)S(1)} %get-tuple-element.62), channel_id=1, source_target_pairs={{0,6},{1,7},{2,4},{3,5},{4,2},{5,3},{6,0},{7,1},{8,14},{9,15},{10,... | collective-permute-start | bytes 221192 | tf_op jit(solution)/shard_map/ppermute | solution.py:33
  75.8 7.7 %collective-permute-start.33 = (f16[144,256]{1,0:T(8,128)(2,1)S(1)}, f16[144,256]{1,0:T(8,128)(2,1)S(1)}, u32[]{:S(2)}, u32[]{:S(2)}) collective-permute-start(f16[144,256]{1,0:T(8,128)(2,1)S(1)} %convert_element_type.86), channel_id=1, source_target_pairs={{0,8},{4,12},{8,0},{12,4},{16,24},{20,28},{24,16},{28,20},{1,9},{5... | collective-permute-start | bytes 221192 | tf_op jit(solution)/shard_map/ppermute | solution.py:22
  76.9 7.3 %collective-permute-start.34 = (f16[144,256]{1,0:T(8,128)(2,1)S(1)}, f16[144,256]{1,0:T(8,128)(2,1)S(1)}, u32[]{:S(2)}, u32[]{:S(2)}) collective-permute-start(f16[144,256]{1,0:T(8,128)(2,1)S(1)} %convert_element_type.86), channel_id=1, source_target_pairs={{0,16},{4,20},{8,24},{12,28},{16,0},{20,4},{24,8},{28,12},{1,17},{... | collective-permute-start | bytes 221192 | tf_op jit(solution)/shard_map/ppermute | solution.py:22
  79.9 6.2 %collective-permute-start.35 = (f16[144,256]{1,0:T(8,128)(2,1)S(1)}, f16[144,256]{1,0:T(8,128)(2,1)S(1)}, u32[]{:S(2)}, u32[]{:S(2)}) collective-permute-start(f16[144,256]{1,0:T(8,128)(2,1)S(1)} %convert_element_type.86), channel_id=1, source_target_pairs={{0,24},{4,28},{8,16},{12,20},{16,8},{20,12},{24,0},{28,4},{1,25},{... | collective-permute-start | bytes 221192 | tf_op jit(solution)/shard_map/ppermute | solution.py:22
  86.2 4.4 %collective-permute-start.36 = (f16[144,256]{1,0:T(8,128)(2,1)S(1)}, f16[144,256]{1,0:T(8,128)(2,1)S(1)}, u32[]{:S(2)}, u32[]{:S(2)}) collective-permute-start(f16[144,256]{1,0:T(8,128)(2,1)S(1)} %convert_element_type.91), channel_id=1, source_target_pairs={{0,4},{4,0},{8,12},{12,8},{16,20},{20,16},{24,28},{28,24},{1,5},{5... | collective-permute-start | bytes 221192 | tf_op jit(solution)/shard_map/ppermute | solution.py:22
  87.1 6.5 %collective-permute-start.37 = (f16[144,256]{1,0:T(8,128)(2,1)S(1)}, f16[144,256]{1,0:T(8,128)(2,1)S(1)}, u32[]{:S(2)}, u32[]{:S(2)}) collective-permute-start(f16[144,256]{1,0:T(8,128)(2,1)S(1)} %convert_element_type.91), channel_id=1, source_target_pairs={{0,2},{1,3},{2,0},{3,1},{4,6},{5,7},{6,4},{7,5},{8,10},{9,11},{10,... | collective-permute-start | bytes 221192 | tf_op jit(solution)/shard_map/ppermute | solution.py:22
  87.6 6.1 %collective-permute-start.38 = (f16[144,256]{1,0:T(8,128)(2,1)S(1)}, f16[144,256]{1,0:T(8,128)(2,1)S(1)}, u32[]{:S(2)}, u32[]{:S(2)}) collective-permute-start(f16[144,256]{1,0:T(8,128)(2,1)S(1)} %convert_element_type.91), channel_id=1, source_target_pairs={{0,6},{1,7},{2,4},{3,5},{4,2},{5,3},{6,0},{7,1},{8,14},{9,15},{10,... | collective-permute-start | bytes 221192 | tf_op jit(solution)/shard_map/ppermute | solution.py:33
  93.8 1.6 %collective-permute-start.39 = (f16[2,2,144,256]{3,2,1,0:T(8,128)(2,1)S(1)}, f16[2,2,144,256]{3,2,1,0:T(8,128)(2,1)S(1)}, u32[]{:S(2)}, u32[]{:S(2)}) collective-permute-start(f16[2,2,144,256]{3,2,1,0:T(8,128)(2,1)S(1)} %pad_maximum_fusion), channel_id=1, source_target_pairs={{0,1},{1,0},{2,3},{3,2},{4,5},{5,4},{6,7},{7,6},{8,9},{9,8},{10,11... | collective-permute-start | bytes 884744 | tf_op jit(solution)/shard_map/ppermute | solution.py:22

commit v4 on v3

--- a/solution.py
+++ b/solution.py
@@ -398,13 +398,13 @@
             middle = jnp.concatenate(split(middle, 3), axis=1)
             total = total + dot(middle, jnp.concatenate([right] * 3, axis=0))
     z_ref[...] = total
-    eliminate(z_ref, 0, 3 * size // 256, 32, 16)
+    eliminate(z_ref, 0, size // 64, 32, 16)
 
 
 def inverse_kernel(in_ref, scale_ref, out_ref, z_ref):
     size = z_ref.shape[0]
     z_ref[...] = in_ref[...]
-    eliminate(z_ref, 3 * size // 256, size // 32, 32, 16)
+    eliminate(z_ref, size // 64, size // 32, 32, 16)
     high, mid, low = split(lower_of(z_ref[...]), 3)
     left = jnp.concatenate([high, high, mid, mid, high, low], axis=0)
     right = jnp.concatenate([high, mid, high, mid, low, high], axis=0)

time: 97.5 us -> 97.2 us (level)
  waiting for transfers between devices: 20.7 us -> 18 us
  starting transfers between devices: 44.1 us -> 46.5 us
    ppermute x38, starting transfers between devices: 39.5 us -> 44.3 us  [swap(): return lax.ppermute(x, axis, [(i, i ^ mask) for i in range(size)])]
    ppermute x38, waiting for transfers between devices: 20 us -> 16.2 us  [swap(): return lax.ppermute(x, axis, [(i, i ^ mask) for i in range(size)])]
    ppermute x2, starting transfers between devices: 4.61 us -> 2.23 us  [swap_both(): lax.ppermute(x, ('rows', 'cols'), [(i, i ^ mask) for i in range(size)])]
    ppermute x2, waiting for transfers between devices: 0.71 us -> 1.78 us  [swap_both(): lax.ppermute(x, ('rows', 'cols'), [(i, i ^ mask) for i in range(size)])]
  transfers between devices with their start and end apart: 40 -> 40, of which waited for: 20 -> 19; matrix products, arithmetic and copies ran while one was open for 1% -> 1% of each run, Pallas kernels for 28% -> 28%
where the time goes in v4:
time: 97.2 us; the launch traced here: 97.1 us
  starting transfers between devices  46.5 us (48%)
  Pallas kernels  29.5 us (30%)
  waiting for transfers between devices  18 us (19%)
  between operations  1.07 us (1%)
    ppermute x38, starting transfers between devices, swap(): return lax.ppermute(x, axis, [(i, i ^ mask) for i in range(size)])  44.3 us
    ppermute x38, waiting for transfers between devices, swap(): return lax.ppermute(x, axis, [(i, i ^ mask) for i in range(size)])  16.2 us
    pallas_call x4, Pallas kernels, square_call(): pl.pallas_call(kernel, out_shape=jax.ShapeDtypeStruct((rank, rank), jnp.f...  15 us
    pallas_call x1, Pallas kernels, first_pass(): pl.pallas_call(functools.partial(first_kernel, bits_c=bits_of('cols')), o...  4.85 us
    pallas_call x1, Pallas kernels, prepare(): pl.pallas_call(functools.partial(prepare_kernel, half=n_rows // 2, terms=...  3.17 us
    pallas_call x1, Pallas kernels, second_pass(): pl.pallas_call(functools.partial(second_kernel, bits_c=bits_of('cols')),...  2.76 us
    pallas_call x2, Pallas kernels, call(): pl.pallas_call(functools.partial(kernel, bits_c=bits_of('cols')), out_sha...  2.64 us
    ppermute x2, starting transfers between devices, swap_both(): lax.ppermute(x, ('rows', 'cols'), [(i, i ^ mask) for i in range(size)])  2.23 us
  transfers between devices with their start and end apart: 40, of which 19 were waited for; matrix products, arithmetic and copies ran while one was open for 1% of the time, Pallas kernels for 28%

profile of v4, /device:TPU:0, one launch (start us, length us, event | category | flops | bytes accessed | tf_op | source)
XLA Modules:
  0.0 97.1 jit_solution(1916038455154007609)
XLA Ops:
  0.6 3.1 %collective-permute-start = (bf16[128,256]{1,0:T(8,128)(2,1)}, bf16[128,256]{1,0:T(8,128)(2,1)S(1)}, u32[]{:S(2)}, u32[]{:S(2)}) collective-permute-start(bf16[128,256]{1,0:T(8,128)(2,1)} %factor_hbm.1), channel_id=1, source_target_pairs={{0,8},{4,12},{8,0},{12,4},{16,24},{20,28},{24,16},{28,20},{1,9},{5... | collective-permute-start | bytes 196616 | tf_op jit(solution)/shard_map/ppermute | solution.py:22
  3.7 2.6 %collective-permute-start.1 = (bf16[128,256]{1,0:T(8,128)(2,1)}, bf16[128,256]{1,0:T(8,128)(2,1)S(1)}, u32[]{:S(2)}, u32[]{:S(2)}) collective-permute-start(bf16[128,256]{1,0:T(8,128)(2,1)} %factor_hbm.1), channel_id=1, source_target_pairs={{0,16},{4,20},{8,24},{12,28},{16,0},{20,4},{24,8},{28,12},{1,17},{... | collective-permute-start | bytes 196616 | tf_op jit(solution)/shard_map/ppermute | solution.py:22
  6.3 1.7 %collective-permute-start.3 = (bf16[128,256]{1,0:T(8,128)(2,1)}, bf16[128,256]{1,0:T(8,128)(2,1)S(1)}, u32[]{:S(2)}, u32[]{:S(2)}) collective-permute-start(bf16[128,256]{1,0:T(8,128)(2,1)} %factor_hbm.1), channel_id=1, source_target_pairs={{0,4},{4,0},{8,12},{12,8},{16,20},{20,16},{24,28},{28,24},{1,5},{5... | collective-permute-start | bytes 196616 | tf_op jit(solution)/shard_map/ppermute | solution.py:22
  8.1 0.7 copy.8.counts_ref
  8.8 3.2 %prepare.1 = (s32[4,24]{1,0:T(4,128)S(1)}, f32[1,256]{1,0:T(1,128)S(1)}, bf16[4,12,128,128]{3,2,1,0:T(8,128)(2,1)S(1)}, bf16[4,256,256]{2,1,0:T(8,128)(2,1)S(1)}, bf16[128,256]{1,0:T(8,128)(2,1)S(1)}) custom-call(s32[4,1,12]{2,1,0:T(1,128)} %rows_hbm.1, s32[4,1,12]{2,1,0:T(1,128)} %cols_hbm.1, s32[4,1,1]{2,1,0:T(1,128)S(1)} %copy.8.counts_ref, ...), custom_call_target="tpu_custom_call" | custom-call | flops 2200000000 | bytes 100000 | tf_op jit(solution)/shard_map/prepare/pallas_call | solution.py:179
  12.6 1.5 %collective-permute-start.4 = (bf16[128,256]{1,0:T(8,128)(2,1)S(1)}, bf16[128,256]{1,0:T(8,128)(2,1)S(1)}, u32[]{:S(2)}, u32[]{:S(2)}) collective-permute-start(bf16[128,256]{1,0:T(8,128)(2,1)S(1)} %collective-permute-done.refs_1_), channel_id=1, source_target_pairs={{0,4},{4,0},{8,12},{12,8},{16,20},{20,16},{24,28},{28,24},{1,5},{5... | collective-permute-start | bytes 196616 | tf_op jit(solution)/shard_map/ppermute | solution.py:22
  14.6 1.5 %collective-permute-start.6 = (bf16[128,256]{1,0:T(8,128)(2,1)S(1)}, bf16[128,256]{1,0:T(8,128)(2,1)S(1)}, u32[]{:S(2)}, u32[]{:S(2)}) collective-permute-start(bf16[128,256]{1,0:T(8,128)(2,1)S(1)} %collective-permute-done.2.refs_3_), channel_id=1, source_target_pairs={{0,4},{4,0},{8,12},{12,8},{16,20},{20,16},{24,28},{28,24},{1,5},{5... | collective-permute-start | bytes 196616 | tf_op jit(solution)/shard_map/ppermute | solution.py:22
  16.2 1.6 %collective-permute-start.9 = (bf16[256,256]{1,0:T(8,128)(2,1)S(1)}, bf16[256,256]{1,0:T(8,128)(2,1)S(1)}, u32[]{:S(2)}, u32[]{:S(2)}) collective-permute-start(bf16[256,256]{1,0:T(8,128)(2,1)S(1)} %pad_maximum_fusion.3), channel_id=1, source_target_pairs={{0,2},{1,3},{2,0},{3,1},{4,6},{5,7},{6,4},{7,5},{8,10},{9,11},{10,... | collective-permute-start | bytes 393224 | tf_op jit(solution)/shard_map/ppermute | solution.py:22
  17.7 0.9 collective-permute-done.5.refs_6_
  18.7 0.7 collective-permute-done.6.refs_7_
  19.9 1.4 %collective-permute-done.9 = bf16[256,256]{1,0:T(8,128)(2,1)S(1)} collective-permute-done((bf16[256,256]{1,0:T(8,128)(2,1)S(1)}, bf16[256,256]{1,0:T(8,128)(2,1)S(1)}, u32[]{:S(2)}, u32[]{:S(2)}) %collective-permute-start.9) | collective-permute-done | bytes 131104 | tf_op jit(solution)/shard_map/ppermute | solution.py:22
  21.3 1.6 %collective-permute-start.10 = (f32[3,128,128]{2,1,0:T(8,128)S(1)}, f32[3,128,128]{2,1,0:T(8,128)S(1)}, u32[]{:S(2)}, u32[]{:S(2)}) collective-permute-start(f32[3,128,128]{2,1,0:T(8,128)S(1)} %add.33.mine_ref), channel_id=1, source_target_pairs={{0,2},{1,3},{2,0},{3,1},{4,6},{5,7},{6,4},{7,5},{8,10},{9,11},{10,... | collective-permute-start | bytes 589832 | tf_op jit(solution)/shard_map/ppermute | solution.py:22
  22.9 4.8 %first_pass.1 = (f32[4,128,256]{2,1,0:T(8,128)S(1)}, f32[8,128,256]{2,1,0:T(8,128)S(1)}) custom-call(s32[4,24]{1,0:T(4,128)S(1)} %get-tuple-element.29.places_ref, f32[1,256]{1,0:T(1,128)S(1)} %get-tuple-element.30.scale_ref, bf16[4,12,128,128]{3,2,1,0:T(8,128)(2,1)S(1)} %get-tuple-element.31.tiles_ref, bf16[8,128,256]{2,1,0:T(8,128)(2,1)S(1)} %bitcast.28, ...), custom_call_target="tpu_custom_call" | custom-call | flops 5280000000 | bytes 100000 | tf_op jit(solution)/shard_map/first_pass/pallas_call | solution.py:242
  28.5 1.1 %collective-permute-start.13 = (f16[2,128,256]{2,1,0:T(8,128)(2,1)S(1)}, f16[2,128,256]{2,1,0:T(8,128)(2,1)S(1)}, u32[]{:S(2)}, u32[]{:S(2)}) collective-permute-start(f16[2,128,256]{2,1,0:T(8,128)(2,1)S(1)} %get-tuple-element.61), channel_id=1, source_target_pairs={{0,4},{4,0},{8,12},{12,8},{16,20},{20,16},{24,28},{28,24},{1,5},{5... | collective-permute-start | bytes 393224 | tf_op jit(solution)/shard_map/ppermute | solution.py:22
  29.6 1.0 %collective-permute-start.15 = (f16[2,128,256]{2,1,0:T(8,128)(2,1)S(1)}, f16[2,128,256]{2,1,0:T(8,128)(2,1)S(1)}, u32[]{:S(2)}, u32[]{:S(2)}) collective-permute-start(f16[2,128,256]{2,1,0:T(8,128)(2,1)S(1)} %get-tuple-element.60), channel_id=1, source_target_pairs={{0,4},{4,0},{8,12},{12,8},{16,20},{20,16},{24,28},{28,24},{1,5},{5... | collective-permute-start | bytes 393224 | tf_op jit(solution)/shard_map/ppermute | solution.py:22
  30.7 5.3 %system.1.in_ref = f32[256,256]{1,0:T(8,128)S(1)} custom-call(f32[3,128,128]{2,1,0:T(8,128)S(1)} %add.33.mine_ref, f32[3,128,128]{2,1,0:T(8,128)S(1)} %collective-permute-done.10.other_ref, bf16[4,256,256]{2,1,0:T(8,128)(2,1)S(1)} %get-tuple-element.39.cores_ref), custom_call_target="tpu_custom_call" | custom-call | flops 4180000000 | bytes 100000 | tf_op jit(solution)/shard_map/system/pallas_call | solution.py:500
  36.8 3.7 %collective-permute-start.16 = (f16[128,256]{1,0:T(8,128)(2,1)S(1)}, f16[128,256]{1,0:T(8,128)(2,1)S(1)}, u32[]{:S(2)}, u32[]{:S(2)}) collective-permute-start(f16[128,256]{1,0:T(8,128)(2,1)S(1)} %get-tuple-element.45), channel_id=1, source_target_pairs={{0,16},{4,20},{8,24},{12,28},{16,0},{20,4},{24,8},{28,12},{1,17},{... | collective-permute-start | bytes 196616 | tf_op jit(solution)/shard_map/ppermute | solution.py:22
  40.8 1.6 %collective-permute-start.12 = (f16[1,128,256]{2,1,0:T(8,128)(2,1)S(1)}, f16[1,128,256]{2,1,0:T(8,128)(2,1)S(1)}, u32[]{:S(2)}, u32[]{:S(2)}) collective-permute-start(f16[1,128,256]{2,1,0:T(8,128)(2,1)S(1)} %slice_convert_fusion.1), channel_id=1, source_target_pairs={{0,2},{1,3},{2,0},{3,1},{4,6},{5,7},{6,4},{7,5},{8,10},{9,11},{10,... | collective-permute-start | bytes 196616 | tf_op jit(solution)/shard_map/ppermute | solution.py:22
  42.4 3.5 %inverse.1 = f32[256,256]{1,0:T(8,128)S(1)} custom-call(f32[256,256]{1,0:T(8,128)S(1)} %system.1.in_ref, f32[1,256]{1,0:T(1,128)S(1)} %get-tuple-element.30.scale_ref), custom_call_target="tpu_custom_call" | custom-call | flops 5720000000 | bytes 100000 | tf_op jit(solution)/shard_map/inverse/pallas_call | solution.py:500
  45.9 0.7 collective-permute-done.17
  47.1 1.1 %collective-permute-start.18 = (bf16[128,256]{1,0:T(8,128)(2,1)S(1)}, bf16[128,256]{1,0:T(8,128)(2,1)S(1)}, u32[]{:S(2)}, u32[]{:S(2)}) collective-permute-start(bf16[128,256]{1,0:T(8,128)(2,1)S(1)} %convolution_convert_fusion.refs_0_), channel_id=1, source_target_pairs={{0,8},{4,12},{8,0},{12,4},{16,24},{20,28},{24,16},{28,20},{1,9},{5... | collective-permute-start | bytes 196616 | tf_op jit(solution)/shard_map/ppermute | solution.py:22
  48.1 2.4 %collective-permute-start.19 = (bf16[128,256]{1,0:T(8,128)(2,1)S(1)}, bf16[128,256]{1,0:T(8,128)(2,1)S(1)}, u32[]{:S(2)}, u32[]{:S(2)}) collective-permute-start(bf16[128,256]{1,0:T(8,128)(2,1)S(1)} %convolution_convert_fusion.refs_0_), channel_id=1, source_target_pairs={{0,16},{4,20},{8,24},{12,28},{16,0},{20,4},{24,8},{28,12},{1,17},{... | collective-permute-start | bytes 196616 | tf_op jit(solution)/shard_map/ppermute | solution.py:22
  50.6 0.9 collective-permute-start.20
  51.5 1.5 %collective-permute-start.28 = (bf16[256,256]{1,0:T(8,128)(2,1)S(1)}, bf16[256,256]{1,0:T(8,128)(2,1)S(1)}, u32[]{:S(2)}, u32[]{:S(2)}) collective-permute-start(bf16[256,256]{1,0:T(8,128)(2,1)S(1)} %pad_maximum_fusion.4), channel_id=1, source_target_pairs={{0,2},{1,3},{2,0},{3,1},{4,6},{5,7},{6,4},{7,5},{8,10},{9,11},{10,... | collective-permute-start | bytes 393224 | tf_op jit(solution)/shard_map/ppermute | solution.py:22
  53.5 1.6 %collective-permute-start.22 = (bf16[128,256]{1,0:T(8,128)(2,1)S(1)}, bf16[128,256]{1,0:T(8,128)(2,1)S(1)}, u32[]{:S(2)}, u32[]{:S(2)}) collective-permute-start(bf16[128,256]{1,0:T(8,128)(2,1)S(1)} %collective-permute-done.18.refs_1_), channel_id=1, source_target_pairs={{0,4},{4,0},{8,12},{12,8},{16,20},{20,16},{24,28},{28,24},{1,5},{5... | collective-permute-start | bytes 196616 | tf_op jit(solution)/shard_map/ppermute | solution.py:22
  55.1 0.7 collective-permute-done.19.refs_2_
  56.7 1.2 %collective-permute-start.24 = (bf16[128,256]{1,0:T(8,128)(2,1)S(1)}, bf16[128,256]{1,0:T(8,128)(2,1)S(1)}, u32[]{:S(2)}, u32[]{:S(2)}) collective-permute-start(bf16[128,256]{1,0:T(8,128)(2,1)S(1)} %collective-permute-done.20.refs_3_), channel_id=1, source_target_pairs={{0,4},{4,0},{8,12},{12,8},{16,20},{20,16},{24,28},{28,24},{1,5},{5... | collective-permute-start | bytes 196616 | tf_op jit(solution)/shard_map/ppermute | solution.py:22
  57.9 1.2 %collective-permute-done.22.refs_5_ = bf16[128,256]{1,0:T(8,128)(2,1)S(1)} collective-permute-done((bf16[128,256]{1,0:T(8,128)(2,1)S(1)}, bf16[128,256]{1,0:T(8,128)(2,1)S(1)}, u32[]{:S(2)}, u32[]{:S(2)}) %collective-permute-start.22) | collective-permute-done | bytes 65568 | tf_op jit(solution)/shard_map/ppermute | solution.py:22
  59.1 1.0 %collective-permute-done.23.refs_6_ = bf16[128,256]{1,0:T(8,128)(2,1)S(1)} collective-permute-done((bf16[128,256]{1,0:T(8,128)(2,1)S(1)}, bf16[128,256]{1,0:T(8,128)(2,1)S(1)}, u32[]{:S(2)}, u32[]{:S(2)}) %collective-permute-start.23) | collective-permute-done | bytes 65568 | tf_op jit(solution)/shard_map/ppermute | solution.py:22
  60.1 0.8 collective-permute-done.24.refs_7_
  61.5 2.8 %second_pass.1 = f32[4,2,128,256]{3,2,1,0:T(8,128)S(1)} custom-call(s32[4,24]{1,0:T(4,128)S(1)} %get-tuple-element.29.places_ref, bf16[4,12,128,128]{3,2,1,0:T(8,128)(2,1)S(1)} %get-tuple-element.31.tiles_ref, bf16[8,128,256]{2,1,0:T(8,128)(2,1)S(1)} %bitcast.29, bf16[512,256]{1,0:T(8,128)(2,1)S(1)} %pad_maximum_fusion.2.panel_ref), custom_call_target="tpu_custom_call" | custom-call | flops 3080000000 | bytes 100000 | tf_op jit(solution)/shard_map/second_pass/pallas_call | solution.py:293
  64.9 2.1 %collective-permute-start.26 = (f32[3,128,128]{2,1,0:T(8,128)S(1)}, f32[3,128,128]{2,1,0:T(8,128)S(1)}, u32[]{:S(2)}, u32[]{:S(2)}) collective-permute-start(f32[3,128,128]{2,1,0:T(8,128)S(1)} %add.43.mine_ref), channel_id=1, source_target_pairs={{0,2},{1,3},{2,0},{3,1},{4,6},{5,7},{6,4},{7,5},{8,10},{9,11},{10,... | collective-permute-start | bytes 589832 | tf_op jit(solution)/shard_map/ppermute | solution.py:22
  67.2 1.4 %collective-permute-start.30 = (f16[144,256]{1,0:T(8,128)(2,1)S(1)}, f16[144,256]{1,0:T(8,128)(2,1)S(1)}, u32[]{:S(2)}, u32[]{:S(2)}) collective-permute-start(f16[144,256]{1,0:T(8,128)(2,1)S(1)} %get-tuple-element.64), channel_id=1, source_target_pairs={{0,4},{4,0},{8,12},{12,8},{16,20},{20,16},{24,28},{28,24},{1,5},{5... | collective-permute-start | bytes 221192 | tf_op jit(solution)/shard_map/ppermute | solution.py:22
  68.6 1.5 %collective-permute-start.31 = (f16[144,256]{1,0:T(8,128)(2,1)S(1)}, f16[144,256]{1,0:T(8,128)(2,1)S(1)}, u32[]{:S(2)}, u32[]{:S(2)}) collective-permute-start(f16[144,256]{1,0:T(8,128)(2,1)S(1)} %get-tuple-element.63), channel_id=1, source_target_pairs={{0,2},{1,3},{2,0},{3,1},{4,6},{5,7},{6,4},{7,5},{8,10},{9,11},{10,... | collective-permute-start | bytes 221192 | tf_op jit(solution)/shard_map/ppermute | solution.py:22
  70.8 0.9 collective-permute-done.30
  71.6 2.6 %collective-permute-done.31 = f16[144,256]{1,0:T(8,128)(2,1)S(1)} collective-permute-done((f16[144,256]{1,0:T(8,128)(2,1)S(1)}, f16[144,256]{1,0:T(8,128)(2,1)S(1)}, u32[]{:S(2)}, u32[]{:S(2)}) %collective-permute-start.31) | collective-permute-done | bytes 73760 | tf_op jit(solution)/shard_map/ppermute | solution.py:22
  74.3 1.8 %collective-permute-done.32 = f16[144,256]{1,0:T(8,128)(2,1)S(1)} collective-permute-done((f16[144,256]{1,0:T(8,128)(2,1)S(1)}, f16[144,256]{1,0:T(8,128)(2,1)S(1)}, u32[]{:S(2)}, u32[]{:S(2)}) %collective-permute-start.32) | collective-permute-done | bytes 73760 | tf_op jit(solution)/shard_map/ppermute | solution.py:33
  76.4 3.2 %collective-permute-start.34 = (f16[144,256]{1,0:T(8,128)(2,1)S(1)}, f16[144,256]{1,0:T(8,128)(2,1)S(1)}, u32[]{:S(2)}, u32[]{:S(2)}) collective-permute-start(f16[144,256]{1,0:T(8,128)(2,1)S(1)} %convert_element_type.86), channel_id=1, source_target_pairs={{0,16},{4,20},{8,24},{12,28},{16,0},{20,4},{24,8},{28,12},{1,17},{... | collective-permute-start | bytes 221192 | tf_op jit(solution)/shard_map/ppermute | solution.py:22
  79.6 1.1 %collective-permute-start.35 = (f16[144,256]{1,0:T(8,128)(2,1)S(1)}, f16[144,256]{1,0:T(8,128)(2,1)S(1)}, u32[]{:S(2)}, u32[]{:S(2)}) collective-permute-start(f16[144,256]{1,0:T(8,128)(2,1)S(1)} %convert_element_type.86), channel_id=1, source_target_pairs={{0,24},{4,28},{8,16},{12,20},{16,8},{20,12},{24,0},{28,4},{1,25},{... | collective-permute-start | bytes 221192 | tf_op jit(solution)/shard_map/ppermute | solution.py:22
  80.6 3.2 %begin.1.in_ref = f32[256,256]{1,0:T(8,128)S(1)} custom-call(f32[3,128,128]{2,1,0:T(8,128)S(1)} %add.43.mine_ref, f32[3,128,128]{2,1,0:T(8,128)S(1)} %collective-permute-done.26.other_ref), custom_call_target="tpu_custom_call" | custom-call | flops 3630000128 | bytes 100000 | tf_op jit(solution)/shard_map/begin/pallas_call | solution.py:500
  84.3 1.5 %collective-permute-done.35 = f16[144,256]{1,0:T(8,128)(2,1)S(1)} collective-permute-done((f16[144,256]{1,0:T(8,128)(2,1)S(1)}, f16[144,256]{1,0:T(8,128)(2,1)S(1)}, u32[]{:S(2)}, u32[]{:S(2)}) %collective-permute-start.35) | collective-permute-done | bytes 73760 | tf_op jit(solution)/shard_map/ppermute | solution.py:22
  86.0 0.8 collective-permute-start.36
  86.7 1.2 %collective-permute-start.37 = (f16[144,256]{1,0:T(8,128)(2,1)S(1)}, f16[144,256]{1,0:T(8,128)(2,1)S(1)}, u32[]{:S(2)}, u32[]{:S(2)}) collective-permute-start(f16[144,256]{1,0:T(8,128)(2,1)S(1)} %convert_element_type.91), channel_id=1, source_target_pairs={{0,2},{1,3},{2,0},{3,1},{4,6},{5,7},{6,4},{7,5},{8,10},{9,11},{10,... | collective-permute-start | bytes 221192 | tf_op jit(solution)/shard_map/ppermute | solution.py:22
  87.9 1.6 %collective-permute-start.38 = (f16[144,256]{1,0:T(8,128)(2,1)S(1)}, f16[144,256]{1,0:T(8,128)(2,1)S(1)}, u32[]{:S(2)}, u32[]{:S(2)}) collective-permute-start(f16[144,256]{1,0:T(8,128)(2,1)S(1)} %convert_element_type.91), channel_id=1, source_target_pairs={{0,6},{1,7},{2,4},{3,5},{4,2},{5,3},{6,0},{7,1},{8,14},{9,15},{10,... | collective-permute-start | bytes 221192 | tf_op jit(solution)/shard_map/ppermute | solution.py:33
  89.5 0.9 collective-permute-done.36
  90.4 2.9 %end.1.z_ref = f32[256,256]{1,0:T(8,128)S(1)} custom-call(f32[256,256]{1,0:T(8,128)S(1)} %begin.1.in_ref), custom_call_target="tpu_custom_call" | custom-call | flops 3190000128 | bytes 100000 | tf_op jit(solution)/shard_map/end/pallas_call | solution.py:500
  93.7 0.8 whiten.2.refs_0_
  95.2 1.8 %whiten.3 = f32[4,256,256]{2,1,0:T(8,128)} custom-call(f32[256,256]{1,0:T(8,128)S(1)} %end.1.z_ref, f32[2,2,144,256]{3,2,1,0:T(8,128)S(1)} %convert_element_type.92.core_ref, f32[2,256,256]{2,1,0:T(8,128)S(1)} %whiten.2.refs_0_), custom_call_target="tpu_custom_call" | custom-call | flops 1320000000 | bytes 100000 | tf_op jit(solution)/shard_map/whiten/pallas_call | solution.py:566
  (83 shorter events, 9.0 us)
Async XLA Ops:
  0.6 11.3 %collective-permute-start = (bf16[128,256]{1,0:T(8,128)(2,1)}, bf16[128,256]{1,0:T(8,128)(2,1)S(1)}, u32[]{:S(2)}, u32[]{:S(2)}) collective-permute-start(bf16[128,256]{1,0:T(8,128)(2,1)} %factor_hbm.1), channel_id=1, source_target_pairs={{0,8},{4,12},{8,0},{12,4},{16,24},{20,28},{24,16},{28,20},{1,9},{5... | collective-permute-start | bytes 196616 | tf_op jit(solution)/shard_map/ppermute | solution.py:22
  3.7 8.3 %collective-permute-start.1 = (bf16[128,256]{1,0:T(8,128)(2,1)}, bf16[128,256]{1,0:T(8,128)(2,1)S(1)}, u32[]{:S(2)}, u32[]{:S(2)}) collective-permute-start(bf16[128,256]{1,0:T(8,128)(2,1)} %factor_hbm.1), channel_id=1, source_target_pairs={{0,16},{4,20},{8,24},{12,28},{16,0},{20,4},{24,8},{28,12},{1,17},{... | collective-permute-start | bytes 196616 | tf_op jit(solution)/shard_map/ppermute | solution.py:22
  6.3 6.3 %collective-permute-start.2 = (bf16[128,256]{1,0:T(8,128)(2,1)}, bf16[128,256]{1,0:T(8,128)(2,1)S(1)}, u32[]{:S(2)}, u32[]{:S(2)}) collective-permute-start(bf16[128,256]{1,0:T(8,128)(2,1)} %factor_hbm.1), channel_id=1, source_target_pairs={{0,24},{4,28},{8,16},{12,20},{16,8},{20,12},{24,0},{28,4},{1,25},{... | collective-permute-start | bytes 196616 | tf_op jit(solution)/shard_map/ppermute | solution.py:22
  6.3 11.4 %collective-permute-start.3 = (bf16[128,256]{1,0:T(8,128)(2,1)}, bf16[128,256]{1,0:T(8,128)(2,1)S(1)}, u32[]{:S(2)}, u32[]{:S(2)}) collective-permute-start(bf16[128,256]{1,0:T(8,128)(2,1)} %factor_hbm.1), channel_id=1, source_target_pairs={{0,4},{4,0},{8,12},{12,8},{16,20},{20,16},{24,28},{28,24},{1,5},{5... | collective-permute-start | bytes 196616 | tf_op jit(solution)/shard_map/ppermute | solution.py:22
  8.1 8.1 %collective-permute-start.8 = (bf16[128,256]{1,0:T(8,128)(2,1)}, bf16[128,256]{1,0:T(8,128)(2,1)S(1)}, u32[]{:S(2)}, u32[]{:S(2)}) collective-permute-start(bf16[128,256]{1,0:T(8,128)(2,1)} %factor_hbm.1), channel_id=1, source_target_pairs={{0,1},{1,0},{2,3},{3,2},{4,5},{5,4},{6,7},{7,6},{8,9},{9,8},{10,11... | collective-permute-start | bytes 196616 | tf_op jit(solution)/shard_map/ppermute | solution.py:22
  8.8 7.4 %copy-start.1 = (bf16[128,256]{1,0:T(8,128)(2,1)S(1)}, bf16[128,256]{1,0:T(8,128)(2,1)}, u32[]{:S(2)}) copy-start(bf16[128,256]{1,0:T(8,128)(2,1)} %factor_hbm.1) | copy-start | bytes 196612
  12.6 5.1 %collective-permute-start.4 = (bf16[128,256]{1,0:T(8,128)(2,1)S(1)}, bf16[128,256]{1,0:T(8,128)(2,1)S(1)}, u32[]{:S(2)}, u32[]{:S(2)}) collective-permute-start(bf16[128,256]{1,0:T(8,128)(2,1)S(1)} %collective-permute-done.refs_1_), channel_id=1, source_target_pairs={{0,4},{4,0},{8,12},{12,8},{16,20},{20,16},{24,28},{28,24},{1,5},{5... | collective-permute-start | bytes 196616 | tf_op jit(solution)/shard_map/ppermute | solution.py:22
  14.1 4.6 %collective-permute-start.5 = (bf16[128,256]{1,0:T(8,128)(2,1)S(1)}, bf16[128,256]{1,0:T(8,128)(2,1)S(1)}, u32[]{:S(2)}, u32[]{:S(2)}) collective-permute-start(bf16[128,256]{1,0:T(8,128)(2,1)S(1)} %collective-permute-done.1.refs_2_), channel_id=1, source_target_pairs={{0,4},{4,0},{8,12},{12,8},{16,20},{20,16},{24,28},{28,24},{1,5},{5... | collective-permute-start | bytes 196616 | tf_op jit(solution)/shard_map/ppermute | solution.py:22
  14.6 4.7 %collective-permute-start.6 = (bf16[128,256]{1,0:T(8,128)(2,1)S(1)}, bf16[128,256]{1,0:T(8,128)(2,1)S(1)}, u32[]{:S(2)}, u32[]{:S(2)}) collective-permute-start(bf16[128,256]{1,0:T(8,128)(2,1)S(1)} %collective-permute-done.2.refs_3_), channel_id=1, source_target_pairs={{0,4},{4,0},{8,12},{12,8},{16,20},{20,16},{24,28},{28,24},{1,5},{5... | collective-permute-start | bytes 196616 | tf_op jit(solution)/shard_map/ppermute | solution.py:22
  16.2 5.0 %collective-permute-start.9 = (bf16[256,256]{1,0:T(8,128)(2,1)S(1)}, bf16[256,256]{1,0:T(8,128)(2,1)S(1)}, u32[]{:S(2)}, u32[]{:S(2)}) collective-permute-start(bf16[256,256]{1,0:T(8,128)(2,1)S(1)} %pad_maximum_fusion.3), channel_id=1, source_target_pairs={{0,2},{1,3},{2,0},{3,1},{4,6},{5,7},{6,4},{7,5},{8,10},{9,11},{10,... | collective-permute-start | bytes 393224 | tf_op jit(solution)/shard_map/ppermute | solution.py:22
  19.8 1.5 %collective-permute-start.7 = (f32[3,128,128]{2,1,0:T(8,128)S(1)}, f32[3,128,128]{2,1,0:T(8,128)S(1)}, u32[]{:S(2)}, u32[]{:S(2)}) collective-permute-start(f32[3,128,128]{2,1,0:T(8,128)S(1)} %get-tuple-element.37), channel_id=1, source_target_pairs={{0,1},{1,0},{2,3},{3,2},{4,5},{5,4},{6,7},{7,6},{8,9},{9,8},{10,11... | collective-permute-start | bytes 589832 | tf_op jit(solution)/shard_map/ppermute | solution.py:22
  21.3 7.0 %collective-permute-start.10 = (f32[3,128,128]{2,1,0:T(8,128)S(1)}, f32[3,128,128]{2,1,0:T(8,128)S(1)}, u32[]{:S(2)}, u32[]{:S(2)}) collective-permute-start(f32[3,128,128]{2,1,0:T(8,128)S(1)} %add.33.mine_ref), channel_id=1, source_target_pairs={{0,2},{1,3},{2,0},{3,1},{4,6},{5,7},{6,4},{7,5},{8,10},{9,11},{10,... | collective-permute-start | bytes 589832 | tf_op jit(solution)/shard_map/ppermute | solution.py:22
  28.5 7.5 %collective-permute-start.13 = (f16[2,128,256]{2,1,0:T(8,128)(2,1)S(1)}, f16[2,128,256]{2,1,0:T(8,128)(2,1)S(1)}, u32[]{:S(2)}, u32[]{:S(2)}) collective-permute-start(f16[2,128,256]{2,1,0:T(8,128)(2,1)S(1)} %get-tuple-element.61), channel_id=1, source_target_pairs={{0,4},{4,0},{8,12},{12,8},{16,20},{20,16},{24,28},{28,24},{1,5},{5... | collective-permute-start | bytes 393224 | tf_op jit(solution)/shard_map/ppermute | solution.py:22
  29.6 6.5 %collective-permute-start.15 = (f16[2,128,256]{2,1,0:T(8,128)(2,1)S(1)}, f16[2,128,256]{2,1,0:T(8,128)(2,1)S(1)}, u32[]{:S(2)}, u32[]{:S(2)}) collective-permute-start(f16[2,128,256]{2,1,0:T(8,128)(2,1)S(1)} %get-tuple-element.60), channel_id=1, source_target_pairs={{0,4},{4,0},{8,12},{12,8},{16,20},{20,16},{24,28},{28,24},{1,5},{5... | collective-permute-start | bytes 393224 | tf_op jit(solution)/shard_map/ppermute | solution.py:22
  30.6 10.1 %collective-permute-start.11 = (f32[2,128,256]{2,1,0:T(8,128)S(1)}, f32[2,128,256]{2,1,0:T(8,128)S(1)}, u32[]{:S(2)}, u32[]{:S(2)}) collective-permute-start(f32[2,128,256]{2,1,0:T(8,128)S(1)} %split.20), channel_id=1, source_target_pairs={{0,1},{1,0},{2,3},{3,2},{4,5},{5,4},{6,7},{7,6},{8,9},{9,8},{10,11... | collective-permute-start | bytes 786440 | tf_op jit(solution)/shard_map/ppermute | solution.py:22
  36.1 9.8 %collective-permute-start.14 = (f16[128,256]{1,0:T(8,128)(2,1)S(1)}, f16[128,256]{1,0:T(8,128)(2,1)S(1)}, u32[]{:S(2)}, u32[]{:S(2)}) collective-permute-start(f16[128,256]{1,0:T(8,128)(2,1)S(1)} %fusion.9), channel_id=1, source_target_pairs={{0,8},{4,12},{8,0},{12,4},{16,24},{20,28},{24,16},{28,20},{1,9},{5... | collective-permute-start | bytes 196616 | tf_op jit(solution)/shard_map/ppermute | solution.py:22
  36.8 9.1 %collective-permute-start.16 = (f16[128,256]{1,0:T(8,128)(2,1)S(1)}, f16[128,256]{1,0:T(8,128)(2,1)S(1)}, u32[]{:S(2)}, u32[]{:S(2)}) collective-permute-start(f16[128,256]{1,0:T(8,128)(2,1)S(1)} %get-tuple-element.45), channel_id=1, source_target_pairs={{0,16},{4,20},{8,24},{12,28},{16,0},{20,4},{24,8},{28,12},{1,17},{... | collective-permute-start | bytes 196616 | tf_op jit(solution)/shard_map/ppermute | solution.py:22
  40.5 6.1 %collective-permute-start.17 = (f16[128,256]{1,0:T(8,128)(2,1)S(1)}, f16[128,256]{1,0:T(8,128)(2,1)S(1)}, u32[]{:S(2)}, u32[]{:S(2)}) collective-permute-start(f16[128,256]{1,0:T(8,128)(2,1)S(1)} %get-tuple-element.47), channel_id=1, source_target_pairs={{0,24},{4,28},{8,16},{12,20},{16,8},{20,12},{24,0},{28,4},{1,25},{... | collective-permute-start | bytes 196616 | tf_op jit(solution)/shard_map/ppermute | solution.py:22
  40.8 5.9 %collective-permute-start.12 = (f16[1,128,256]{2,1,0:T(8,128)(2,1)S(1)}, f16[1,128,256]{2,1,0:T(8,128)(2,1)S(1)}, u32[]{:S(2)}, u32[]{:S(2)}) collective-permute-start(f16[1,128,256]{2,1,0:T(8,128)(2,1)S(1)} %slice_convert_fusion.1), channel_id=1, source_target_pairs={{0,2},{1,3},{2,0},{3,1},{4,6},{5,7},{6,4},{7,5},{8,10},{9,11},{10,... | collective-permute-start | bytes 196616 | tf_op jit(solution)/shard_map/ppermute | solution.py:22
  47.0 17.3 %copy-start = (bf16[128,256]{1,0:T(8,128)(2,1)}, bf16[128,256]{1,0:T(8,128)(2,1)S(1)}, u32[]{:S(2)}) copy-start(bf16[128,256]{1,0:T(8,128)(2,1)S(1)} %convolution_convert_fusion.refs_0_) | copy-start | bytes 196612
  47.0 4.5 %collective-permute-start.27 = (bf16[128,256]{1,0:T(8,128)(2,1)S(1)}, bf16[128,256]{1,0:T(8,128)(2,1)S(1)}, u32[]{:S(2)}, u32[]{:S(2)}) collective-permute-start(bf16[128,256]{1,0:T(8,128)(2,1)S(1)} %convolution_convert_fusion.refs_0_), channel_id=1, source_target_pairs={{0,1},{1,0},{2,3},{3,2},{4,5},{5,4},{6,7},{7,6},{8,9},{9,8},{10,11... | collective-permute-start | bytes 196616 | tf_op jit(solution)/shard_map/ppermute | solution.py:22
  47.1 6.4 %collective-permute-start.18 = (bf16[128,256]{1,0:T(8,128)(2,1)S(1)}, bf16[128,256]{1,0:T(8,128)(2,1)S(1)}, u32[]{:S(2)}, u32[]{:S(2)}) collective-permute-start(bf16[128,256]{1,0:T(8,128)(2,1)S(1)} %convolution_convert_fusion.refs_0_), channel_id=1, source_target_pairs={{0,8},{4,12},{8,0},{12,4},{16,24},{20,28},{24,16},{28,20},{1,9},{5... | collective-permute-start | bytes 196616 | tf_op jit(solution)/shard_map/ppermute | solution.py:22
  48.1 7.7 %collective-permute-start.19 = (bf16[128,256]{1,0:T(8,128)(2,1)S(1)}, bf16[128,256]{1,0:T(8,128)(2,1)S(1)}, u32[]{:S(2)}, u32[]{:S(2)}) collective-permute-start(bf16[128,256]{1,0:T(8,128)(2,1)S(1)} %convolution_convert_fusion.refs_0_), channel_id=1, source_target_pairs={{0,16},{4,20},{8,24},{12,28},{16,0},{20,4},{24,8},{28,12},{1,17},{... | collective-permute-start | bytes 196616 | tf_op jit(solution)/shard_map/ppermute | solution.py:22
  50.6 6.1 %collective-permute-start.20 = (bf16[128,256]{1,0:T(8,128)(2,1)S(1)}, bf16[128,256]{1,0:T(8,128)(2,1)S(1)}, u32[]{:S(2)}, u32[]{:S(2)}) collective-permute-start(bf16[128,256]{1,0:T(8,128)(2,1)S(1)} %convolution_convert_fusion.refs_0_), channel_id=1, source_target_pairs={{0,24},{4,28},{8,16},{12,20},{16,8},{20,12},{24,0},{28,4},{1,25},{... | collective-permute-start | bytes 196616 | tf_op jit(solution)/shard_map/ppermute | solution.py:22
  51.5 9.9 %collective-permute-start.28 = (bf16[256,256]{1,0:T(8,128)(2,1)S(1)}, bf16[256,256]{1,0:T(8,128)(2,1)S(1)}, u32[]{:S(2)}, u32[]{:S(2)}) collective-permute-start(bf16[256,256]{1,0:T(8,128)(2,1)S(1)} %pad_maximum_fusion.4), channel_id=1, source_target_pairs={{0,2},{1,3},{2,0},{3,1},{4,6},{5,7},{6,4},{7,5},{8,10},{9,11},{10,... | collective-permute-start | bytes 393224 | tf_op jit(solution)/shard_map/ppermute | solution.py:22
  53.1 4.8 %collective-permute-start.21 = (bf16[128,256]{1,0:T(8,128)(2,1)S(1)}, bf16[128,256]{1,0:T(8,128)(2,1)S(1)}, u32[]{:S(2)}, u32[]{:S(2)}) collective-permute-start(bf16[128,256]{1,0:T(8,128)(2,1)S(1)} %convolution_convert_fusion.refs_0_), channel_id=1, source_target_pairs={{0,4},{4,0},{8,12},{12,8},{16,20},{20,16},{24,28},{28,24},{1,5},{5... | collective-permute-start | bytes 196616 | tf_op jit(solution)/shard_map/ppermute | solution.py:22
  53.5 5.6 %collective-permute-start.22 = (bf16[128,256]{1,0:T(8,128)(2,1)S(1)}, bf16[128,256]{1,0:T(8,128)(2,1)S(1)}, u32[]{:S(2)}, u32[]{:S(2)}) collective-permute-start(bf16[128,256]{1,0:T(8,128)(2,1)S(1)} %collective-permute-done.18.refs_1_), channel_id=1, source_target_pairs={{0,4},{4,0},{8,12},{12,8},{16,20},{20,16},{24,28},{28,24},{1,5},{5... | collective-permute-start | bytes 196616 | tf_op jit(solution)/shard_map/ppermute | solution.py:22
  55.8 4.3 %collective-permute-start.23 = (bf16[128,256]{1,0:T(8,128)(2,1)S(1)}, bf16[128,256]{1,0:T(8,128)(2,1)S(1)}, u32[]{:S(2)}, u32[]{:S(2)}) collective-permute-start(bf16[128,256]{1,0:T(8,128)(2,1)S(1)} %collective-permute-done.19.refs_2_), channel_id=1, source_target_pairs={{0,4},{4,0},{8,12},{12,8},{16,20},{20,16},{24,28},{28,24},{1,5},{5... | collective-permute-start | bytes 196616 | tf_op jit(solution)/shard_map/ppermute | solution.py:22
  56.7 4.3 %collective-permute-start.24 = (bf16[128,256]{1,0:T(8,128)(2,1)S(1)}, bf16[128,256]{1,0:T(8,128)(2,1)S(1)}, u32[]{:S(2)}, u32[]{:S(2)}) collective-permute-start(bf16[128,256]{1,0:T(8,128)(2,1)S(1)} %collective-permute-done.20.refs_3_), channel_id=1, source_target_pairs={{0,4},{4,0},{8,12},{12,8},{16,20},{20,16},{24,28},{28,24},{1,5},{5... | collective-permute-start | bytes 196616 | tf_op jit(solution)/shard_map/ppermute | solution.py:22
  61.3 2.9 %collective-permute-start.25 = (f32[3,128,128]{2,1,0:T(8,128)S(1)}, f32[3,128,128]{2,1,0:T(8,128)S(1)}, u32[]{:S(2)}, u32[]{:S(2)}) collective-permute-start(f32[3,128,128]{2,1,0:T(8,128)S(1)} %get-tuple-element.48), channel_id=1, source_target_pairs={{0,1},{1,0},{2,3},{3,2},{4,5},{5,4},{6,7},{7,6},{8,9},{9,8},{10,11... | collective-permute-start | bytes 589832 | tf_op jit(solution)/shard_map/ppermute | solution.py:22
  64.4 2.6 %collective-permute-start.29 = (f32[2,2,128,256]{3,2,1,0:T(8,128)S(1)}, f32[2,2,128,256]{3,2,1,0:T(8,128)S(1)}, u32[]{:S(2)}, u32[]{:S(2)}) collective-permute-start(f32[2,2,128,256]{3,2,1,0:T(8,128)S(1)} %get-tuple-element.56), channel_id=1, source_target_pairs={{0,1},{1,0},{2,3},{3,2},{4,5},{5,4},{6,7},{7,6},{8,9},{9,8},{10,11... | collective-permute-start | bytes 1572872 | tf_op jit(solution)/shard_map/ppermute | solution.py:22
  64.9 15.7 %collective-permute-start.26 = (f32[3,128,128]{2,1,0:T(8,128)S(1)}, f32[3,128,128]{2,1,0:T(8,128)S(1)}, u32[]{:S(2)}, u32[]{:S(2)}) collective-permute-start(f32[3,128,128]{2,1,0:T(8,128)S(1)} %add.43.mine_ref), channel_id=1, source_target_pairs={{0,2},{1,3},{2,0},{3,1},{4,6},{5,7},{6,4},{7,5},{8,10},{9,11},{10,... | collective-permute-start | bytes 589832 | tf_op jit(solution)/shard_map/ppermute | solution.py:22
  67.2 4.4 %collective-permute-start.30 = (f16[144,256]{1,0:T(8,128)(2,1)S(1)}, f16[144,256]{1,0:T(8,128)(2,1)S(1)}, u32[]{:S(2)}, u32[]{:S(2)}) collective-permute-start(f16[144,256]{1,0:T(8,128)(2,1)S(1)} %get-tuple-element.64), channel_id=1, source_target_pairs={{0,4},{4,0},{8,12},{12,8},{16,20},{20,16},{24,28},{28,24},{1,5},{5... | collective-permute-start | bytes 221192 | tf_op jit(solution)/shard_map/ppermute | solution.py:22
  68.6 5.7 %collective-permute-start.31 = (f16[144,256]{1,0:T(8,128)(2,1)S(1)}, f16[144,256]{1,0:T(8,128)(2,1)S(1)}, u32[]{:S(2)}, u32[]{:S(2)}) collective-permute-start(f16[144,256]{1,0:T(8,128)(2,1)S(1)} %get-tuple-element.63), channel_id=1, source_target_pairs={{0,2},{1,3},{2,0},{3,1},{4,6},{5,7},{6,4},{7,5},{8,10},{9,11},{10,... | collective-permute-start | bytes 221192 | tf_op jit(solution)/shard_map/ppermute | solution.py:22
  70.1 5.9 %collective-permute-start.32 = (f16[144,256]{1,0:T(8,128)(2,1)S(1)}, f16[144,256]{1,0:T(8,128)(2,1)S(1)}, u32[]{:S(2)}, u32[]{:S(2)}) collective-permute-start(f16[144,256]{1,0:T(8,128)(2,1)S(1)} %get-tuple-element.62), channel_id=1, source_target_pairs={{0,6},{1,7},{2,4},{3,5},{4,2},{5,3},{6,0},{7,1},{8,14},{9,15},{10,... | collective-permute-start | bytes 221192 | tf_op jit(solution)/shard_map/ppermute | solution.py:33
  76.2 7.7 %collective-permute-start.33 = (f16[144,256]{1,0:T(8,128)(2,1)S(1)}, f16[144,256]{1,0:T(8,128)(2,1)S(1)}, u32[]{:S(2)}, u32[]{:S(2)}) collective-permute-start(f16[144,256]{1,0:T(8,128)(2,1)S(1)} %convert_element_type.86), channel_id=1, source_target_pairs={{0,8},{4,12},{8,0},{12,4},{16,24},{20,28},{24,16},{28,20},{1,9},{5... | collective-permute-start | bytes 221192 | tf_op jit(solution)/shard_map/ppermute | solution.py:22
  76.4 7.9 %collective-permute-start.34 = (f16[144,256]{1,0:T(8,128)(2,1)S(1)}, f16[144,256]{1,0:T(8,128)(2,1)S(1)}, u32[]{:S(2)}, u32[]{:S(2)}) collective-permute-start(f16[144,256]{1,0:T(8,128)(2,1)S(1)} %convert_element_type.86), channel_id=1, source_target_pairs={{0,16},{4,20},{8,24},{12,28},{16,0},{20,4},{24,8},{28,12},{1,17},{... | collective-permute-start | bytes 221192 | tf_op jit(solution)/shard_map/ppermute | solution.py:22
  79.6 6.3 %collective-permute-start.35 = (f16[144,256]{1,0:T(8,128)(2,1)S(1)}, f16[144,256]{1,0:T(8,128)(2,1)S(1)}, u32[]{:S(2)}, u32[]{:S(2)}) collective-permute-start(f16[144,256]{1,0:T(8,128)(2,1)S(1)} %convert_element_type.86), channel_id=1, source_target_pairs={{0,24},{4,28},{8,16},{12,20},{16,8},{20,12},{24,0},{28,4},{1,25},{... | collective-permute-start | bytes 221192 | tf_op jit(solution)/shard_map/ppermute | solution.py:22
  86.0 4.4 %collective-permute-start.36 = (f16[144,256]{1,0:T(8,128)(2,1)S(1)}, f16[144,256]{1,0:T(8,128)(2,1)S(1)}, u32[]{:S(2)}, u32[]{:S(2)}) collective-permute-start(f16[144,256]{1,0:T(8,128)(2,1)S(1)} %convert_element_type.91), channel_id=1, source_target_pairs={{0,4},{4,0},{8,12},{12,8},{16,20},{20,16},{24,28},{28,24},{1,5},{5... | collective-permute-start | bytes 221192 | tf_op jit(solution)/shard_map/ppermute | solution.py:22
  86.7 6.7 %collective-permute-start.37 = (f16[144,256]{1,0:T(8,128)(2,1)S(1)}, f16[144,256]{1,0:T(8,128)(2,1)S(1)}, u32[]{:S(2)}, u32[]{:S(2)}) collective-permute-start(f16[144,256]{1,0:T(8,128)(2,1)S(1)} %convert_element_type.91), channel_id=1, source_target_pairs={{0,2},{1,3},{2,0},{3,1},{4,6},{5,7},{6,4},{7,5},{8,10},{9,11},{10,... | collective-permute-start | bytes 221192 | tf_op jit(solution)/shard_map/ppermute | solution.py:22
  87.9 5.5 %collective-permute-start.38 = (f16[144,256]{1,0:T(8,128)(2,1)S(1)}, f16[144,256]{1,0:T(8,128)(2,1)S(1)}, u32[]{:S(2)}, u32[]{:S(2)}) collective-permute-start(f16[144,256]{1,0:T(8,128)(2,1)S(1)} %convert_element_type.91), channel_id=1, source_target_pairs={{0,6},{1,7},{2,4},{3,5},{4,2},{5,3},{6,0},{7,1},{8,14},{9,15},{10,... | collective-permute-start | bytes 221192 | tf_op jit(solution)/shard_map/ppermute | solution.py:33
  93.6 1.6 %collective-permute-start.39 = (f16[2,2,144,256]{3,2,1,0:T(8,128)(2,1)S(1)}, f16[2,2,144,256]{3,2,1,0:T(8,128)(2,1)S(1)}, u32[]{:S(2)}, u32[]{:S(2)}) collective-permute-start(f16[2,2,144,256]{3,2,1,0:T(8,128)(2,1)S(1)} %pad_maximum_fusion), channel_id=1, source_target_pairs={{0,1},{1,0},{2,3},{3,2},{4,5},{5,4},{6,7},{7,6},{8,9},{9,8},{10,11... | collective-permute-start | bytes 884744 | tf_op jit(solution)/shard_map/ppermute | solution.py:22
